TPU v7x, 32 devices: a whole 2x2x4 slice. The times are simulated.
32 devices in a mesh: wide: 4 (over x, core), narrow: 8 (over z, y).
Axes of the slice: x: 2, y: 2, z: 4, core: 2. Of those that a mesh axis runs over, the one named last changes fastest.
Arguments:
- tokens: bfloat16 [32768, 768], P(('wide', 'narrow')), may hold values from -60 to 60
- cotangent: bfloat16 [32768, 768], P(('wide', 'narrow')), may hold values from -8 to 8
- segment_ids: int32 [32768], P(('wide', 'narrow')), may hold values from 0 to 14, as said below
- pad_mask: int32 [32768], P(('wide', 'narrow')), may hold values from 0 to 1, as said below
- lengths: int32 [32], P(('wide', 'narrow')), may hold values from 706 to 966, as said below
- params: float32 [55424, 128], P(('wide', 'narrow')), may hold values from -10 to 10
Outputs:
- output: bfloat16 [32768, 768], P(('wide', 'narrow'))
- grad_input: float32 [32768, 768], P(('wide', 'narrow'))
- grad_params: float32 [55424, 128], P(('wide', 'narrow'))
Inputs may be any that keep to these rules, and one draw needn't show every extreme that they name: `segment_ids`: within each sequence of 1024 slots the numbers start at 0 and never fall. An image is one class token, 4 registers and h * w patches with h and w from 8 to 16; images are packed in order while they fit in 1024 - 1024 % (69) slots, and slots past the length carry the number after the last image. The first sequence holds only images of 8 x 8 patches. `pad_mask`: 1 exactly at the positions below its sequence's length. `lengths`: A sequence's length is the number of tokens of its images.
All inputs are finite; a program needn't handle non-finite values.
Results may differ from a plain program's by a relative error of at most 0.0097.
Values may be sent and summed in bfloat16 or wider, within the bound.
No kernel may reach another device: no remote copies, remote signals or barrier semaphores. Data moves between devices by JAX's collectives and lax.ppermute only.
A program may use at most 256 MiB of HBM per device.

v0:
```python
import math
from functools import partial

import jax
import jax.numpy as jnp
from jax import lax
from jax.experimental import pallas as pl
from jax.experimental.pallas import tpu as pltpu
from jax.sharding import PartitionSpec as P

FF = 3072
HEADS = 12
EPSILON = 1e-06
NEGATIVE = -1e30
AXES = ("wide", "narrow")
LANES = 128
SUB = 16
QB = 128
MEGA = 1 << 20
GRANT = 58 * MEGA
F32 = jnp.float32
BF16 = jnp.bfloat16

BLOCKS = 32
QKV_BLOCKS, QKV_RT, QKV_CT = 24, 2, 18
WO_BLOCKS, WO_RT, WO_CT = 8, 6, 6
W1_BLOCKS, W1_RT, W1_CT = 16, 3, 24
W2_BLOCKS, W2_RT, W2_CT = 16, 12, 6
ATT_HALF, MLP_HALF = 18, 36
ATT_SENT = ATT_HALF + 1
ATT_PART = 9
HALF_BLOCKS = BLOCKS // 2
CHUNK = 768
CHUNKS = FF // CHUNK

G1, C1, BQ, BV, BO, S1 = 0, 6, 12, 18, 24, 30
G2, C2, B1, B2, S2 = 36, 42, 48, 72, 78
SMALL = 88

NT = (((1,), (1,)), ((), ()))
NN = (((1,), (0,)), ((), ()))
TN = (((0,), (0,)), ((), ()))


def mm(lhs, rhs, dims):
    return lax.dot_general(lhs, rhs, dims, preferred_element_type=F32)


def row_of(ref, first, count):
    return jnp.concatenate([ref[first + k : first + k + 1, :] for k in range(count)], axis=1)


def put_row(ref, first, values):
    for k in range(values.shape[1] // LANES):
        ref[first + k : first + k + 1, :] = values[:, k * LANES : (k + 1) * LANES]


def fold8(values):
    rows, columns = values.shape
    return jnp.sum(values.reshape(rows // 8, 8, columns), axis=0)


def total(values):
    return jnp.sum(values, axis=0, keepdims=True)


def vmem():
    return pl.BlockSpec(memory_space=pltpu.VMEM)


def smem():
    return pl.BlockSpec(memory_space=pltpu.SMEM)


def hbm():
    return pl.BlockSpec(memory_space=pltpu.HBM)


def shape(dims, kind):
    return jax.ShapeDtypeStruct(dims, kind)


def cost(flops, moved, exps=0):
    return pl.CostEstimate(flops=int(flops), transcendentals=int(exps), bytes_accessed=int(moved))


def normalized(values):
    center = values - jnp.mean(values, axis=-1, keepdims=True)
    inverse = lax.rsqrt(jnp.mean(center * center, axis=-1, keepdims=True) + EPSILON)
    return center * inverse, inverse


def norm_pullback(unit, inverse, grad, gain):
    scaled = grad * gain
    first = jnp.mean(scaled, axis=-1, keepdims=True)
    second = jnp.mean(scaled * unit, axis=-1, keepdims=True)
    return inverse * (scaled - first - unit * second)


def gelu_pair(z):
    magnitude = jnp.abs(z)
    t = 1.0 / (1.0 + (0.3275911 * math.sqrt(0.5)) * magnitude)
    density = jnp.exp(z * z * -0.5)
    tail = 0.5 * 1.061405429
    tail = tail * t + 0.5 * -1.453152027
    tail = tail * t + 0.5 * 1.421413741
    tail = tail * t + 0.5 * -0.284496736
    tail = tail * t + 0.5 * 0.254829592
    tail = tail * t * density
    cumulative = jnp.where(z < 0, tail, 1.0 - tail)
    return z * cumulative, cumulative + z * density * (1.0 / math.sqrt(2.0 * math.pi))


def fetch(copies):
    for copy in copies:
        copy.start()


def settle(copies):
    for copy in copies:
        copy.wait()


ATT_BEFORE, ATT_AFTER = 64, 32
MLP_BEFORE, MLP_AFTER = 64, 40


def window_offsets(me, att_rows, mlp_rows):
    att = ATT_BEFORE + 12 + me * (576 - att_rows) + jnp.where(me < QKV_BLOCKS, 0, 12)
    mlp = MLP_BEFORE + 12 + me * (1152 - mlp_rows) + jnp.where(me < W1_BLOCKS, 0, 24)
    return att, mlp


def each_tile(me, act):
    for name, blocks, rt_count, ct_count, mine in (
        ("qkv", QKV_BLOCKS, QKV_RT, QKV_CT, me < QKV_BLOCKS),
        ("wo", WO_BLOCKS, WO_RT, WO_CT, me >= QKV_BLOCKS),
        ("w1", W1_BLOCKS, W1_RT, W1_CT, me < W1_BLOCKS),
        ("w2", W2_BLOCKS, W2_RT, W2_CT, me >= W1_BLOCKS),
    ):

        @pl.when(mine)
        def _(name=name, rt_count=rt_count, ct_count=ct_count):
            for ct in range(ct_count):
                for rt in range(rt_count):
                    act(name, rt, ct, rt * SUB * ct_count + ct, ct_count)


def half_place(name, rt, ct):
    if name == "qkv":
        return ct // 9, ct % 9 * QKV_RT + rt
    if name == "wo":
        return rt // 3, rt % 3 * WO_CT + ct
    if name == "w1":
        return ct // 12, ct % 12 * W1_RT + rt
    return rt // 6, rt % 6 * W2_CT + ct


def part_place(name, rt, ct):
    if name == "qkv":
        return ct % 6 // 3, rt, ct // 6 * 3 + ct % 3
    place = rt * WO_CT + ct
    return place // 18, place // ATT_PART % 2, place % ATT_PART


def qkv_group(g):
    return [6 * third + 3 * g + i for third in range(3) for i in range(3)]


def small_rows(me, act):
    @pl.when(me == 0)
    def _():
        act("att", True, 12, G1)
        act("mlp", True, 12, G2)

    @pl.when(me == QKV_BLOCKS - 1)
    def _():
        act("att", False, 12, BQ)

    @pl.when(me == W1_BLOCKS - 1)
    def _():
        act("mlp", False, 24, B1)

    @pl.when(me == BLOCKS - 1)
    def _():
        act("att", False, 12, BO)
        act("mlp", False, 12, B2)


OWNERS = (0, W1_BLOCKS - 1, QKV_BLOCKS - 1, BLOCKS - 1)


def sent_rows(kind, first):
    return 12 if kind == "mlp" and first in (G2, B2) else 0


def pack_kernel(att_rows, me_ref, own, tails, heads, att, mlp, win_a, win_m, table):
    me = me_ref[0]
    mlp_rows = own.shape[0] - att_rows
    win_a[0:ATT_BEFORE, :] = tails[0:ATT_BEFORE, :]
    win_a[ATT_BEFORE : ATT_BEFORE + att_rows, :] = own[0:att_rows, :]
    win_a[ATT_BEFORE + att_rows :, :] = heads[0:ATT_AFTER, :]
    win_m[0:MLP_BEFORE, :] = tails[ATT_BEFORE:, :]
    win_m[MLP_BEFORE : MLP_BEFORE + mlp_rows, :] = own[att_rows:, :]
    win_m[MLP_BEFORE + mlp_rows :, :] = heads[ATT_AFTER:, :]
    att_off, mlp_off = window_offsets(me, att_rows, mlp_rows)

    def tile(name, rt, ct, first, stride):
        attention = name in ("qkv", "wo")
        window, out, off = (win_a, att, att_off) if attention else (win_m, mlp, mlp_off)
        values = window[pl.ds(off + first, SUB, stride=stride), :]
        out[half_place(name, rt, ct)] = values.astype(BF16)

    each_tile(me, tile)
    table[...] = jnp.zeros_like(table)

    def vector(kind, before, rows, first):
        window, off, size = (win_a, att_off, 576) if kind == "att" else (win_m, mlp_off, 1152)
        start = off - 12 if before else off + size
        place = sent_rows(kind, first)
        table[place : place + rows, :] = window[pl.ds(start, rows), :]

    small_rows(me, vector)
    att[0, ATT_HALF] = table[0:SUB, :].astype(BF16)
    att[1, ATT_HALF] = table[SUB : 2 * SUB, :].astype(BF16)


def pack(me, own, tails, heads, att_rows):
    mlp_rows = own.shape[0] - att_rows
    return pl.pallas_call(
        partial(pack_kernel, att_rows),
        out_shape=(
            shape((2, ATT_SENT, SUB, LANES), BF16),
            shape((2, MLP_HALF, SUB, LANES), BF16),
        ),
        in_specs=[smem(), vmem(), vmem(), vmem()],
        out_specs=(vmem(), vmem()),
        scratch_shapes=[
            pltpu.VMEM((ATT_BEFORE + att_rows + ATT_AFTER, LANES), F32),
            pltpu.VMEM((MLP_BEFORE + mlp_rows + MLP_AFTER, LANES), F32),
            pltpu.VMEM((2 * SUB, LANES), F32),
        ],
        name="pack",
    )(me, own, tails, heads)


def spread_kernel(
    att_rows, scale, me_ref, group0, group1, mlp, mine, to_before, to_after, win_a, win_m, table
):
    me = me_ref[0]
    mlp_rows = mine.shape[0] - att_rows
    att_off, mlp_off = window_offsets(me, att_rows, mlp_rows)
    win_a[...] = jnp.zeros_like(win_a)
    win_m[...] = jnp.zeros_like(win_m)

    def tile(name, rt, ct, first, stride):
        if name in ("qkv", "wo"):
            g, half, index = part_place(name, rt, ct)
            values = (group0, group1)[g][half, index]
            win_a[pl.ds(att_off + first, SUB, stride=stride), :] = values * scale
        else:
            values = mlp[half_place(name, rt, ct)]
            win_m[pl.ds(mlp_off + first, SUB, stride=stride), :] = values * scale

    each_tile(me, tile)
    for h in range(2):
        table[SUB * h : SUB * h + SUB, :] = group1[h, ATT_PART] * scale

    def vector(kind, before, rows, first):
        window, off, size = (win_a, att_off, 576) if kind == "att" else (win_m, mlp_off, 1152)
        start = off - 12 if before else off + size
        place = sent_rows(kind, first)
        window[pl.ds(start, rows), :] = table[place : place + rows, :]

    small_rows(me, vector)
    mine[0:att_rows, :] = win_a[ATT_BEFORE : ATT_BEFORE + att_rows, :]
    mine[att_rows:, :] = win_m[MLP_BEFORE : MLP_BEFORE + mlp_rows, :]
    to_before[0:ATT_BEFORE, :] = win_a[0:ATT_BEFORE, :]
    to_before[ATT_BEFORE:, :] = win_m[0:MLP_BEFORE, :]
    to_after[0:ATT_AFTER, :] = win_a[ATT_BEFORE + att_rows :, :]
    to_after[ATT_AFTER:, :] = win_m[MLP_BEFORE + mlp_rows :, :]


def spread(me, group0, group1, mlp, att_rows, mlp_rows, scale):
    return pl.pallas_call(
        partial(spread_kernel, att_rows, scale),
        out_shape=(
            shape((att_rows + mlp_rows, LANES), F32),
            shape((ATT_BEFORE + MLP_BEFORE, LANES), F32),
            shape((ATT_AFTER + MLP_AFTER, LANES), F32),
        ),
        in_specs=[smem(), vmem(), vmem(), vmem()],
        out_specs=(vmem(), vmem(), vmem()),
        scratch_shapes=[
            pltpu.VMEM((ATT_BEFORE + att_rows + ATT_AFTER, LANES), F32),
            pltpu.VMEM((MLP_BEFORE + mlp_rows + MLP_AFTER, LANES), F32),
            pltpu.VMEM((2 * SUB, LANES), F32),
        ],
        name="spread",
    )(me, group0, group1, mlp)


def close_kernel(att_rows, mine, below, above, out):
    rows = mine.shape[0]
    out[...] = mine[...]
    out[0:ATT_AFTER, :] += below[0:ATT_AFTER, :]
    out[att_rows : att_rows + MLP_AFTER, :] += below[ATT_AFTER:, :]
    out[att_rows - ATT_BEFORE : att_rows, :] += above[0:ATT_BEFORE, :]
    out[rows - MLP_BEFORE : rows, :] += above[ATT_BEFORE:, :]


def close(mine, below, above, att_rows):
    return pl.pallas_call(
        partial(close_kernel, att_rows),
        out_shape=shape(mine.shape, F32),
        in_specs=[vmem()] * 3,
        out_specs=vmem(),
        name="close",
    )(mine, below, above)


def spot(h, d):
    x, c, z, y = d >> 4, (d >> 3) & 1, (d >> 1) & 3, d & 1
    return c * 16 + (y * 8 + x * 4 if h == 0 else x * 8 + y * 4) + z


SLOTS = [sorted(range(BLOCKS), key=partial(spot, h)) for h in range(2)]


def fill_spots(me, spots):
    for h in range(2):
        mine = spot(h, me)
        for d in range(BLOCKS):
            spots[h, d] = jnp.bitwise_xor(mine, spot(h, d))


def slots_scratch(tiles):
    return pltpu.VMEM((2, BLOCKS, tiles, SUB, LANES), BF16)


def spots_scratch():
    return pltpu.SMEM((2, BLOCKS), jnp.int32)


def arriving_slots(buffers, w, sems):
    return [
        pltpu.make_async_copy(buffers[i], w.at[i // 4, pl.ds(i % 4 * 8, 8)], sems.at[i])
        for i in range(8)
    ]


def leaving_slots(buffers, w, sems):
    return [
        pltpu.make_async_copy(w.at[i // 2, pl.ds(i % 2 * 16, 16)], buffers[i], sems.at[i])
        for i in range(4)
    ]


def qkv_column(w, spots, ct):
    h, place = ct // 9, ct % 9 * QKV_RT
    tiles = [w[h, spots[h, d], place + rt] for d in range(QKV_BLOCKS) for rt in range(QKV_RT)]
    return jnp.concatenate(tiles, axis=0)


def wo_matrix(w, spots):
    columns = []
    for ct in range(WO_CT):
        tiles = [
            w[rt // 3, spots[rt // 3, QKV_BLOCKS + i] & 7, rt % 3 * WO_CT + ct]
            for i in range(WO_BLOCKS)
            for rt in range(WO_RT)
        ]
        columns.append(jnp.concatenate(tiles, axis=0))
    return jnp.concatenate(columns, axis=1)


def dma(count):
    return pltpu.SemaphoreType.DMA((count,))


def norm_rows(rows, gain, shift, source, target, step=256):
    def one(i, carry):
        at = pl.ds(pl.multiple_of(i * step, step), step)
        unit, _ = normalized(source[at, :].astype(F32))
        target[at, :] = (unit * gain + shift).astype(BF16)
        return carry

    lax.fori_loop(0, rows // step, one, 0)


def qkv_kernel(me_ref, tokens, *refs):
    buffers, (n1, qkv, small, w, spots, x, unit, triple, sems, own) = refs[:8], refs[8:]
    coming = pltpu.make_async_copy(tokens, x, own.at[0])
    coming.start()
    weights = arriving_slots(buffers, w, sems)
    fetch(weights)
    fill_spots(me_ref[0], spots)
    settle(weights)
    tables = [
        jnp.concatenate([w[h, spots[h, d], ATT_HALF] for h in range(2)], axis=0).astype(F32)
        for d in OWNERS
    ]
    small[G1 : G1 + 12, :] = tables[0][0:12]
    small[G2 : G2 + 12, :] = tables[0][12:24]
    small[B1 : B1 + 24, :] = tables[1][0:24]
    small[BQ : BQ + 12, :] = tables[2][0:12]
    small[BO : BO + 12, :] = tables[3][0:12]
    small[B2 : B2 + 12, :] = tables[3][12:24]
    small[SMALL - 4 :, :] = jnp.zeros((4, LANES), F32)
    coming.wait()
    norm_rows(x.shape[0], row_of(small, G1, 6), row_of(small, C1, 6), x, unit)
    going = [pltpu.make_async_copy(unit, n1, own.at[0])]
    going[0].start()
    bias = jnp.concatenate(
        [row_of(small, BQ, 6), jnp.zeros((1, 768), F32), row_of(small, BV, 6)], axis=1
    )
    for c in range(QKV_CT // 2):
        weight = jnp.concatenate([qkv_column(w, spots, 2 * c + i) for i in range(2)], axis=1)
        lanes = slice(256 * c, 256 * c + 256)
        triple[:, lanes] = (mm(unit[...], weight, NN) + bias[:, lanes]).astype(BF16)
        going.append(
            pltpu.make_async_copy(triple.at[:, lanes], qkv.at[:, lanes], own.at[1 + c])
        )
        going[-1].start()
    settle(going)


def project_qkv(me, tokens, att):
    rows, width = tokens.shape
    return pl.pallas_call(
        qkv_kernel,
        out_shape=(
            shape((rows, width), BF16),
            shape((rows, 3 * width), BF16),
            shape((SMALL, LANES), F32),
        ),
        in_specs=[smem(), hbm()] + [hbm()] * 8,
        out_specs=(hbm(), hbm(), vmem()),
        scratch_shapes=[
            slots_scratch(ATT_SENT),
            spots_scratch(),
            pltpu.VMEM((rows, width), BF16),
            pltpu.VMEM((rows, width), BF16),
            pltpu.VMEM((rows, 3 * width), BF16),
            dma(8),
            dma(1 + QKV_CT // 2),
        ],
        compiler_params=pltpu.CompilerParams(vmem_limit_bytes=GRANT),
        cost_estimate=cost(6 * rows * width * width, 12 * rows * width),
        name="qkv_forward",
    )(me, tokens, *att)


CLASSES = (128, 256, 320, 384, 448, 512, 768)


def head_masked(block):
    lane = lax.broadcasted_iota(jnp.int32, block.shape, 1)
    zero = jnp.zeros_like(block)
    return jnp.concatenate(
        [jnp.where(lane < 64, block, zero), jnp.where(lane >= 64, block, zero)], axis=0
    )


def pick_heads(both):
    return jnp.concatenate([both[0:64, 0:QB], both[64:128, QB : 2 * QB]], axis=0)


def pieces_of_window(width):
    return [slice(first, min(first + QB, width)) for first in range(0, width, QB)]


def spread_ids(query_ids, key_ids):
    for b in range(query_ids.shape[0]):
        row = jnp.broadcast_to(query_ids[b : b + 1, :], (QB, QB))
        key_ids[b * QB : (b + 1) * QB, :] = row.T


def mask_bias(start, width, b, key_ids, query_ids, bias):
    for piece in pieces_of_window(width):
        size = piece.stop - piece.start
        at = pl.ds(pl.multiple_of(start + piece.start, SUB), size)
        same = key_ids[at, :] == query_ids[pl.ds(b, 1), :]
        bias[piece, :] = jnp.where(same, 0.0, NEGATIVE)


PAIRS = HEADS // 2


def attend_block(b, start, width, qkv, mixed, stats, bias, scores):
    rows = pl.ds(pl.multiple_of(b * QB, QB), QB)
    pieces = pieces_of_window(width)
    for p in range(PAIRS):
        lanes, key_lanes, value_lanes = [
            slice(LANES * (PAIRS * third + p), LANES * (PAIRS * third + p + 1))
            for third in range(3)
        ]
        queries = head_masked(qkv[rows, lanes] * 0.125)
        highest = jnp.full((8, 2 * QB), NEGATIVE, F32)
        for piece in pieces:
            size = piece.stop - piece.start
            at = pl.ds(pl.multiple_of(start + piece.start, SUB), size)
            part = mm(qkv[at, key_lanes], queries, NT)
            part = part + jnp.concatenate([bias[piece, :]] * 2, axis=1)
            scores[p, piece, :] = part
            highest = jnp.maximum(highest, jnp.max(part.reshape(size // 8, 8, 2 * QB), axis=0))
        highest = jnp.max(highest, axis=0, keepdims=True)
        summed = jnp.zeros((8, 2 * QB), F32)
        both = jnp.zeros((LANES, 2 * QB), F32)
        for piece in pieces:
            size = piece.stop - piece.start
            at = pl.ds(pl.multiple_of(start + piece.start, SUB), size)
            raised = jnp.exp(scores[p, piece, :] - highest)
            summed = summed + fold8(raised)
            both = both + mm(qkv[at, value_lanes], raised.astype(BF16), TN)
        inverse = 1.0 / total(summed)
        mixed[rows, lanes] = pick_heads(both * inverse).T.astype(BF16)
        stats[b * PAIRS + p, 0:1, :] = highest
        stats[b * PAIRS + p, 1:2, :] = inverse


def wo_scratch():
    return pltpu.VMEM((2, WO_BLOCKS, ATT_SENT, SUB, LANES), BF16)


def wo_copies(buffers, w, sems, core, x):
    copies = []
    for y in range(2):
        source = buffers[2 * core + y].at[pl.ds(4 * x, 4)]
        copies.append(pltpu.make_async_copy(source, w.at[0, pl.ds(4 * y, 4)], sems.at[y]))
    copies.append(pltpu.make_async_copy(buffers[4 + 2 * core + x], w.at[1], sems.at[2]))
    return copies


def fetch_wo(me, buffers, w, spots, sems):
    fill_spots(me, spots)
    for h in range(2):
        for i in range(WO_BLOCKS):
            place = spot(h, jnp.bitwise_xor(me, QKV_BLOCKS + i) & 7)
            spots[h, QKV_BLOCKS + i] = (place >> (1 if h == 0 else 0)) & 4 | place & 3
    far = jnp.bitwise_xor(me, QKV_BLOCKS)
    for core in range(2):
        for x in range(2):

            @pl.when((far >> 3) == 2 * x + core)
            def _(core=core, x=x):
                fetch(wo_copies(buffers, w, sems, core, x))


def wait_wo(buffers, w, sems):
    settle(wo_copies(buffers, w, sems, 0, 0))


def attend_kernel(me_ref, windows, qkv, tokens, cot, query_ids, small, *refs):
    buffers, refs = refs[:8], refs[8:]
    mixed, x1, branch, n2, dm, stats, gb2 = refs[:7]
    key_ids, triple, x, g, mix, mid, out, unit, scaled, bias, scores, w, spots = refs[7:20]
    sems, own, chunk_sems = refs[20:]
    rows = tokens.shape[0]
    blocks = rows // QB

    def chunk(i):
        at = pl.ds(pl.multiple_of(i * QB, QB), QB)
        return pltpu.make_async_copy(qkv.at[at, :], triple.at[at, :], chunk_sems.at[i])

    for i in range(blocks):
        chunk(i).start()
    coming = [
        pltpu.make_async_copy(tokens, x, own.at[0]),
        pltpu.make_async_copy(cot, g, own.at[1]),
    ]
    fetch(coming)
    fetch_wo(me_ref[0], buffers, w, spots, sems)
    spread_ids(query_ids, key_ids)

    def one_block(b, loaded):
        start = pl.multiple_of(windows[0, b], SUB)
        needed = jnp.maximum(windows[2, b], loaded)

        def arrived(i, carry):
            chunk(i).wait()
            return carry

        lax.fori_loop(loaded, needed, arrived, 0)
        for index, width in enumerate(CLASSES):

            @pl.when(windows[1, b] == index)
            def _(width=width):
                mask_bias(start, width, b, key_ids, query_ids, bias)
                attend_block(b, start, width, triple, mix, stats, bias, scores)

        return needed

    loaded = lax.fori_loop(0, blocks, one_block, jnp.int32(0))

    def arrived(i, carry):
        chunk(i).wait()
        return carry

    lax.fori_loop(loaded, blocks, arrived, 0)
    going = [pltpu.make_async_copy(mix, mixed, own.at[2])]
    going[0].start()
    wait_wo(buffers, w, sems)
    settle(coming)
    bo, s1 = row_of(small, BO, 6), row_of(small, S1, 6)
    gain, shift = row_of(small, G2, 6), row_of(small, C2, 6)
    s2 = row_of(small, S2, 6)
    weight = wo_matrix(w, spots)
    step = 256
    sums = jnp.zeros((8, 768), F32)
    for i in range(rows // step):
        at = slice(i * step, (i + 1) * step)
        made = mm(mix[at, :], weight, NN) + bo
        out[at, :] = made.astype(BF16)
        values = x[at, :].astype(F32) + s1 * made
        mid[at, :] = values
        normal, _ = normalized(values)
        unit[at, :] = (normal * gain + shift).astype(BF16)
        rounded = (g[at, :].astype(F32) * s2).astype(BF16)
        scaled[at, :] = rounded
        sums = sums + fold8(rounded.astype(F32))
        for k, (source, target) in enumerate(
            ((out, branch), (mid, x1), (unit, n2), (scaled, dm))
        ):
            sem = own.at[3 + 4 * i + k]
            going.append(pltpu.make_async_copy(source.at[at, :], target.at[at, :], sem))
            going[-1].start()
    put_row(gb2, 0, total(sums))
    settle(going)


def attend(me, windows, qkv, tokens, cot, query_ids, small, att):
    rows, width = tokens.shape
    row = lambda kind: pltpu.VMEM((rows, width), kind)
    return pl.pallas_call(
        attend_kernel,
        out_shape=(
            shape((rows, width), BF16),
            shape((rows, width), F32),
            shape((rows, width), BF16),
            shape((rows, width), BF16),
            shape((rows, width), BF16),
            shape((rows // QB * PAIRS, 2, 2 * QB), F32),
            shape((6, LANES), F32),
        ),
        in_specs=[smem(), smem(), hbm(), hbm(), hbm(), vmem(), vmem()] + [hbm()] * 8,
        out_specs=(hbm(),) * 5 + (vmem(), vmem()),
        scratch_shapes=[
            pltpu.VMEM((rows, QB), F32),
            pltpu.VMEM((rows, 3 * width), BF16),
            row(BF16),
            row(BF16),
            row(BF16),
            row(F32),
            row(BF16),
            row(BF16),
            row(BF16),
            pltpu.VMEM((CLASSES[-1], QB), F32),
            pltpu.VMEM((PAIRS, CLASSES[-1], 2 * QB), F32),
            wo_scratch(),
            spots_scratch(),
            dma(3),
            dma(3 + 4 * rows // 256),
            dma(rows // QB),
        ],
        compiler_params=pltpu.CompilerParams(vmem_limit_bytes=GRANT),
        cost_estimate=cost(2 * rows * rows * width, 20 * rows * width, 4 * rows * rows),
        name="attend_forward",
    )(me, windows, qkv, tokens, cot, query_ids, small, *att)


def lay_matrix(w, spots, name, blocks, first, rt_count, columns, out):
    def one_block(d, carry):
        places = [spots[h, first + d] for h in range(2)]
        base = pl.multiple_of(d * rt_count * SUB, SUB)
        for rt in range(rt_count):
            for column, ct in enumerate(columns):
                h, index = half_place(name, rt, ct)
                at = pl.ds(pl.multiple_of(base + rt * SUB, SUB), SUB)
                out[at, LANES * column : LANES * (column + 1)] = w[h, places[h], index]
        return carry

    lax.fori_loop(0, blocks, one_block, 0)


def lay_w1(w, spots, out):
    lay_matrix(w, spots, "w1", W1_BLOCKS, 0, W1_RT, range(W1_CT), out)


def lay_w2(w, spots, out):
    lay_matrix(w, spots, "w2", W2_BLOCKS, W1_BLOCKS, W2_RT, range(W2_CT), out)


def w2_place(spots, f, row, ct):
    rt = row % W2_RT
    h = rt // 6
    return h, spots[h, W1_BLOCKS + 4 * f + row // W2_RT], rt % 6 * W2_CT + ct


TALL = 256
PARTS = CHUNK // 256


def device_of(x, c, z, y):
    return x * 16 + c * 8 + z * 2 + y


W1_RUNS = [
    [(0, device_of(0, c, 0, y), 4) for c in range(2) for y in range(2)],
    [(1, device_of(0, c, 0, 0), 8) for c in range(2)],
]
W2_RUNS = [
    [(h, device_of(1, f >> 1, 2 * (f & 1), y), 2) for h in range(2) for y in range(2)]
    for f in range(CHUNKS)
]
RUN_ORDER = W1_RUNS[0] + W2_RUNS[0] + W2_RUNS[1] + W1_RUNS[1] + W2_RUNS[2] + W2_RUNS[3]


class Runs:
    def __init__(self, buffers, w, spots, sems, out=False):
        self.buffers, self.w, self.spots, self.sems, self.out = buffers, w, spots, sems, out
        self.each = len(buffers) // 2

    def copy(self, run, which, index, place):
        h, first, size = run
        outer = self.buffers[self.each * h + which].at[pl.ds(index, size)]
        inner = self.w.at[h, pl.ds(place, size)]
        sem = self.sems.at[RUN_ORDER.index(run)]
        ends = (inner, outer) if self.out else (outer, inner)
        return pltpu.make_async_copy(*ends, sem)

    def start(self, runs):
        length = BLOCKS // self.each
        for run in runs:
            h, first, size = run
            place = self.spots[h, first] & (BLOCKS - size)
            for which in range(self.each):

                @pl.when(place // length == which)
                def _(run=run, which=which, place=place):
                    self.copy(run, which, place & (length - 1), place).start()

    def wait(self, runs):
        for run in runs:
            self.copy(run, 0, 0, 0).wait()


def mlp_kernel(me_ref, n2_in, dm_in, small, *refs):
    arriving, refs = refs[:8], refs[8:]
    u_out, dz_out, vectors, *leaving = refs[:7]
    w, first, second, spots, n2, dm, u, dz, zs, dus, bias_sums, b1_lines, sems, own = refs[7:]
    rows, width = n2.shape
    tiles = rows // TALL
    coming = [
        pltpu.make_async_copy(n2_in, n2, own.at[0]),
        pltpu.make_async_copy(dm_in, dm, own.at[1]),
    ]
    fetch(coming)
    fill_spots(me_ref[0], spots)
    incoming = Runs(arriving, w, spots, sems)
    incoming.start(RUN_ORDER)
    bias_sums[...] = jnp.zeros_like(bias_sums)
    for f in range(CHUNKS):
        b1_lines[f : f + 1, :] = row_of(small, B1 + 6 * f, 6)
    def lay_chunk(f, side):
        h, base = f >> 1, MLP_HALF // 2 * (f & 1)
        for d in range(W1_BLOCKS):
            place = spots[h, d]
            for rt in range(W1_RT):
                at = slice((d * W1_RT + rt) * SUB, (d * W1_RT + rt + 1) * SUB)
                for ct in range(6):
                    lanes = slice(LANES * ct, LANES * ct + LANES)
                    first[side, at, lanes] = w[h, place, base + ct * W1_RT + rt]
        for k in range(4):
            places = [spots[i, W1_BLOCKS + 4 * f + k] for i in range(2)]
            for rt in range(W2_RT):
                at = slice((k * W2_RT + rt) * SUB, (k * W2_RT + rt + 1) * SUB)
                for ct in range(W2_CT):
                    lanes = slice(LANES * ct, LANES * ct + LANES)
                    i, index = half_place("w2", rt, ct)
                    second[side, at, lanes] = w[i, places[i], index]

    incoming.wait(W1_RUNS[0] + W2_RUNS[0])
    lay_chunk(jnp.int32(0), jnp.int32(0))
    settle(coming)

    units = [(t, c) for c in range(PARTS) for t in range(tiles)]

    def lanes_of(f, c):
        return pl.ds(pl.multiple_of(CHUNK * f + 256 * c, 256), 256)

    def outward(f):
        chunk = pl.ds(pl.multiple_of(CHUNK * f, CHUNK), CHUNK)
        return [
            pltpu.make_async_copy(u.at[:, chunk], u_out.at[:, chunk], own.at[2 * f]),
            pltpu.make_async_copy(dz.at[:, chunk], dz_out.at[:, chunk], own.at[2 * f + 1]),
        ]

    def one_chunk(f, carry):
        for index in range(CHUNKS - 1):

            @pl.when(f == index)
            def _(index=index):
                incoming.wait(W2_RUNS[index + 1] + (W1_RUNS[1] if index == 1 else []))

        side = f & 1
        lay_chunk(jnp.minimum(f + 1, CHUNKS - 1), 1 - side)

        def multiply(unit, slot):
            t, c = unit
            at = slice(TALL * t, TALL * t + TALL)
            zs[slot] = mm(n2[at, :], first[side, :, 256 * c : 256 * c + 256], NN)
            dus[slot] = mm(dm[at, :], second[side, 256 * c : 256 * c + 256, :], NT)

        def activate(unit, slot):
            t, c = unit
            lanes = slice(256 * c, 256 * c + 256)
            bias = b1_lines[pl.ds(f, 1), lanes]
            folded = jnp.zeros((8, 256), F32)
            for r in range(TALL // 32):
                part = slice(32 * r, 32 * r + 32)
                place = slice(TALL * t + 32 * r, TALL * t + 32 * r + 32)
                value, slope = gelu_pair(zs[slot, part, :] + bias)
                u[place, lanes_of(f, c)] = value.astype(BF16)
                rounded = (dus[slot, part, :] * slope).astype(BF16)
                dz[place, lanes_of(f, c)] = rounded
                folded = folded + fold8(rounded.astype(F32))
            bias_sums[:, lanes_of(f, c)] += folded

        multiply(units[0], 0)
        for i, unit in enumerate(units):
            if i + 1 < len(units):
                multiply(units[i + 1], (i + 1) % 2)
            activate(unit, i % 2)
        fetch(outward(f))
        return carry

    lax.fori_loop(0, CHUNKS, one_chunk, 0)
    put_row(vectors, 0, total(bias_sums[...]))

    outgoing = Runs(leaving, w, spots, sems, out=True)

    def one_grad(f, carry):
        h, base = f >> 1, MLP_HALF // 2 * (f & 1)
        chunk = pl.ds(pl.multiple_of(CHUNK * f, CHUNK), CHUNK)
        for c in range(PARTS):
            lanes = slice(256 * c, 256 * c + 256)
            grad = mm(n2[:, lanes], dz[:, chunk], TN)
            for r in range(SUB):
                d, rt = (SUB * c + r) // W1_RT, (SUB * c + r) % W1_RT
                for ct in range(6):
                    tile = grad[SUB * r : SUB * r + SUB, LANES * ct : LANES * ct + LANES]
                    w[h, spots[h, d], base + ct * W1_RT + rt] = tile.astype(BF16)
        for side in range(2):

            @pl.when(f == 2 * side + 1)
            def _(side=side):
                outgoing.start(W1_RUNS[side])

        for c in range(PARTS):
            grad = mm(u[:, lanes_of(f, c)], dm[...], TN)
            for r in range(SUB):
                for ct in range(W2_CT):
                    tile = grad[SUB * r : SUB * r + SUB, LANES * ct : LANES * ct + LANES]
                    w[w2_place(spots, f, SUB * c + r, ct)] = tile.astype(BF16)
        for index in range(CHUNKS):

            @pl.when(f == index)
            def _(index=index):
                outgoing.start(W2_RUNS[index])

        return carry

    lax.fori_loop(0, CHUNKS, one_grad, 0)
    for f in range(CHUNKS):
        settle(outward(f))
    outgoing.wait(RUN_ORDER)


def feed_forward(me, n2, dm, small, mlp):
    rows, width = n2.shape
    half = shape((HALF_BLOCKS, MLP_HALF, SUB, LANES), BF16)
    return pl.pallas_call(
        mlp_kernel,
        out_shape=(
            shape((rows, FF), BF16),
            shape((rows, FF), BF16),
            shape((24, LANES), F32),
            half,
            half,
            half,
            half,
        ),
        in_specs=[smem(), hbm(), hbm(), vmem()] + [hbm()] * 8,
        out_specs=(hbm(), hbm(), vmem()) + (hbm(),) * 4,
        scratch_shapes=[
            slots_scratch(MLP_HALF),
            pltpu.VMEM((2, width, CHUNK), BF16),
            pltpu.VMEM((2, CHUNK, width), BF16),
            spots_scratch(),
            pltpu.VMEM((rows, width), BF16),
            pltpu.VMEM((rows, width), BF16),
            pltpu.VMEM((rows, FF), BF16),
            pltpu.VMEM((rows, FF), BF16),
            pltpu.VMEM((2, TALL, 256), F32),
            pltpu.VMEM((2, TALL, 256), F32),
            pltpu.VMEM((8, FF), F32),
            pltpu.VMEM((CHUNKS, CHUNK), F32),
            dma(len(RUN_ORDER)),
            dma(2 * CHUNKS),
        ],
        compiler_params=pltpu.CompilerParams(vmem_limit_bytes=42 * MEGA),
        cost_estimate=cost(8 * rows * width * FF, 40 * MEGA),
        name="feed_forward",
    )(me, n2, dm, small, *mlp)


def matrix_copies(buffers, w, sems, x):
    copies = []
    for i in range(4):
        source = buffers[i].at[pl.ds(4 * x, 4)]
        copies.append(pltpu.make_async_copy(source, w.at[0, pl.ds(4 * i, 4)], sems.at[i]))
    for c in range(2):
        source = buffers[4 + 2 * c + x]
        copies.append(pltpu.make_async_copy(source, w.at[1, pl.ds(8 * c, 8)], sems.at[4 + c]))
    return copies


def fetch_matrix(me, buffers, w, spots, sems, first):
    def place(d):
        return ((d >> 3) & 1) * 8 + (d & 1) * 4 + ((d >> 1) & 3)

    for x in range(2):

        @pl.when((me >> 4) == (x ^ (first >> 4)))
        def _(x=x):
            fetch(matrix_copies(buffers, w, sems, x))

    mine = place(me)
    for d in range(W1_BLOCKS):
        for h in range(2):
            spots[h, first + d] = jnp.bitwise_xor(mine, place(d))


def wait_matrix(buffers, w, sems):
    settle(matrix_copies(buffers, w, sems, 0))


def matrix_scratch():
    return pltpu.VMEM((2, W1_BLOCKS, MLP_HALF, SUB, LANES), BF16)


def mlp_out_kernel(me_ref, u_in, x1_in, cot_in, small, *refs):
    arriving, refs = refs[:8], refs[8:]
    out, vectors, w, second, spots, u, x1, cot, macc, done, sums, sems, own = refs
    rows, width = x1.shape
    tiles = rows // TALL

    def tile_copy(source, target, t, k):
        at = pl.ds(pl.multiple_of(TALL * t, TALL), TALL)
        return pltpu.make_async_copy(source.at[at, :], target.at[at, :], own.at[k, t])

    fetch_matrix(me_ref[0], arriving, w, spots, sems, W1_BLOCKS)
    for t in range(tiles):
        tile_copy(u_in, u, t, 0).start()
    for t in range(tiles):
        tile_copy(x1_in, x1, t, 1).start()
        tile_copy(cot_in, cot, t, 2).start()
    bias, scale = row_of(small, B2, 6), row_of(small, S2, 6)
    sums[...] = jnp.zeros_like(sums)
    wait_matrix(arriving, w, sems)
    lay_w2(w, spots, second)

    def contract(t):
        at = pl.ds(pl.multiple_of(TALL * t, TALL), TALL)
        tile_copy(u_in, u, t, 0).wait()
        macc[at, :] = mm(u[at, :], second[...], NN)

    def finish(t):
        tile_copy(x1_in, x1, t, 1).wait()
        tile_copy(cot_in, cot, t, 2).wait()
        for part in range(TALL // 64):
            at = pl.ds(pl.multiple_of(TALL * t + 64 * part, 64), 64)
            contracted = macc[at, :] + bias
            done[at, :] = (x1[at, :] + scale * contracted).astype(BF16)
            sums[...] += fold8(cot[at, :].astype(F32) * contracted)
        tile_copy(done, out, t, 3).start()

    def one_tile(t, carry):
        contract(t)
        finish(t - 1)
        return carry

    contract(0)
    lax.fori_loop(1, tiles, one_tile, 0)
    finish(tiles - 1)
    put_row(vectors, 0, total(sums[...]))
    for t in range(tiles):
        tile_copy(done, out, t, 3).wait()


def feed_forward_out(me, u, x1, cot, small, mlp):
    rows, width = x1.shape
    row = lambda kind: pltpu.VMEM((rows, width), kind)
    return pl.pallas_call(
        mlp_out_kernel,
        out_shape=(shape((rows, width), BF16), shape((6, LANES), F32)),
        in_specs=[smem()] + [hbm()] * 3 + [vmem()] + [hbm()] * 8,
        out_specs=(hbm(), vmem()),
        scratch_shapes=[
            matrix_scratch(),
            pltpu.VMEM((FF, width), BF16),
            spots_scratch(),
            pltpu.VMEM((rows, FF), BF16),
            row(F32),
            row(BF16),
            row(F32),
            row(BF16),
            pltpu.VMEM((8, width), F32),
            dma(6),
            pltpu.SemaphoreType.DMA((4, rows // TALL)),
        ],
        compiler_params=pltpu.CompilerParams(vmem_limit_bytes=32 * MEGA),
        cost_estimate=cost(2 * rows * width * FF, 20 * MEGA),
        name="feed_forward_out",
    )(me, u, x1, cot, small, *mlp)


def split_kernel(me_ref, dz_in, x1_in, cot_in, branch_in, mixed_in, small, *refs):
    buffers, att_buffers, refs = refs[:8], refs[8:16], refs[16:]
    dx1_out, da_out, gwo0, gwo1, vectors = refs[:5]
    w, first, spots, wo, wo_spots, dz, x1, cot, dnacc, dx1, branch, mixed, db, da = refs[5:19]
    parts, sums, sems, wo_sems, own = refs[19:]
    me = me_ref[0]
    rows, width = x1.shape
    tiles = rows // TALL

    def tile_copy(source, target, t, k):
        at = pl.ds(pl.multiple_of(TALL * t, TALL), TALL)
        return pltpu.make_async_copy(source.at[at, :], target.at[at, :], own.at[k, t])

    fetch_matrix(me, buffers, w, spots, sems, 0)
    for t in range(tiles):
        tile_copy(dz_in, dz, t, 0).start()
    for t in range(tiles):
        tile_copy(x1_in, x1, t, 1).start()
        tile_copy(cot_in, cot, t, 2).start()
        tile_copy(branch_in, branch, t, 3).start()
    fetch_wo(me, att_buffers, wo, wo_spots, wo_sems)
    late = pltpu.make_async_copy(mixed_in, mixed, own.at[4, 0])
    late.start()
    gain, scale = row_of(small, G2, 6), row_of(small, S1, 6)
    sums[...] = jnp.zeros_like(sums)
    wait_matrix(buffers, w, sems)
    lay_w1(w, spots, first)

    def contract(t):
        at = pl.ds(pl.multiple_of(TALL * t, TALL), TALL)
        tile_copy(dz_in, dz, t, 0).wait()
        dnacc[at, :] = mm(dz[at, :], first[...], NT)

    def finish(t):
        tile_copy(x1_in, x1, t, 1).wait()
        tile_copy(cot_in, cot, t, 2).wait()
        tile_copy(branch_in, branch, t, 3).wait()
        for half in range(2):
            at = pl.ds(pl.multiple_of(TALL * t + TALL // 2 * half, TALL // 2), TALL // 2)
            unit, inverse = normalized(x1[at, :])
            grad = dnacc[at, :]
            middle = cot[at, :].astype(F32) + norm_pullback(unit, inverse, grad, gain)
            dx1[at, :] = middle
            rounded = (middle * scale).astype(BF16)
            db[at, :] = rounded
            sums[0:8, :] += fold8(grad * unit)
            sums[8:16, :] += fold8(grad)
            sums[16:24, :] += fold8(rounded.astype(F32))
            sums[24:32, :] += fold8(middle * branch[at, :].astype(F32))
        tile_copy(dx1, dx1_out, t, 1).start()

    def one_tile(t, carry):
        contract(t)
        finish(t - 1)
        return carry

    contract(0)
    lax.fori_loop(1, tiles, one_tile, 0)
    finish(tiles - 1)
    for k in range(4):
        put_row(vectors, 6 * k, total(sums[8 * k : 8 * k + 8, :]))
    wait_wo(att_buffers, wo, wo_sems)
    weight = wo_matrix(wo, wo_spots)
    going = []
    for c in range(3):
        lanes = slice(256 * c, 256 * c + 256)
        da[:, lanes] = mm(db[...], weight[lanes, :], NT).astype(BF16)
        going.append(pltpu.make_async_copy(da.at[:, lanes], da_out.at[:, lanes], own.at[0, c]))
        going[-1].start()
    late.wait()
    for c in range(3):
        grad = mm(mixed[:, 256 * c : 256 * c + 256], db[...], TN)
        for r in range(SUB):
            i, rt = (SUB * c + r) // WO_RT, (SUB * c + r) % WO_RT
            for ct in range(WO_CT):
                tile = grad[SUB * r : SUB * r + SUB, LANES * ct : LANES * ct + LANES]
                g, half, index = part_place("wo", rt, ct)
                parts[g, half, i, index] = tile.astype(BF16)
    for g, target in enumerate((gwo0, gwo1)):
        going.append(pltpu.make_async_copy(parts.at[g], target, own.at[4, g]))
        going[-1].start()
    settle(going)
    for t in range(tiles):
        tile_copy(dx1, dx1_out, t, 1).wait()


def split(me, dz, x1, cot, branch, mixed, small, mlp, att):
    rows, width = x1.shape
    part = (2, WO_BLOCKS, ATT_PART, SUB, LANES)
    row = lambda kind: pltpu.VMEM((rows, width), kind)
    return pl.pallas_call(
        split_kernel,
        out_shape=(
            shape((rows, width), F32),
            shape((rows, width), BF16),
            shape(part, BF16),
            shape(part, BF16),
            shape((24, LANES), F32),
        ),
        in_specs=[smem()] + [hbm()] * 5 + [vmem()] + [hbm()] * 16,
        out_specs=(hbm(),) * 4 + (vmem(),),
        scratch_shapes=[
            matrix_scratch(),
            pltpu.VMEM((width, FF), BF16),
            spots_scratch(),
            wo_scratch(),
            spots_scratch(),
            pltpu.VMEM((rows, FF), BF16),
            row(F32),
            row(BF16),
            row(F32),
            row(F32),
            row(BF16),
            row(BF16),
            row(BF16),
            row(BF16),
            pltpu.VMEM((2,) + part, BF16),
            pltpu.VMEM((32, width), F32),
            dma(6),
            dma(3),
            pltpu.SemaphoreType.DMA((5, rows // TALL)),
        ],
        compiler_params=pltpu.CompilerParams(vmem_limit_bytes=44 * MEGA),
        cost_estimate=cost(2 * rows * width * FF + 4 * rows * width * width, 40 * MEGA),
        name="feed_forward_in",
    )(me, dz, x1, cot, branch, mixed, small, *mlp, *att)


GROUP = PAIRS // 2
GROUP_LANES = GROUP * LANES


def attend_back_block(b, start, width, group, refs):
    q, k, v, da, stats, dq, dkeys, dvalues, bias = refs
    rows = pl.ds(pl.multiple_of(b * QB, QB), QB)
    at = pl.ds(start, width)
    mask = jnp.concatenate([bias[0:width, :]] * 2, axis=1)
    for p in range(GROUP):
        lanes = slice(LANES * p, LANES * p + LANES)
        place = b * PAIRS + GROUP * group + p
        queries = head_masked(q[rows, lanes] * 0.125)
        grads = head_masked(da[rows, lanes])
        highest = stats[place, 0:1, :]
        inverse = stats[place, 1:2, :]
        keys, values = k[at, lanes], v[at, lanes]
        weight = jnp.exp(mm(keys, queries, NT) + mask - highest) * inverse
        dweight = mm(values, grads, NT)
        inner_sum = total(fold8(weight * dweight))
        dvalues[at, lanes] += mm(weight.astype(BF16), grads, NN)
        dscore = (weight * (dweight - inner_sum)).astype(BF16)
        dkeys[at, lanes] += mm(dscore, queries, NN)
        both = mm(keys, dscore, TN)
        dq[rows, lanes] = (pick_heads(both) * 0.125).T.astype(BF16)


def attend_back_kernel(group, windows, qkv, da_in, stats, query_ids, dqkv, *refs):
    q, k, v, da, out, dkeys, dvalues, bias, key_ids, own = refs
    rows = q.shape[0]
    blocks = rows // QB
    lanes = slice(GROUP_LANES * group, GROUP_LANES * group + GROUP_LANES)
    coming = [pltpu.make_async_copy(da_in.at[:, lanes], da, own.at[3])]
    for third, target in enumerate((q, k, v)):
        first = LANES * PAIRS * third + GROUP_LANES * group
        source = qkv.at[:, first : first + GROUP_LANES]
        coming.append(pltpu.make_async_copy(source, target, own.at[third]))
    fetch(coming)
    dkeys[...] = jnp.zeros_like(dkeys)
    dvalues[...] = jnp.zeros_like(dvalues)
    spread_ids(query_ids, key_ids)
    settle(coming)
    dq = out.at[:, 0:GROUP_LANES]

    def one_block(b, carry):
        start = pl.multiple_of(windows[0, b], SUB)
        for index, width in enumerate(CLASSES):

            @pl.when(windows[1, b] == index)
            def _(width=width):
                mask_bias(start, width, b, key_ids, query_ids, bias)
                parts = (q, k, v, da, stats, dq, dkeys, dvalues, bias)
                attend_back_block(b, start, width, group, parts)

        return carry

    lax.fori_loop(0, blocks, one_block, 0)
    going = []
    for i in range(rows // 256):
        at = slice(256 * i, 256 * i + 256)
        out[at, GROUP_LANES : 2 * GROUP_LANES] = dkeys[at, :].astype(BF16)
        out[at, 2 * GROUP_LANES :] = dvalues[at, :].astype(BF16)
        going.append(pltpu.make_async_copy(out.at[at, :], dqkv.at[at, :], own.at[i]))
        going[-1].start()
    settle(going)


def attend_back(group, windows, qkv, da, stats, query_ids):
    rows = qkv.shape[0]
    part = lambda kind: pltpu.VMEM((rows, GROUP_LANES), kind)
    return pl.pallas_call(
        partial(attend_back_kernel, group),
        out_shape=shape((rows, 3 * GROUP_LANES), BF16),
        in_specs=[smem(), hbm(), hbm(), vmem(), vmem()],
        out_specs=hbm(),
        scratch_shapes=[
            part(BF16),
            part(BF16),
            part(BF16),
            part(BF16),
            pltpu.VMEM((rows, 3 * GROUP_LANES), BF16),
            part(F32),
            part(F32),
            pltpu.VMEM((CLASSES[-1], QB), F32),
            pltpu.VMEM((rows, QB), F32),
            dma(4),
        ],
        compiler_params=pltpu.CompilerParams(vmem_limit_bytes=32 * MEGA),
        cost_estimate=cost(3 * rows * rows * rows, 14 * rows * rows, 4 * rows * rows),
        name="attend_backward",
    )(windows, qkv, da, stats, query_ids)


def put_qkv_grad(n1, dqkv, w, spots):
    for c in range(3):
        grad = mm(n1[:, 256 * c : 256 * c + 256], dqkv[...], TN)
        for r in range(SUB):
            d, rt = (SUB * c + r) // QKV_RT, (SUB * c + r) % QKV_RT
            place = spots[rt, d]
            for index in range(ATT_PART):
                tile = grad[SUB * r : SUB * r + SUB, LANES * index : LANES * index + LANES]
                w[rt, place, index] = tile.astype(BF16)


def put_wo_grad(gwo, w, spots):
    for h in range(2):
        for i in range(WO_BLOCKS):
            w[h, spots[h, QKV_BLOCKS + i], 0:ATT_PART] = gwo[h, i]


def weight_grad_kernel(me_ref, n1_in, dqkv_in, gwo_in, *refs):
    leaving, (w, spots, n1, dqkv, gwo, sems, own) = refs[:4], refs[4:]
    coming = [
        pltpu.make_async_copy(n1_in, n1, own.at[0]),
        pltpu.make_async_copy(dqkv_in, dqkv, own.at[1]),
        pltpu.make_async_copy(gwo_in, gwo, own.at[2]),
    ]
    fetch(coming)
    fill_spots(me_ref[0], spots)
    settle(coming)
    put_wo_grad(gwo, w, spots)
    put_qkv_grad(n1, dqkv, w, spots)
    copies = leaving_slots(leaving, w, sems)
    fetch(copies)
    settle(copies)


def weight_grad(me, n1, dqkv, gwo):
    rows, width = n1.shape
    half = shape((HALF_BLOCKS, ATT_PART, SUB, LANES), BF16)
    return pl.pallas_call(
        weight_grad_kernel,
        out_shape=(half,) * 4,
        in_specs=[smem()] + [hbm()] * 3,
        out_specs=(hbm(),) * 4,
        scratch_shapes=[
            slots_scratch(ATT_PART),
            spots_scratch(),
            pltpu.VMEM((rows, width), BF16),
            pltpu.VMEM(dqkv.shape, BF16),
            pltpu.VMEM(gwo.shape, BF16),
            dma(4),
            dma(3),
        ],
        compiler_params=pltpu.CompilerParams(vmem_limit_bytes=20 * MEGA),
        cost_estimate=cost(3 * rows * width * width, 10 * rows * width),
        name="qkv_weight_grad",
    )(me, n1, dqkv, gwo)


def qkv_back_kernel(
    me_ref, tokens_in, n1_in, dx1_in, dqkv0_in, dqkv1_in, small, proj, mlp, gwo_in, *refs
):
    arriving, refs = refs[:8], refs[8:]
    dx_out, *leaving = refs[:5]
    w, gw, weight, spots, gwo, tokens, n1, dx1, dqkv0, dqkv1, dn, dx, sums, table = refs[5:19]
    sems, out_sems, own = refs[19:]
    rows = tokens.shape[0]
    tiles = rows // TALL

    def tile_copy(source, target, t, k):
        at = pl.ds(pl.multiple_of(TALL * t, TALL), TALL)
        return pltpu.make_async_copy(source.at[at, :], target.at[at, :], own.at[k, t])

    for t in range(tiles):
        tile_copy(dqkv0_in, dqkv0, t, 0).start()
        tile_copy(dqkv1_in, dqkv1, t, 1).start()
    weights = arriving_slots(arriving, w, sems)
    fetch(weights)
    for t in range(tiles):
        tile_copy(tokens_in, tokens, t, 2).start()
        tile_copy(dx1_in, dx1, t, 3).start()
    late = [
        pltpu.make_async_copy(n1_in, n1, own.at[4, 0]),
        pltpu.make_async_copy(gwo_in, gwo, own.at[4, 1]),
    ]
    fetch(late)
    sums[...] = jnp.zeros_like(sums)
    gain = row_of(small, G1, 6)
    fill_spots(me_ref[0], spots)
    settle(weights)
    columns = qkv_group(0) + qkv_group(1)
    lay_matrix(w, spots, "qkv", QKV_BLOCKS, 0, QKV_RT, columns, weight)

    def contract(t):
        at = pl.ds(pl.multiple_of(TALL * t, TALL), TALL)
        for g, (source, part) in enumerate(((dqkv0_in, dqkv0), (dqkv1_in, dqkv1))):
            tile_copy(source, part, t, g).wait()
            lanes = slice(384 * g, 384 * g + 384)
            sums[16:24, lanes] += fold8(part[at, 0:384].astype(F32))
            sums[24:32, lanes] += fold8(part[at, 768:1152].astype(F32))
        both = jnp.concatenate([dqkv0[at, :], dqkv1[at, :]], axis=1)
        dn[at, :] = mm(both, weight[...], NT)

    def finish(t):
        tile_copy(tokens_in, tokens, t, 2).wait()
        tile_copy(dx1_in, dx1, t, 3).wait()
        for half in range(2):
            at = pl.ds(pl.multiple_of(TALL * t + TALL // 2 * half, TALL // 2), TALL // 2)
            unit, inverse = normalized(tokens[at, :].astype(F32))
            grad = dn[at, :]
            dx[at, :] = dx1[at, :] + norm_pullback(unit, inverse, grad, gain)
            sums[0:8, :] += fold8(grad * unit)
            sums[8:16, :] += fold8(grad)
        tile_copy(dx, dx_out, t, 3).start()

    def one_tile(t, carry):
        contract(t)
        finish(t - 1)
        return carry

    contract(0)
    lax.fori_loop(1, tiles, one_tile, 0)
    finish(tiles - 1)

    def put_table(owner, *places):
        table[...] = jnp.zeros_like(table)
        for place, values in places:
            if values.shape[1] == LANES:
                table[place : place + values.shape[0], :] = values
            else:
                put_row(table, place, values)
        for h in range(2):
            gw[h, spots[h, owner], ATT_PART] = table[SUB * h : SUB * h + SUB, :].astype(BF16)

    put_table(
        OWNERS[0], (0, total(sums[0:8, :])), (6, total(sums[8:16, :])), (12, mlp[0:12, :])
    )
    put_table(OWNERS[1], (0, mlp[12:36, :]))
    put_table(OWNERS[2], (0, total(sums[16:24, :])), (6, total(sums[24:32, :])))
    put_table(OWNERS[3], (0, proj[...]), (12, mlp[36:48, :]))
    settle(late)
    put_wo_grad(gwo, gw, spots)
    put_qkv_grad(n1, dqkv1, gw, spots)
    copies = leaving_slots(leaving, gw, out_sems)
    fetch(copies)
    for t in range(tiles):
        tile_copy(dx, dx_out, t, 3).wait()
    settle(copies)


def qkv_back(me, tokens, n1, dx1, dqkv0, dqkv1, small, proj, mlp, gwo, att):
    rows, width = tokens.shape
    tiles = ATT_PART + 1
    half = shape((HALF_BLOCKS, tiles, SUB, LANES), BF16)
    row = lambda kind: pltpu.VMEM((rows, width), kind)
    return pl.pallas_call(
        qkv_back_kernel,
        out_shape=(shape((rows, width), F32), half, half, half, half),
        in_specs=[smem()] + [hbm()] * 5 + [vmem()] * 3 + [hbm()] * 9,
        out_specs=(hbm(),) * 5,
        scratch_shapes=[
            slots_scratch(ATT_SENT),
            slots_scratch(tiles),
            pltpu.VMEM((width, 3 * width), BF16),
            spots_scratch(),
            pltpu.VMEM(gwo.shape, BF16),
            row(BF16),
            row(BF16),
            row(F32),
            pltpu.VMEM(dqkv0.shape, BF16),
            pltpu.VMEM(dqkv1.shape, BF16),
            row(F32),
            row(F32),
            pltpu.VMEM((32, width), F32),
            pltpu.VMEM((2 * SUB, LANES), F32),
            dma(8),
            dma(4),
            pltpu.SemaphoreType.DMA((5, rows // TALL)),
        ],
        compiler_params=pltpu.CompilerParams(vmem_limit_bytes=46 * MEGA),
        cost_estimate=cost(9 * rows * width * width, 30 * rows * width),
        name="qkv_backward",
    )(me, tokens, n1, dx1, dqkv0, dqkv1, small, proj, mlp, gwo, *att)


X, C, Z1, Z0, Y = 16, 8, 4, 2, 1


def exchange(values, bit):
    return lax.ppermute(values, AXES, [(d, d ^ bit) for d in range(BLOCKS)])


def shifted(values, by):
    pairs = [(d, d + by) for d in range(BLOCKS) if 0 <= d + by < BLOCKS]
    return lax.ppermute(values, AXES, pairs)


def together(*values):
    return lax.optimization_barrier(values)


def along_z(first, second, received):
    return (
        jnp.stack([first] + [r[0] for r in received]),
        jnp.stack([second] + [r[1] for r in received]),
    )


def joined(own, received):
    return jnp.concatenate([own, received])


def sum_terms(terms):
    summed = terms[0].astype(F32)
    for term in terms[1:]:
        summed = summed + term.astype(F32)
    return summed


def kept(terms):
    return [t[: t.shape[0] // 2] for t in terms]


def z_part(first, second, k):
    return jnp.stack([sum_terms([t[k] for t in terms]) for terms in (first, second)])


def sent(terms):
    return sum_terms([t[t.shape[0] // 2 :] for t in terms]).astype(BF16)


def attention_amounts(width):
    return [width, width, 3 * width * width, width, width, width * width, width, width]


def feedforward_amounts(width):
    return [width, width, width * FF, FF, FF * width, width, width]


def pieces_of(vector, amounts):
    out, offset = [], 0
    for amount in amounts:
        out.append(vector[offset : offset + amount])
        offset += amount
    return out


def tiles_by_column(matrix, blocks, rt):
    ct = matrix.shape[1] // LANES
    return matrix.reshape(blocks, rt, SUB, ct, LANES).transpose(0, 3, 1, 2, 4)


def tiles_by_row(matrix, blocks, rt):
    ct = matrix.shape[1] // LANES
    return matrix.reshape(blocks, rt, SUB, ct, LANES).transpose(0, 1, 3, 2, 4)


def gather_plainly(params, att_rows, width):
    rounded = params.astype(BF16)
    att = lax.all_gather(rounded[:att_rows], AXES, axis=0, tiled=True).reshape(-1)
    mlp = lax.all_gather(rounded[att_rows:], AXES, axis=0, tiled=True).reshape(-1)
    g1, c1, wqkv, bq, bv, wo, bo, s1 = pieces_of(att, attention_amounts(width))
    g2, c2, w1, b1, w2, b2, s2 = pieces_of(mlp, feedforward_amounts(width))
    tile = (SUB, LANES)
    att = jnp.concatenate(
        [
            tiles_by_column(wqkv.reshape(width, -1), QKV_BLOCKS, QKV_RT).reshape((-1, 36) + tile),
            tiles_by_row(wo.reshape(width, -1), WO_BLOCKS, WO_RT).reshape((-1, 36) + tile),
        ]
    )
    mlp = jnp.concatenate(
        [
            tiles_by_column(w1.reshape(width, -1), W1_BLOCKS, W1_RT).reshape((-1, 72) + tile),
            tiles_by_row(w2.reshape(FF, -1), W2_BLOCKS, W2_RT).reshape((-1, 72) + tile),
        ]
    )
    vectors = jnp.concatenate([g1, c1, bq, bv, bo, s1, g2, c2, b1, b2, s2]).astype(F32)
    lines = vectors.reshape(-1, LANES)
    sent = jnp.zeros((BLOCKS, 2 * SUB, LANES), F32)
    for owner, place, first, count in (
        (OWNERS[0], 0, G1, 12),
        (OWNERS[0], 12, G2, 12),
        (OWNERS[1], 0, B1, 24),
        (OWNERS[2], 0, BQ, 12),
        (OWNERS[3], 0, BO, 12),
        (OWNERS[3], 12, B2, 12),
    ):
        sent = sent.at[owner, place : place + count].set(lines[first : first + count])
    sent = sent.astype(BF16).reshape((BLOCKS, 2, 1) + tile)
    att = [jnp.concatenate([att[:, 18 * h : 18 * h + 18], sent[:, h]], axis=1) for h in range(2)]
    return by_slot(*att), by_slot(mlp[:, :36], mlp[:, 36:])


def by_slot(first, second):
    halves = (first, second)
    return [
        jnp.stack([halves[i // 4][slot] for slot in SLOTS[i // 4][i % 4 * 8 : i % 4 * 8 + 8]])
        for i in range(8)
    ]


def from_slots(buffers):
    halves = []
    for h in range(2):
        slots = jnp.concatenate(buffers[2 * h : 2 * h + 2])
        halves.append(jnp.stack([slots[spot(h, d)] for d in range(BLOCKS)]))
    return halves


def reduce_plainly(gatt0, gatt1, gmlp, att_rows, mlp_rows, width, devices):
    groups = [from_slots(gatt0), from_slots(gatt1)]
    vectors = jnp.concatenate([groups[1][h][:, ATT_PART:] for h in range(2)], axis=1)
    vectors = vectors.astype(F32).reshape(BLOCKS, 2 * SUB, LANES)

    def matrix(name, first, last, rt_count, ct_count):
        rows = []
        for rt in range(rt_count):
            places = [part_place(name, rt, ct) for ct in range(ct_count)]
            rows.append(jnp.stack([groups[g][h][first:last, i] for g, h, i in places], axis=2))
        return jnp.stack(rows, axis=1).astype(F32).reshape(-1)

    wqkv = matrix("qkv", 0, QKV_BLOCKS, QKV_RT, QKV_CT)
    wo = matrix("wo", QKV_BLOCKS, BLOCKS, WO_RT, WO_CT)
    mlp = jnp.concatenate(from_slots(gmlp), axis=1).astype(F32)
    five = lambda v, dims: v.reshape((v.shape[0],) + dims + (SUB, LANES))
    w1 = five(mlp[:W1_BLOCKS], (W1_CT, W1_RT)).transpose(0, 2, 3, 1, 4).reshape(-1)
    w2 = five(mlp[W1_BLOCKS:], (W2_RT, W2_CT)).transpose(0, 1, 3, 2, 4).reshape(-1)
    line = lambda owner, first, count: vectors[owner, first : first + count].reshape(-1)
    att = [line(OWNERS[0], 0, 12), wqkv, line(OWNERS[2], 0, 12), wo, line(OWNERS[3], 0, 12)]
    mlp = [line(OWNERS[0], 12, 12), w1, line(OWNERS[1], 0, 24), w2, line(OWNERS[3], 12, 12)]

    def lay(parts, rows):
        vector = jnp.concatenate(parts)
        vector = jnp.pad(vector, (0, devices * rows * LANES - vector.shape[0]))
        return vector.reshape(devices, rows, LANES)

    whole = jnp.concatenate([lay(att, att_rows), lay(mlp, mlp_rows)], axis=1)
    return lax.psum_scatter(whole.reshape(-1, LANES), AXES, scatter_dimension=0, tiled=True)


def key_windows(segments, real):
    length = segments.shape[0]
    position = jnp.arange(length, dtype=jnp.int32)
    ids = jnp.where(real, segments, length + position)
    first = segments[0::QB]
    final = segments[QB - 1 :: QB]
    begin = jnp.sum((segments[None, :] < first[:, None]).astype(jnp.int32), axis=1)
    begin = jnp.where(real[0::QB], begin, position[0::QB])
    end = jnp.sum(((segments[None, :] <= final[:, None]) & real[None, :]).astype(jnp.int32), axis=1)
    end = jnp.where(real[QB - 1 :: QB], end, position[QB - 1 :: QB] + 1)
    begin = begin // SUB * SUB
    need = end - begin
    kind = sum((need > width).astype(jnp.int32) for width in CLASSES[:-1])
    widths = sum(
        jnp.where(kind == i, width, 0) for i, width in enumerate(CLASSES)
    )
    begin = jnp.minimum(begin, length - widths)
    chunks = (begin + widths + QB - 1) // QB
    return ids, jnp.stack([begin, kind, chunks]).astype(jnp.int32)


def local(tokens, cotangent, segment_ids, pad_mask, lengths, params):
    rows, width = tokens.shape
    wide, narrow = lax.axis_size("wide"), lax.axis_size("narrow")
    devices = wide * narrow
    att_count = 4 * width * width + 6 * width
    att_rows = (att_count // LANES + devices - 1) // devices
    mlp_rows = params.shape[0] - att_rows
    paired = (wide, narrow) == (4, 8)
    scale = 1.0 / math.sqrt(rows * devices)

    position = jnp.arange(rows, dtype=jnp.int32)
    real = (pad_mask > 0) & (position < lengths[0])
    ids, windows = key_windows(segment_ids, real)
    query_ids = ids.astype(F32).reshape(rows // QB, QB)

    if not paired:
        me = jnp.zeros((1,), jnp.int32)
        att, mlp = gather_plainly(params, att_rows, width)
        n1, qkv, small = project_qkv(me, tokens, att)
        mixed, x1, branch, n2, dm, stats, gb2 = attend(
            me, windows, qkv, tokens, cotangent, query_ids, small, att
        )
        u, dz, gb1, *gmlp = feed_forward(me, n2, dm, small, mlp)
        output, gs2 = feed_forward_out(me, u, x1, cotangent, small, mlp)
        dx1, da, gwo0, gwo1, others = split(
            me, dz, x1, cotangent, branch, mixed, small, mlp, att
        )
        small_mlp = jnp.concatenate([others[:12], gb1, gb2, gs2])
        small_proj = others[12:]
        dqkv0 = attend_back(0, windows, qkv, da, stats, query_ids)
        dqkv1 = attend_back(1, windows, qkv, da, stats, query_ids)
        gatt0 = weight_grad(me, n1, dqkv0, gwo0)
        grad_input, *gatt1 = qkv_back(
            me, tokens, n1, dx1, dqkv0, dqkv1, small, small_proj, small_mlp, gwo1, att
        )
        owned = reduce_plainly(gatt0, gatt1, gmlp, att_rows, mlp_rows, width, devices)
        return output, grad_input, owned * scale

    me = lax.axis_index(AXES).astype(jnp.int32).reshape(1)
    tails = jnp.concatenate([params[att_rows - ATT_BEFORE : att_rows], params[-MLP_BEFORE:]])
    heads = jnp.concatenate([params[:ATT_AFTER], params[att_rows : att_rows + MLP_AFTER]])
    tails, heads = shifted(tails, 1), shifted(heads, -1)
    att_own, mlp_own = pack(me, params, tails, heads, att_rows)

    got = [exchange(att_own, k * Z0) for k in range(1, 4)]
    a, b = along_z(att_own[0], att_own[1], got)
    a, b, mlp_own, windows, query_ids = together(a, b, mlp_own, windows, query_ids)
    ax, by = exchange(a, X), exchange(b, Y)
    z1, z3 = exchange(mlp_own, Z0), exchange(mlp_own, 3 * Z0)
    a, b = joined(a, ax), joined(b, by)
    a, b, z1, z3, mlp_own = together(a, b, z1, z3, mlp_own)
    ay, bx = exchange(a, Y), exchange(b, X)
    ac, bc = exchange(a, C), exchange(b, C)
    z2 = exchange(mlp_own, 2 * Z0)
    m, n = along_z(mlp_own[0], mlp_own[1], [z1, z2, z3])
    ay, bx, ac, bc, m, n = together(ay, bx, ac, bc, m, n)
    ayc, bxc = exchange(ay, C), exchange(bx, C)
    att = together(a, ay, ac, ayc, b, bx, bc, bxc, m, n, tokens)
    *att, m, n, tokens_now = att
    mx, ny = exchange(m, X), exchange(n, Y)
    n1, qkv, small = project_qkv(me, tokens_now, att)
    m, n = joined(m, mx), joined(n, ny)
    m, n, qkv = together(m, n, qkv)
    my, nx = exchange(m, Y), exchange(n, X)
    mc, nc = exchange(m, C), exchange(n, C)
    mixed, x1, branch, n2, dm, stats, gb2 = attend(
        me, windows, qkv, tokens, cotangent, query_ids, small, att
    )
    m, n, my, nx, mc, nc, n2 = together(m, n, my, nx, mc, nc, n2)
    myc, nxc = exchange(my, C), exchange(nx, C)
    mlp = (m, my, mc, myc, n, nx, nc, nxc)

    u, dz, gb1, *gmlp = feed_forward(me, n2, dm, small, mlp)

    mc, nc = exchange(gmlp[1], C), exchange(gmlp[3], C)
    output, gs2 = feed_forward_out(me, u, x1, cotangent, small, mlp)
    mc, nc, dz, gs2 = together(mc, nc, dz, gs2)
    m, n = [gmlp[0], mc], [gmlp[2], nc]
    my, nx, dz = together(sent(m), sent(n), dz)
    my, nx = exchange(my, Y), exchange(nx, X)
    dx1, da, gwo0, gwo1, others = split(
        me, dz, x1, cotangent, branch, mixed, small, mlp, att
    )
    dqkv0 = attend_back(0, windows, qkv, da, stats, query_ids)
    gatt0 = weight_grad(me, n1, dqkv0, gwo0)
    my, nx, da, *gatt0 = together(my, nx, da, *gatt0)
    m, n = kept(m) + [my], kept(n) + [nx]
    mx, ny, da, *gatt0 = together(sent(m), sent(n), da, *gatt0)
    mx, ny = exchange(mx, X), exchange(ny, Y)
    ac, bc = exchange(gatt0[1], C), exchange(gatt0[3], C)
    dqkv1 = attend_back(1, windows, qkv, da, stats, query_ids)
    mx, ny, ac, bc, dqkv1 = together(mx, ny, ac, bc, dqkv1)
    m, n = kept(m) + [mx], kept(n) + [ny]
    z1, z2, z3 = [z_part(m, n, k).astype(BF16) for k in range(1, 4)]
    a, b = [gatt0[0], ac], [gatt0[2], bc]
    ay, bx, z1, z2, z3, dqkv1 = together(sent(a), sent(b), z1, z2, z3, dqkv1)
    z1, z2 = exchange(z1, Z0), exchange(z2, 2 * Z0)
    ay, bx = exchange(ay, Y), exchange(bx, X)
    small_mlp = jnp.concatenate([others[:12], gb1, gb2, gs2])
    grad_input, *gatt1 = qkv_back(
        me, tokens, n1, dx1, dqkv0, dqkv1, small, others[12:], small_mlp, gwo1, att
    )
    ay, bx, z1, z2, *gatt1 = together(ay, bx, z1, z2, *gatt1)
    a, b = kept(a) + [ay], kept(b) + [bx]
    ax, by, c1, d1, z3 = together(sent(a), sent(b), gatt1[1], gatt1[3], z3)
    c1, d1 = exchange(c1, C), exchange(d1, C)
    ax, by = exchange(ax, X), exchange(by, Y)
    z3a = exchange(z3[0], 3 * Z0)
    c, d = [gatt1[0], c1], [gatt1[2], d1]
    a, b = kept(a) + [ax], kept(b) + [by]
    sends = [z_part(a, b, k).astype(BF16) for k in range(1, 4)]
    cy, dx, z3a, z3, *sends = together(sent(c), sent(d), z3a, z3, *sends)
    cy, dx = exchange(cy, Y), exchange(dx, X)
    got = [exchange(part, (k + 1) * Z0) for k, part in enumerate(sends)]
    c, d = kept(c) + [cy], kept(d) + [dx]
    cx, dy, z3, *got = together(sent(c), sent(d), z3, *got)
    z3b = exchange(z3[1], 3 * Z0)
    group0 = sum_terms([z_part(a, b, 0)] + got)
    cx, dy = exchange(cx, X), exchange(dy, Y)
    c, d = kept(c) + [cx], kept(d) + [dy]
    m_own = sum_terms([z_part(m, n, 0), z1, z2, jnp.stack([z3a, z3b])])
    sends = [z_part(c, d, k).astype(BF16) for k in range(1, 4)]
    group0, m_own, *sends = together(group0, m_own, *sends)
    got = [exchange(part, (k + 1) * Z0) for k, part in enumerate(sends)]
    group1 = sum_terms([z_part(c, d, 0)] + got)
    mine, to_before, to_after = spread(me, group0, group1, m_own, att_rows, mlp_rows, scale)
    grad_params = close(mine, shifted(to_after, 1), shifted(to_before, -1), att_rows)
    return output, grad_input, grad_params


def solution(mesh):
    return jax.shard_map(
        local,
        mesh=mesh,
        in_specs=(
            P(AXES, None),
            P(AXES, None),
            P(AXES),
            P(AXES),
            P(AXES),
            P(AXES, None),
        ),
        out_specs=(P(AXES, None), P(AXES, None), P(AXES, None)),
        check_vma=False,
    )
```

profile of v0, /device:TPU:1, one launch (start us, length us, event | category | flops | bytes accessed | tf_op | source)
XLA Modules:
  0.0 316.7 jit_solution(12567718785523464018)
XLA Ops:
  2.1 7.6 %collective-permute-start.1 = (f32[72,128]{1,0:T(8,128)S(1)}, f32[72,128]{1,0:T(8,128)S(1)}, u32[]{:S(2)}, u32[]{:S(2)}) collective-permute-start(f32[72,128]{1,0:T(8,128)S(1)} %pad_maximum_fusion.18), channel_id=1, source_target_pairs={{1,0},{2,1},{3,2},{4,3},{5,4},{6,5},{7,6},{8,7},{9,8},{10,9},{11,1... | collective-permute-start | bytes 110600 | tf_op jit(solution)/shard_map/ppermute | solution.py:1442
  10.5 1.9 collective-permute-start
  14.6 1.3 convert_bitcast_fusion
  17.9 1.5 collective-permute-done.tails
  20.0 2.2 pack.1
  22.3 3.5 %collective-permute-start.2 = (bf16[2,19,16,128]{3,2,1,0:T(8,128)(2,1)}, bf16[2,19,16,128]{3,2,1,0:T(8,128)(2,1)S(1)}, u32[]{:S(2)}, u32[]{:S(2)}) collective-permute-start(bf16[2,19,16,128]{3,2,1,0:T(8,128)(2,1)} %get-tuple-element.141), channel_id=1, source_target_pairs={{0,2},{1,3},{2,0},{3,1},{4,6},{5,7},{6,4},{7,5},{8,10},{9,11},{10,... | collective-permute-start | bytes 466952 | tf_op jit(solution)/shard_map/ppermute | solution.py:1437
  26.7 2.6 collective-permute-done.4
  29.3 4.5 %collective-permute-done.3 = bf16[2,19,16,128]{3,2,1,0:T(8,128)(2,1)S(1)} collective-permute-done((bf16[2,19,16,128]{3,2,1,0:T(8,128)(2,1)}, bf16[2,19,16,128]{3,2,1,0:T(8,128)(2,1)S(1)}, u32[]{:S(2)}, u32[]{:S(2)}) %collective-permute-start.3) | collective-permute-done | bytes 155680 | tf_op jit(solution)/shard_map/ppermute | solution.py:1437
  34.0 2.1 collective-permute-start.5
  36.1 1.4 collective-permute-start.6
  37.4 2.3 collective-permute-start.8
  39.7 2.5 collective-permute-done.5
  43.2 3.0 collective-permute-done.8
  46.3 8.3 %collective-permute-done.7 = bf16[2,36,16,128]{3,2,1,0:T(8,128)(2,1)S(1)} collective-permute-done((bf16[2,36,16,128]{3,2,1,0:T(8,128)(2,1)S(1)}, bf16[2,36,16,128]{3,2,1,0:T(8,128)(2,1)S(1)}, u32[]{:S(2)}, u32[]{:S(2)}) %collective-permute-start.7) | collective-permute-done | bytes 294944 | tf_op jit(solution)/shard_map/ppermute | solution.py:1437
  56.1 1.3 collective-permute-start.10
  57.5 12.4 %collective-permute-done.13 = bf16[2,36,16,128]{3,2,1,0:T(8,128)(2,1)S(1)} collective-permute-done((bf16[2,36,16,128]{3,2,1,0:T(8,128)(2,1)S(1)}, bf16[2,36,16,128]{3,2,1,0:T(8,128)(2,1)S(1)}, u32[]{:S(2)}, u32[]{:S(2)}) %collective-permute-start.13) | collective-permute-done | bytes 294944 | tf_op jit(solution)/shard_map/ppermute | solution.py:1437
  70.1 1.3 collective-permute-done.9.refs_1_.refs_9_
  72.6 1.7 collective-permute-done.14.refs_3_.refs_11_
  75.1 1.3 collective-permute-start.16
  76.4 1.5 collective-permute-start.17
  77.9 10.2 %qkv_forward.1 = (bf16[1024,768]{1,0:T(8,128)(2,1)}, bf16[1024,2304]{1,0:T(8,128)(2,1)}, f32[88,128]{1,0:T(8,128)}) custom-call(s32[1]{0:T(128)} %bitcast.me_ref, bf16[1024,768]{1,0:T(8,128)(2,1)} %tokens_in.1, bf16[8,19,16,128]{3,2,1,0:T(8,128)(2,1)} %copy-done.4, bf16[8,19,16,128]{3,2,1,0:T(8,128)(2,1)} %copy-done.19, bf16[8,19,16,128]{3,2,1,0:T(8,128)(2,1)} %copy-done.17, ...), custom_call_target="tpu_custom_call" | custom-call | flops 3623878656 | bytes 9437184 | tf_op jit(solution)/shard_map/qkv_forward/pallas_call | solution.py:430
  88.1 1.7 collective-permute-done.16
  89.8 1.2 pad_maximum_fusion.refs_0_
  91.1 1.3 collective-permute-start.20
  92.4 1.5 collective-permute-start.18
  94.2 1.3 collective-permute-start.19
  95.5 17.9 %attend_forward.1 = (bf16[1024,768]{1,0:T(8,128)(2,1)}, f32[1024,768]{1,0:T(8,128)}, bf16[1024,768]{1,0:T(8,128)(2,1)}, bf16[1024,768]{1,0:T(8,128)(2,1)}, bf16[...) custom-call(s32[1]{0:T(128)} %bitcast.me_ref, s32[3,8]{1,0:T(4,128)} %pad_add_fusion.windows, ...), custom_call_target="tpu_custom_call" | custom-call | flops 1610612736 | bytes 15728640 | tf_op jit(solution)/shard_map/attend_forward/pallas_call | solution.py:635
  113.4 6.6 %collective-permute-done.18.refs_1_ = bf16[8,36,16,128]{3,2,1,0:T(8,128)(2,1)S(1)} collective-permute-done((bf16[8,36,16,128]{3,2,1,0:T(8,128)(2,1)S(1)}, bf16[8,36,16,128]{3,2,1,0:T(8,128)(2,1)S(1)}, u32[]{:S(2)}, u32[]{:S(2)}) %collective-permute-start.18) | collective-permute-done | bytes 1179680 | tf_op jit(solution)/shard_map/ppermute | solution.py:1437
  120.0 1.7 collective-permute-done.19.refs_5_
  122.7 4.1 %collective-permute-done.22.refs_3_ = bf16[8,36,16,128]{3,2,1,0:T(8,128)(2,1)S(1)} collective-permute-done((bf16[8,36,16,128]{3,2,1,0:T(8,128)(2,1)S(1)}, bf16[8,36,16,128]{3,2,1,0:T(8,128)(2,1)S(1)}, u32[]{:S(2)}, u32[]{:S(2)}) %collective-permute-start.22) | collective-permute-done | bytes 1179680 | tf_op jit(solution)/shard_map/ppermute | solution.py:1437
  127.0 2.0 copy-done.34
  129.1 35.2 %feed_forward.1 = (bf16[1024,3072]{1,0:T(8,128)(2,1)}, bf16[1024,3072]{1,0:T(8,128)(2,1)}, f32[24,128]{1,0:T(8,128)S(1)}, bf16[16,36,16,128]{3,2,1,0:T(8,128)(2,...) custom-call(s32[1]{0:T(128)} %bitcast.me_ref, ...), custom_call_target="tpu_custom_call" | custom-call | flops 19327352832 | bytes 41943040 | tf_op jit(solution)/shard_map/feed_forward/pallas_call | solution.py:883
  165.5 2.8 copy-done.3
  168.3 1.3 copy-done.14
  169.6 1.3 copy-done.16
  170.9 10.7 %feed_forward_out.1 = (bf16[1024,768]{1,0:T(8,128)(2,1)}, f32[6,128]{1,0:T(8,128)S(1)}) custom-call(s32[1]{0:T(128)} %bitcast.me_ref, bf16[1024,3072]{1,0:T(8,128)(2,1)S(1)} %copy-done.3, f32[1024,768]{1,0:T(8,128)S(1)} %copy-done.1, bf16[1024,768]{1,0:T(8,128)(2,1)S(1)} %copy-done, f32[88,128]{1,0:T(8,128)S(1)} %copy-done.30, ...), custom_call_target="tpu_custom_call" | custom-call | flops 4831838208 | bytes 20971520 | tf_op jit(solution)/shard_map/feed_forward_out/pallas_call | solution.py:1005
  181.7 1.3 add_convert_fusion.1
  186.6 16.2 %feed_forward_in.1 = (f32[1024,768]{1,0:T(8,128)}, bf16[1024,768]{1,0:T(8,128)(2,1)}, bf16[2,8,9,16,128]{4,3,2,1,0:T(8,128)(2,1)S(1)}, bf16[2,8,9,16,128]{4,3,2,1,0:T(8,128)(2,1)S(1)}, f32[24,128]{1,0:T(8,128)S(1)}) custom-call(s32[1]{0:T(128)} %bitcast.me_ref, bf16[1024,3072]{1,0:T(8,128)(2,1)} %get-tuple-element.197.dz_in, ...), custom_call_target="tpu_custom_call" | custom-call | flops 7247757312 | bytes 41943040 | tf_op jit(solution)/shard_map/feed_forward_in/pallas_call | solution.py:1119
  202.9 1.4 copy-done.33
  204.3 12.9 %attend_backward.2.dqkv_in.dqkv0_in = bf16[1024,1152]{1,0:T(8,128)(2,1)S(1)} custom-call(s32[3,8]{1,0:T(4,128)S(1)} %copy-done.32, bf16[1024,2304]{1,0:T(8,128)(2,1)S(1)} %bitcast.17, bf16[1024,768]{1,0:T(8,128)(2,1)S(1)} %copy-done.33, f32[48,2,256]{2,1,0:T(2,128)S(1)} %copy-done.35, f32[8,128]{1,0:T(8,128)S(1)} %copy-done.31), custom_call_target="tpu_custom_call" | custom-call | flops 3221225472 | bytes 14680064 | tf_op jit(solution)/shard_map/attend_backward/pallas_call | solution.py:1227
  217.2 3.2 %qkv_weight_grad.1 = (bf16[16,9,16,128]{3,2,1,0:T(8,128)(2,1)S(1)}, bf16[16,9,16,128]{3,2,1,0:T(8,128)(2,1)S(1)}, bf16[16,9,16,128]{3,2,1,0:T(8,128)(2,1)S(1)}, bf16[16,9,16,128]{3,2,1,0:T(8,128)(2,1)S(1)}) custom-call(s32[1]{0:T(128)} %bitcast.me_ref, bf16[1024,768]{1,0:T(8,128)(2,1)S(1)} %copy-done.37, ...), custom_call_target="tpu_custom_call" | custom-call | flops 1811939328 | bytes 7864320 | tf_op jit(solution)/shard_map/qkv_weight_grad/pallas_call | solution.py:1287
  220.5 1.5 add_convert_fusion.3
  222.3 1.3 add_convert_fusion.2
  225.1 13.1 %attend_backward.3.dqkv1_in = bf16[1024,1152]{1,0:T(8,128)(2,1)S(1)} custom-call(s32[3,8]{1,0:T(4,128)S(1)} %copy-done.32, bf16[1024,2304]{1,0:T(8,128)(2,1)S(1)} %bitcast.17, bf16[1024,768]{1,0:T(8,128)(2,1)S(1)} %copy-done.33, f32[48,2,256]{2,1,0:T(2,128)S(1)} %copy-done.35, f32[8,128]{1,0:T(8,128)S(1)} %copy-done.31), custom_call_target="tpu_custom_call" | custom-call | flops 3221225472 | bytes 14680064 | tf_op jit(solution)/shard_map/attend_backward/pallas_call | solution.py:1227
  238.7 1.8 convert_add_fusion
  240.4 1.4 convert_add_fusion.1
  244.3 2.3 collective-permute-start.35
  246.7 12.9 %qkv_backward.1 = (f32[1024,768]{1,0:T(8,128)}, bf16[16,10,16,128]{3,2,1,0:T(8,128)(2,1)S(1)}, bf16[16,10,16,128]{3,2,1,0:T(8,128)(2,1)S(1)}, bf16[16,10,16,128]...) custom-call(s32[1]{0:T(128)} %bitcast.me_ref, bf16[1024,768]{1,0:T(8,128)(2,1)} %tokens_in.1, ...), custom_call_target="tpu_custom_call" | custom-call | flops 5435817984 | bytes 23592960 | tf_op jit(solution)/shard_map/qkv_backward/pallas_call | solution.py:1403
  262.0 3.8 %collective-permute-start.38 = (bf16[16,10,16,128]{3,2,1,0:T(8,128)(2,1)S(1)}, bf16[16,10,16,128]{3,2,1,0:T(8,128)(2,1)S(1)}, u32[]{:S(2)}, u32[]{:S(2)}) collective-permute-start(bf16[16,10,16,128]{3,2,1,0:T(8,128)(2,1)S(1)} %get-tuple-element.252), channel_id=1, source_target_pairs={{0,8},{1,9},{2,10},{3,11},{4,12},{5,13},{6,14},{7,15},{8,0},{9,1},... | collective-permute-start | bytes 1966088 | tf_op jit(solution)/shard_map/ppermute | solution.py:1437
  266.0 1.5 collective-permute-done.38
  270.0 1.4 collective-permute-start.44
  271.4 2.1 collective-permute-start.45
  273.5 2.4 collective-permute-done.41
  277.0 1.9 collective-permute-start.46
  281.0 2.0 collective-permute-done.46
  284.8 1.6 collective-permute-start.50
  286.3 1.4 collective-permute-start.51
  288.4 1.4 collective-permute-done.50
  289.9 1.7 collective-permute-done.51
  292.2 2.5 spread.1
  294.7 10.8 %collective-permute-start.53 = (f32[128,128]{1,0:T(8,128)}, f32[128,128]{1,0:T(8,128)S(1)}, u32[]{:S(2)}, u32[]{:S(2)}) collective-permute-start(f32[128,128]{1,0:T(8,128)} %get-tuple-element.278), channel_id=1, source_target_pairs={{1,0},{2,1},{3,2},{4,3},{5,4},{6,5},{7,6},{8,7},{9,8},{10,9},{11,1... | collective-permute-start | bytes 196616 | tf_op jit(solution)/shard_map/ppermute | solution.py:1442
  305.6 1.9 collective-permute-start.52
  307.5 6.3 %collective-permute-done.52.below = f32[72,128]{1,0:T(8,128)S(1)} collective-permute-done((f32[72,128]{1,0:T(8,128)}, f32[72,128]{1,0:T(8,128)S(1)}, u32[]{:S(2)}, u32[]{:S(2)}) %collective-permute-start.52) | collective-permute-done | bytes 36896 | tf_op jit(solution)/shard_map/ppermute | solution.py:1442
  314.4 2.2 close.1
  (234 shorter events, 35.5 us)
Async XLA Ops:
  2.1 15.8 %collective-permute-start.1 = (f32[72,128]{1,0:T(8,128)S(1)}, f32[72,128]{1,0:T(8,128)S(1)}, u32[]{:S(2)}, u32[]{:S(2)}) collective-permute-start(f32[72,128]{1,0:T(8,128)S(1)} %pad_maximum_fusion.18), channel_id=1, source_target_pairs={{1,0},{2,1},{3,2},{4,3},{5,4},{6,5},{7,6},{8,7},{9,8},{10,9},{11,1... | collective-permute-start | bytes 110600 | tf_op jit(solution)/shard_map/ppermute | solution.py:1442
  10.5 8.9 %collective-permute-start = (f32[128,128]{1,0:T(8,128)S(1)}, f32[128,128]{1,0:T(8,128)S(1)}, u32[]{:S(2)}, u32[]{:S(2)}) collective-permute-start(f32[128,128]{1,0:T(8,128)S(1)} %pad_maximum_fusion.17), channel_id=1, source_target_pairs={{0,1},{1,2},{2,3},{3,4},{4,5},{5,6},{6,7},{7,8},{8,9},{9,10},{10,1... | collective-permute-start | bytes 196616 | tf_op jit(solution)/shard_map/ppermute | solution.py:1442
  22.2 7.1 %collective-permute-start.4 = (bf16[2,19,16,128]{3,2,1,0:T(8,128)(2,1)}, bf16[2,19,16,128]{3,2,1,0:T(8,128)(2,1)S(1)}, u32[]{:S(2)}, u32[]{:S(2)}) collective-permute-start(bf16[2,19,16,128]{3,2,1,0:T(8,128)(2,1)} %get-tuple-element.141), channel_id=1, source_target_pairs={{0,6},{1,7},{2,4},{3,5},{4,2},{5,3},{6,0},{7,1},{8,14},{9,15},{10,... | collective-permute-start | bytes 466952 | tf_op jit(solution)/shard_map/ppermute | solution.py:1437
  22.2 11.6 %collective-permute-start.3 = (bf16[2,19,16,128]{3,2,1,0:T(8,128)(2,1)}, bf16[2,19,16,128]{3,2,1,0:T(8,128)(2,1)S(1)}, u32[]{:S(2)}, u32[]{:S(2)}) collective-permute-start(bf16[2,19,16,128]{3,2,1,0:T(8,128)(2,1)} %get-tuple-element.141), channel_id=1, source_target_pairs={{0,4},{1,5},{2,6},{3,7},{4,0},{5,1},{6,2},{7,3},{8,12},{9,13},{10,... | collective-permute-start | bytes 466952 | tf_op jit(solution)/shard_map/ppermute | solution.py:1437
  22.3 11.6 %collective-permute-start.2 = (bf16[2,19,16,128]{3,2,1,0:T(8,128)(2,1)}, bf16[2,19,16,128]{3,2,1,0:T(8,128)(2,1)S(1)}, u32[]{:S(2)}, u32[]{:S(2)}) collective-permute-start(bf16[2,19,16,128]{3,2,1,0:T(8,128)(2,1)} %get-tuple-element.141), channel_id=1, source_target_pairs={{0,2},{1,3},{2,0},{3,1},{4,6},{5,7},{6,4},{7,5},{8,10},{9,11},{10,... | collective-permute-start | bytes 466952 | tf_op jit(solution)/shard_map/ppermute | solution.py:1437
  34.0 8.3 %collective-permute-start.5 = (bf16[4,19,16,128]{3,2,1,0:T(8,128)(2,1)S(1)}, bf16[4,19,16,128]{3,2,1,0:T(8,128)(2,1)S(1)}, u32[]{:S(2)}, u32[]{:S(2)}) collective-permute-start(bf16[4,19,16,128]{3,2,1,0:T(8,128)(2,1)S(1)} %get-tuple-element.143), channel_id=1, source_target_pairs={{0,16},{1,17},{2,18},{3,19},{4,20},{5,21},{6,22},{7,23},{8,24},{9,... | collective-permute-start | bytes 933896 | tf_op jit(solution)/shard_map/ppermute | solution.py:1437
  36.1 7.1 %collective-permute-start.6 = (bf16[4,19,16,128]{3,2,1,0:T(8,128)(2,1)S(1)}, bf16[4,19,16,128]{3,2,1,0:T(8,128)(2,1)S(1)}, u32[]{:S(2)}, u32[]{:S(2)}) collective-permute-start(bf16[4,19,16,128]{3,2,1,0:T(8,128)(2,1)S(1)} %get-tuple-element.144), channel_id=1, source_target_pairs={{0,1},{1,0},{2,3},{3,2},{4,5},{5,4},{6,7},{7,6},{8,9},{9,8},{10,11... | collective-permute-start | bytes 933896 | tf_op jit(solution)/shard_map/ppermute | solution.py:1437
  37.4 8.8 %collective-permute-start.8 = (bf16[2,36,16,128]{3,2,1,0:T(8,128)(2,1)S(1)}, bf16[2,36,16,128]{3,2,1,0:T(8,128)(2,1)S(1)}, u32[]{:S(2)}, u32[]{:S(2)}) collective-permute-start(bf16[2,36,16,128]{3,2,1,0:T(8,128)(2,1)S(1)} %copy-done.47), channel_id=1, source_target_pairs={{0,6},{1,7},{2,4},{3,5},{4,2},{5,3},{6,0},{7,1},{8,14},{9,15},{10,... | collective-permute-start | bytes 884744 | tf_op jit(solution)/shard_map/ppermute | solution.py:1437
  39.7 14.9 %collective-permute-start.7 = (bf16[2,36,16,128]{3,2,1,0:T(8,128)(2,1)S(1)}, bf16[2,36,16,128]{3,2,1,0:T(8,128)(2,1)S(1)}, u32[]{:S(2)}, u32[]{:S(2)}) collective-permute-start(bf16[2,36,16,128]{3,2,1,0:T(8,128)(2,1)S(1)} %copy-done.47), channel_id=1, source_target_pairs={{0,2},{1,3},{2,0},{3,1},{4,6},{5,7},{6,4},{7,5},{8,10},{9,11},{10,... | collective-permute-start | bytes 884744 | tf_op jit(solution)/shard_map/ppermute | solution.py:1437
  42.3 27.5 %copy-start.4 = (bf16[8,19,16,128]{3,2,1,0:T(8,128)(2,1)}, bf16[8,19,16,128]{3,2,1,0:T(8,128)(2,1)S(1)}, u32[]{:S(2)}) copy-start(bf16[8,19,16,128]{3,2,1,0:T(8,128)(2,1)S(1)} %pad_maximum_fusion.2.refs_0_.refs_8_) | copy-start | bytes 1867780
  54.6 15.2 %collective-permute-start.13 = (bf16[2,36,16,128]{3,2,1,0:T(8,128)(2,1)S(1)}, bf16[2,36,16,128]{3,2,1,0:T(8,128)(2,1)S(1)}, u32[]{:S(2)}, u32[]{:S(2)}) collective-permute-start(bf16[2,36,16,128]{3,2,1,0:T(8,128)(2,1)S(1)} %copy-done.47), channel_id=1, source_target_pairs={{0,4},{1,5},{2,6},{3,7},{4,0},{5,1},{6,2},{7,3},{8,12},{9,13},{10,... | collective-permute-start | bytes 884744 | tf_op jit(solution)/shard_map/ppermute | solution.py:1437
  54.7 15.3 %collective-permute-start.11 = (bf16[8,19,16,128]{3,2,1,0:T(8,128)(2,1)S(1)}, bf16[8,19,16,128]{3,2,1,0:T(8,128)(2,1)S(1)}, u32[]{:S(2)}, u32[]{:S(2)}) collective-permute-start(bf16[8,19,16,128]{3,2,1,0:T(8,128)(2,1)S(1)} %pad_maximum_fusion.2.refs_0_.refs_8_), channel_id=1, source_target_pairs={{0,8},{1,9},{2,10},{3,11},{4,12},{5,13},{6,14},{7,15},{8,0},{9,1},... | collective-permute-start | bytes 1867784 | tf_op jit(solution)/shard_map/ppermute | solution.py:1437
  55.7 15.7 %collective-permute-start.9 = (bf16[8,19,16,128]{3,2,1,0:T(8,128)(2,1)S(1)}, bf16[8,19,16,128]{3,2,1,0:T(8,128)(2,1)S(1)}, u32[]{:S(2)}, u32[]{:S(2)}) collective-permute-start(bf16[8,19,16,128]{3,2,1,0:T(8,128)(2,1)S(1)} %pad_maximum_fusion.2.refs_0_.refs_8_), channel_id=1, source_target_pairs={{0,1},{1,0},{2,3},{3,2},{4,5},{5,4},{6,7},{7,6},{8,9},{9,8},{10,11... | collective-permute-start | bytes 1867784 | tf_op jit(solution)/shard_map/ppermute | solution.py:1437
  55.8 15.6 %collective-permute-start.12 = (bf16[8,19,16,128]{3,2,1,0:T(8,128)(2,1)S(1)}, bf16[8,19,16,128]{3,2,1,0:T(8,128)(2,1)S(1)}, u32[]{:S(2)}, u32[]{:S(2)}) collective-permute-start(bf16[8,19,16,128]{3,2,1,0:T(8,128)(2,1)S(1)} %pad_maximum_fusion.3.refs_4_.refs_12_), channel_id=1, source_target_pairs={{0,8},{1,9},{2,10},{3,11},{4,12},{5,13},{6,14},{7,15},{8,0},{9,1},... | collective-permute-start | bytes 1867784 | tf_op jit(solution)/shard_map/ppermute | solution.py:1437
  56.1 15.4 %collective-permute-start.10 = (bf16[8,19,16,128]{3,2,1,0:T(8,128)(2,1)S(1)}, bf16[8,19,16,128]{3,2,1,0:T(8,128)(2,1)S(1)}, u32[]{:S(2)}, u32[]{:S(2)}) collective-permute-start(bf16[8,19,16,128]{3,2,1,0:T(8,128)(2,1)S(1)} %pad_maximum_fusion.3.refs_4_.refs_12_), channel_id=1, source_target_pairs={{0,16},{1,17},{2,18},{3,19},{4,20},{5,21},{6,22},{7,23},{8,24},{9,... | collective-permute-start | bytes 1867784 | tf_op jit(solution)/shard_map/ppermute | solution.py:1437
  71.5 2.7 collective-permute-start.14
  72.6 2.6 collective-permute-start.15
  75.1 14.6 %collective-permute-start.16 = (bf16[4,36,16,128]{3,2,1,0:T(8,128)(2,1)S(1)}, bf16[4,36,16,128]{3,2,1,0:T(8,128)(2,1)}, u32[]{:S(2)}, u32[]{:S(2)}) collective-permute-start(bf16[4,36,16,128]{3,2,1,0:T(8,128)(2,1)S(1)} %pad_maximum_fusion.4), channel_id=1, source_target_pairs={{0,16},{1,17},{2,18},{3,19},{4,20},{5,21},{6,22},{7,23},{8,24},{9,... | collective-permute-start | bytes 1769480 | tf_op jit(solution)/shard_map/ppermute | solution.py:1437
  76.4 14.5 %collective-permute-start.17 = (bf16[4,36,16,128]{3,2,1,0:T(8,128)(2,1)S(1)}, bf16[4,36,16,128]{3,2,1,0:T(8,128)(2,1)S(1)}, u32[]{:S(2)}, u32[]{:S(2)}) collective-permute-start(bf16[4,36,16,128]{3,2,1,0:T(8,128)(2,1)S(1)} %pad_maximum_fusion.5), channel_id=1, source_target_pairs={{0,1},{1,0},{2,3},{3,2},{4,5},{5,4},{6,7},{7,6},{8,9},{9,8},{10,11... | collective-permute-start | bytes 1769480 | tf_op jit(solution)/shard_map/ppermute | solution.py:1437
  91.1 74.4 %copy-start.2 = (bf16[8,36,16,128]{3,2,1,0:T(8,128)(2,1)}, bf16[8,36,16,128]{3,2,1,0:T(8,128)(2,1)S(1)}, u32[]{:S(2)}) copy-start(bf16[8,36,16,128]{3,2,1,0:T(8,128)(2,1)S(1)} %pad_maximum_fusion.1.refs_4_) | copy-start | bytes 3538948
  91.1 22.3 %collective-permute-start.20 = (bf16[8,36,16,128]{3,2,1,0:T(8,128)(2,1)S(1)}, bf16[8,36,16,128]{3,2,1,0:T(8,128)(2,1)S(1)}, u32[]{:S(2)}, u32[]{:S(2)}) collective-permute-start(bf16[8,36,16,128]{3,2,1,0:T(8,128)(2,1)S(1)} %pad_maximum_fusion.refs_0_), channel_id=1, source_target_pairs={{0,8},{1,9},{2,10},{3,11},{4,12},{5,13},{6,14},{7,15},{8,0},{9,1},... | collective-permute-start | bytes 3538952 | tf_op jit(solution)/shard_map/ppermute | solution.py:1437
  92.4 27.7 %collective-permute-start.18 = (bf16[8,36,16,128]{3,2,1,0:T(8,128)(2,1)S(1)}, bf16[8,36,16,128]{3,2,1,0:T(8,128)(2,1)S(1)}, u32[]{:S(2)}, u32[]{:S(2)}) collective-permute-start(bf16[8,36,16,128]{3,2,1,0:T(8,128)(2,1)S(1)} %pad_maximum_fusion.refs_0_), channel_id=1, source_target_pairs={{0,1},{1,0},{2,3},{3,2},{4,5},{5,4},{6,7},{7,6},{8,9},{9,8},{10,11... | collective-permute-start | bytes 3538952 | tf_op jit(solution)/shard_map/ppermute | solution.py:1437
  93.8 26.2 %collective-permute-start.21 = (bf16[8,36,16,128]{3,2,1,0:T(8,128)(2,1)S(1)}, bf16[8,36,16,128]{3,2,1,0:T(8,128)(2,1)S(1)}, u32[]{:S(2)}, u32[]{:S(2)}) collective-permute-start(bf16[8,36,16,128]{3,2,1,0:T(8,128)(2,1)S(1)} %pad_maximum_fusion.1.refs_4_), channel_id=1, source_target_pairs={{0,8},{1,9},{2,10},{3,11},{4,12},{5,13},{6,14},{7,15},{8,0},{9,1},... | collective-permute-start | bytes 3538952 | tf_op jit(solution)/shard_map/ppermute | solution.py:1437
  94.2 27.5 %collective-permute-start.19 = (bf16[8,36,16,128]{3,2,1,0:T(8,128)(2,1)S(1)}, bf16[8,36,16,128]{3,2,1,0:T(8,128)(2,1)}, u32[]{:S(2)}, u32[]{:S(2)}) collective-permute-start(bf16[8,36,16,128]{3,2,1,0:T(8,128)(2,1)S(1)} %pad_maximum_fusion.1.refs_4_), channel_id=1, source_target_pairs={{0,16},{1,17},{2,18},{3,19},{4,20},{5,21},{6,22},{7,23},{8,24},{9,... | collective-permute-start | bytes 3538952 | tf_op jit(solution)/shard_map/ppermute | solution.py:1437
  95.5 31.6 %copy-start.30 = (f32[88,128]{1,0:T(8,128)S(1)}, f32[88,128]{1,0:T(8,128)}, u32[]{:S(2)}) copy-start(f32[88,128]{1,0:T(8,128)} %get-tuple-element.174.small) | copy-start | bytes 135172
  113.4 52.1 %copy-start.8 = (bf16[8,36,16,128]{3,2,1,0:T(8,128)(2,1)}, bf16[8,36,16,128]{3,2,1,0:T(8,128)(2,1)S(1)}, u32[]{:S(2)}) copy-start(bf16[8,36,16,128]{3,2,1,0:T(8,128)(2,1)S(1)} %collective-permute-done.20.refs_2_) | copy-start | bytes 3538948
  120.0 45.5 %copy-start.10 = (bf16[8,36,16,128]{3,2,1,0:T(8,128)(2,1)}, bf16[8,36,16,128]{3,2,1,0:T(8,128)(2,1)S(1)}, u32[]{:S(2)}) copy-start(bf16[8,36,16,128]{3,2,1,0:T(8,128)(2,1)S(1)} %collective-permute-done.18.refs_1_) | copy-start | bytes 3538948
  120.0 45.5 %copy-start.12 = (bf16[8,36,16,128]{3,2,1,0:T(8,128)(2,1)}, bf16[8,36,16,128]{3,2,1,0:T(8,128)(2,1)S(1)}, u32[]{:S(2)}) copy-start(bf16[8,36,16,128]{3,2,1,0:T(8,128)(2,1)S(1)} %collective-permute-done.21.refs_6_) | copy-start | bytes 3538948
  121.7 5.1 %collective-permute-start.22 = (bf16[8,36,16,128]{3,2,1,0:T(8,128)(2,1)S(1)}, bf16[8,36,16,128]{3,2,1,0:T(8,128)(2,1)S(1)}, u32[]{:S(2)}, u32[]{:S(2)}) collective-permute-start(bf16[8,36,16,128]{3,2,1,0:T(8,128)(2,1)S(1)} %collective-permute-done.18.refs_1_), channel_id=1, source_target_pairs={{0,8},{1,9},{2,10},{3,11},{4,12},{5,13},{6,14},{7,15},{8,0},{9,1},... | collective-permute-start | bytes 3538952 | tf_op jit(solution)/shard_map/ppermute | solution.py:1437
  122.7 4.4 %collective-permute-start.23 = (bf16[8,36,16,128]{3,2,1,0:T(8,128)(2,1)}, bf16[8,36,16,128]{3,2,1,0:T(8,128)(2,1)S(1)}, u32[]{:S(2)}, u32[]{:S(2)}) collective-permute-start(bf16[8,36,16,128]{3,2,1,0:T(8,128)(2,1)} %collective-permute-done.19.refs_5_), channel_id=1, source_target_pairs={{0,8},{1,9},{2,10},{3,11},{4,12},{5,13},{6,14},{7,15},{8,0},{9,1},... | collective-permute-start | bytes 3538952 | tf_op jit(solution)/shard_map/ppermute | solution.py:1437
  126.8 37.5 %copy-start.13 = (bf16[8,36,16,128]{3,2,1,0:T(8,128)(2,1)}, bf16[8,36,16,128]{3,2,1,0:T(8,128)(2,1)S(1)}, u32[]{:S(2)}) copy-start(bf16[8,36,16,128]{3,2,1,0:T(8,128)(2,1)S(1)} %collective-permute-done.22.refs_3_) | copy-start | bytes 3538948
  127.0 37.2 %copy-start.15 = (bf16[8,36,16,128]{3,2,1,0:T(8,128)(2,1)}, bf16[8,36,16,128]{3,2,1,0:T(8,128)(2,1)S(1)}, u32[]{:S(2)}) copy-start(bf16[8,36,16,128]{3,2,1,0:T(8,128)(2,1)S(1)} %collective-permute-done.23.refs_7_) | copy-start | bytes 3538948
  129.1 36.5 %copy-start = (bf16[1024,768]{1,0:T(8,128)(2,1)S(1)}, bf16[1024,768]{1,0:T(8,128)(2,1)}, u32[]{:S(2)}) copy-start(bf16[1024,768]{1,0:T(8,128)(2,1)} %cot_in.3) | copy-start | bytes 4718596
  129.1 36.5 %copy-start.1 = (f32[1024,768]{1,0:T(8,128)S(1)}, f32[1024,768]{1,0:T(8,128)}, u32[]{:S(2)}) copy-start(f32[1024,768]{1,0:T(8,128)} %get-tuple-element.185.x1_in) | copy-start | bytes 9437188
  164.3 17.3 %collective-permute-start.24 = (bf16[16,36,16,128]{3,2,1,0:T(8,128)(2,1)}, bf16[16,36,16,128]{3,2,1,0:T(8,128)(2,1)S(1)}, u32[]{:S(2)}, u32[]{:S(2)}) collective-permute-start(bf16[16,36,16,128]{3,2,1,0:T(8,128)(2,1)} %get-tuple-element.189), channel_id=1, source_target_pairs={{0,8},{1,9},{2,10},{3,11},{4,12},{5,13},{6,14},{7,15},{8,0},{9,1},... | collective-permute-start | bytes 7077896 | tf_op jit(solution)/shard_map/ppermute | solution.py:1437
  165.4 16.2 %collective-permute-start.25 = (bf16[16,36,16,128]{3,2,1,0:T(8,128)(2,1)}, bf16[16,36,16,128]{3,2,1,0:T(8,128)(2,1)S(1)}, u32[]{:S(2)}, u32[]{:S(2)}) collective-permute-start(bf16[16,36,16,128]{3,2,1,0:T(8,128)(2,1)} %get-tuple-element.190), channel_id=1, source_target_pairs={{0,8},{1,9},{2,10},{3,11},{4,12},{5,13},{6,14},{7,15},{8,0},{9,1},... | collective-permute-start | bytes 7077896 | tf_op jit(solution)/shard_map/ppermute | solution.py:1437
  183.8 36.7 %collective-permute-start.26 = (bf16[8,36,16,128]{3,2,1,0:T(8,128)(2,1)}, bf16[8,36,16,128]{3,2,1,0:T(8,128)(2,1)}, u32[]{:S(2)}, u32[]{:S(2)}) collective-permute-start(bf16[8,36,16,128]{3,2,1,0:T(8,128)(2,1)} %add_convert_fusion.1), channel_id=1, source_target_pairs={{0,1},{1,0},{2,3},{3,2},{4,5},{5,4},{6,7},{7,6},{8,9},{9,8},{10,11... | collective-permute-start | bytes 3538952 | tf_op jit(solution)/shard_map/ppermute | solution.py:1437
  183.8 36.6 %collective-permute-start.27 = (bf16[8,36,16,128]{3,2,1,0:T(8,128)(2,1)S(1)}, bf16[8,36,16,128]{3,2,1,0:T(8,128)(2,1)}, u32[]{:S(2)}, u32[]{:S(2)}) collective-permute-start(bf16[8,36,16,128]{3,2,1,0:T(8,128)(2,1)S(1)} %add_convert_fusion), channel_id=1, source_target_pairs={{0,16},{1,17},{2,18},{3,19},{4,20},{5,21},{6,22},{7,23},{8,24},{9,... | collective-permute-start | bytes 3538952 | tf_op jit(solution)/shard_map/ppermute | solution.py:1437
  223.6 15.0 %collective-permute-start.28 = (bf16[4,36,16,128]{3,2,1,0:T(8,128)(2,1)S(1)}, bf16[4,36,16,128]{3,2,1,0:T(8,128)(2,1)S(1)}, u32[]{:S(2)}, u32[]{:S(2)}) collective-permute-start(bf16[4,36,16,128]{3,2,1,0:T(8,128)(2,1)S(1)} %add_convert_fusion.3), channel_id=1, source_target_pairs={{0,16},{1,17},{2,18},{3,19},{4,20},{5,21},{6,22},{7,23},{8,24},{9,... | collective-permute-start | bytes 1769480 | tf_op jit(solution)/shard_map/ppermute | solution.py:1437
  224.3 14.3 %collective-permute-start.29 = (bf16[4,36,16,128]{3,2,1,0:T(8,128)(2,1)S(1)}, bf16[4,36,16,128]{3,2,1,0:T(8,128)(2,1)S(1)}, u32[]{:S(2)}, u32[]{:S(2)}) collective-permute-start(bf16[4,36,16,128]{3,2,1,0:T(8,128)(2,1)S(1)} %add_convert_fusion.2), channel_id=1, source_target_pairs={{0,1},{1,0},{2,3},{3,2},{4,5},{5,4},{6,7},{7,6},{8,9},{9,8},{10,11... | collective-permute-start | bytes 1769480 | tf_op jit(solution)/shard_map/ppermute | solution.py:1437
  224.3 14.3 %collective-permute-start.30 = (bf16[16,9,16,128]{3,2,1,0:T(8,128)(2,1)S(1)}, bf16[16,9,16,128]{3,2,1,0:T(8,128)(2,1)S(1)}, u32[]{:S(2)}, u32[]{:S(2)}) collective-permute-start(bf16[16,9,16,128]{3,2,1,0:T(8,128)(2,1)S(1)} %get-tuple-element.220), channel_id=1, source_target_pairs={{0,8},{1,9},{2,10},{3,11},{4,12},{5,13},{6,14},{7,15},{8,0},{9,1},... | collective-permute-start | bytes 1769480 | tf_op jit(solution)/shard_map/ppermute | solution.py:1437
  225.1 13.6 %collective-permute-start.31 = (bf16[16,9,16,128]{3,2,1,0:T(8,128)(2,1)S(1)}, bf16[16,9,16,128]{3,2,1,0:T(8,128)(2,1)S(1)}, u32[]{:S(2)}, u32[]{:S(2)}) collective-permute-start(bf16[16,9,16,128]{3,2,1,0:T(8,128)(2,1)S(1)} %get-tuple-element.221), channel_id=1, source_target_pairs={{0,8},{1,9},{2,10},{3,11},{4,12},{5,13},{6,14},{7,15},{8,0},{9,1},... | collective-permute-start | bytes 1769480 | tf_op jit(solution)/shard_map/ppermute | solution.py:1437
  242.2 17.4 %collective-permute-start.32 = (bf16[8,9,16,128]{3,2,1,0:T(8,128)(2,1)S(1)}, bf16[8,9,16,128]{3,2,1,0:T(8,128)(2,1)S(1)}, u32[]{:S(2)}, u32[]{:S(2)}) collective-permute-start(bf16[8,9,16,128]{3,2,1,0:T(8,128)(2,1)S(1)} %add_convert_fusion.7), channel_id=1, source_target_pairs={{0,1},{1,0},{2,3},{3,2},{4,5},{5,4},{6,7},{7,6},{8,9},{9,8},{10,11... | collective-permute-start | bytes 884744 | tf_op jit(solution)/shard_map/ppermute | solution.py:1437
  243.0 16.6 %collective-permute-start.33 = (bf16[8,9,16,128]{3,2,1,0:T(8,128)(2,1)S(1)}, bf16[8,9,16,128]{3,2,1,0:T(8,128)(2,1)S(1)}, u32[]{:S(2)}, u32[]{:S(2)}) collective-permute-start(bf16[8,9,16,128]{3,2,1,0:T(8,128)(2,1)S(1)} %add_convert_fusion.6), channel_id=1, source_target_pairs={{0,16},{1,17},{2,18},{3,19},{4,20},{5,21},{6,22},{7,23},{8,24},{9,... | collective-permute-start | bytes 884744 | tf_op jit(solution)/shard_map/ppermute | solution.py:1437
  243.8 15.8 %collective-permute-start.34 = (bf16[2,36,16,128]{3,2,1,0:T(8,128)(2,1)S(1)}, bf16[2,36,16,128]{3,2,1,0:T(8,128)(2,1)S(1)}, u32[]{:S(2)}, u32[]{:S(2)}) collective-permute-start(bf16[2,36,16,128]{3,2,1,0:T(8,128)(2,1)S(1)} %pad_maximum_fusion.8), channel_id=1, source_target_pairs={{0,2},{1,3},{2,0},{3,1},{4,6},{5,7},{6,4},{7,5},{8,10},{9,11},{10,... | collective-permute-start | bytes 884744 | tf_op jit(solution)/shard_map/ppermute | solution.py:1437
  244.3 15.3 %collective-permute-start.35 = (bf16[2,36,16,128]{3,2,1,0:T(8,128)(2,1)S(1)}, bf16[2,36,16,128]{3,2,1,0:T(8,128)(2,1)S(1)}, u32[]{:S(2)}, u32[]{:S(2)}) collective-permute-start(bf16[2,36,16,128]{3,2,1,0:T(8,128)(2,1)S(1)} %pad_maximum_fusion.9), channel_id=1, source_target_pairs={{0,4},{1,5},{2,6},{3,7},{4,0},{5,1},{6,2},{7,3},{8,12},{9,13},{10,... | collective-permute-start | bytes 884744 | tf_op jit(solution)/shard_map/ppermute | solution.py:1437
  259.8 6.0 %collective-permute-start.36 = (bf16[4,9,16,128]{3,2,1,0:T(8,128)(2,1)S(1)}, bf16[4,9,16,128]{3,2,1,0:T(8,128)(2,1)S(1)}, u32[]{:S(2)}, u32[]{:S(2)}) collective-permute-start(bf16[4,9,16,128]{3,2,1,0:T(8,128)(2,1)S(1)} %add_convert_fusion.11), channel_id=1, source_target_pairs={{0,16},{1,17},{2,18},{3,19},{4,20},{5,21},{6,22},{7,23},{8,24},{9,... | collective-permute-start | bytes 442376 | tf_op jit(solution)/shard_map/ppermute | solution.py:1437
  260.3 8.2 %collective-permute-start.40 = (bf16[36,16,128]{2,1,0:T(8,128)(2,1)S(1)}, bf16[36,16,128]{2,1,0:T(8,128)(2,1)S(1)}, u32[]{:S(2)}, u32[]{:S(2)}) collective-permute-start(bf16[36,16,128]{2,1,0:T(8,128)(2,1)S(1)} %slice_bitcast_fusion.1), channel_id=1, source_target_pairs={{0,6},{1,7},{2,4},{3,5},{4,2},{5,3},{6,0},{7,1},{8,14},{9,15},{10,... | collective-permute-start | bytes 442376 | tf_op jit(solution)/shard_map/ppermute | solution.py:1437
  261.3 4.6 %collective-permute-start.37 = (bf16[4,9,16,128]{3,2,1,0:T(8,128)(2,1)S(1)}, bf16[4,9,16,128]{3,2,1,0:T(8,128)(2,1)S(1)}, u32[]{:S(2)}, u32[]{:S(2)}) collective-permute-start(bf16[4,9,16,128]{3,2,1,0:T(8,128)(2,1)S(1)} %add_convert_fusion.10), channel_id=1, source_target_pairs={{0,1},{1,0},{2,3},{3,2},{4,5},{5,4},{6,7},{7,6},{8,9},{9,8},{10,11... | collective-permute-start | bytes 442376 | tf_op jit(solution)/shard_map/ppermute | solution.py:1437
  262.0 5.5 %collective-permute-start.38 = (bf16[16,10,16,128]{3,2,1,0:T(8,128)(2,1)S(1)}, bf16[16,10,16,128]{3,2,1,0:T(8,128)(2,1)S(1)}, u32[]{:S(2)}, u32[]{:S(2)}) collective-permute-start(bf16[16,10,16,128]{3,2,1,0:T(8,128)(2,1)S(1)} %get-tuple-element.252), channel_id=1, source_target_pairs={{0,8},{1,9},{2,10},{3,11},{4,12},{5,13},{6,14},{7,15},{8,0},{9,1},... | collective-permute-start | bytes 1966088 | tf_op jit(solution)/shard_map/ppermute | solution.py:1437
  265.8 2.7 collective-permute-start.39
  268.6 7.4 %collective-permute-start.41 = (bf16[8,10,16,128]{3,2,1,0:T(8,128)(2,1)S(1)}, bf16[8,10,16,128]{3,2,1,0:T(8,128)(2,1)S(1)}, u32[]{:S(2)}, u32[]{:S(2)}) collective-permute-start(bf16[8,10,16,128]{3,2,1,0:T(8,128)(2,1)S(1)} %add_convert_fusion.5), channel_id=1, source_target_pairs={{0,1},{1,0},{2,3},{3,2},{4,5},{5,4},{6,7},{7,6},{8,9},{9,8},{10,11... | collective-permute-start | bytes 983048 | tf_op jit(solution)/shard_map/ppermute | solution.py:1437
  269.5 7.3 %collective-permute-start.42 = (bf16[8,10,16,128]{3,2,1,0:T(8,128)(2,1)S(1)}, bf16[8,10,16,128]{3,2,1,0:T(8,128)(2,1)S(1)}, u32[]{:S(2)}, u32[]{:S(2)}) collective-permute-start(bf16[8,10,16,128]{3,2,1,0:T(8,128)(2,1)S(1)} %add_convert_fusion.4), channel_id=1, source_target_pairs={{0,16},{1,17},{2,18},{3,19},{4,20},{5,21},{6,22},{7,23},{8,24},{9,... | collective-permute-start | bytes 983048 | tf_op jit(solution)/shard_map/ppermute | solution.py:1437
  270.0 6.9 %collective-permute-start.43 = (bf16[2,9,16,128]{3,2,1,0:T(8,128)(2,1)S(1)}, bf16[2,9,16,128]{3,2,1,0:T(8,128)(2,1)S(1)}, u32[]{:S(2)}, u32[]{:S(2)}) collective-permute-start(bf16[2,9,16,128]{3,2,1,0:T(8,128)(2,1)S(1)} %pad_maximum_fusion.14), channel_id=1, source_target_pairs={{0,2},{1,3},{2,0},{3,1},{4,6},{5,7},{6,4},{7,5},{8,10},{9,11},{10,... | collective-permute-start | bytes 221192 | tf_op jit(solution)/shard_map/ppermute | solution.py:1437
  270.0 6.9 %collective-permute-start.44 = (bf16[2,9,16,128]{3,2,1,0:T(8,128)(2,1)S(1)}, bf16[2,9,16,128]{3,2,1,0:T(8,128)(2,1)S(1)}, u32[]{:S(2)}, u32[]{:S(2)}) collective-permute-start(bf16[2,9,16,128]{3,2,1,0:T(8,128)(2,1)S(1)} %pad_maximum_fusion.15), channel_id=1, source_target_pairs={{0,4},{1,5},{2,6},{3,7},{4,0},{5,1},{6,2},{7,3},{8,12},{9,13},{10,... | collective-permute-start | bytes 221192 | tf_op jit(solution)/shard_map/ppermute | solution.py:1437
  271.4 5.5 %collective-permute-start.45 = (bf16[2,9,16,128]{3,2,1,0:T(8,128)(2,1)S(1)}, bf16[2,9,16,128]{3,2,1,0:T(8,128)(2,1)S(1)}, u32[]{:S(2)}, u32[]{:S(2)}) collective-permute-start(bf16[2,9,16,128]{3,2,1,0:T(8,128)(2,1)S(1)} %pad_maximum_fusion.16), channel_id=1, source_target_pairs={{0,6},{1,7},{2,4},{3,5},{4,2},{5,3},{6,0},{7,1},{8,14},{9,15},{10,... | collective-permute-start | bytes 221192 | tf_op jit(solution)/shard_map/ppermute | solution.py:1437
  277.0 6.0 %collective-permute-start.46 = (bf16[36,16,128]{2,1,0:T(8,128)(2,1)S(1)}, bf16[36,16,128]{2,1,0:T(8,128)(2,1)S(1)}, u32[]{:S(2)}, u32[]{:S(2)}) collective-permute-start(bf16[36,16,128]{2,1,0:T(8,128)(2,1)S(1)} %slice_bitcast_fusion), channel_id=1, source_target_pairs={{0,6},{1,7},{2,4},{3,5},{4,2},{5,3},{6,0},{7,1},{8,14},{9,15},{10,... | collective-permute-start | bytes 442376 | tf_op jit(solution)/shard_map/ppermute | solution.py:1437
  278.9 5.0 %collective-permute-start.47 = (bf16[4,10,16,128]{3,2,1,0:T(8,128)(2,1)S(1)}, bf16[4,10,16,128]{3,2,1,0:T(8,128)(2,1)S(1)}, u32[]{:S(2)}, u32[]{:S(2)}) collective-permute-start(bf16[4,10,16,128]{3,2,1,0:T(8,128)(2,1)S(1)} %add_convert_fusion.9), channel_id=1, source_target_pairs={{0,16},{1,17},{2,18},{3,19},{4,20},{5,21},{6,22},{7,23},{8,24},{9,... | collective-permute-start | bytes 491528 | tf_op jit(solution)/shard_map/ppermute | solution.py:1437
  279.7 4.3 %collective-permute-start.48 = (bf16[4,10,16,128]{3,2,1,0:T(8,128)(2,1)S(1)}, bf16[4,10,16,128]{3,2,1,0:T(8,128)(2,1)S(1)}, u32[]{:S(2)}, u32[]{:S(2)}) collective-permute-start(bf16[4,10,16,128]{3,2,1,0:T(8,128)(2,1)S(1)} %add_convert_fusion.8), channel_id=1, source_target_pairs={{0,1},{1,0},{2,3},{3,2},{4,5},{5,4},{6,7},{7,6},{8,9},{9,8},{10,11... | collective-permute-start | bytes 491528 | tf_op jit(solution)/shard_map/ppermute | solution.py:1437
  284.2 4.3 %collective-permute-start.49 = (bf16[2,10,16,128]{3,2,1,0:T(8,128)(2,1)S(1)}, bf16[2,10,16,128]{3,2,1,0:T(8,128)(2,1)S(1)}, u32[]{:S(2)}, u32[]{:S(2)}) collective-permute-start(bf16[2,10,16,128]{3,2,1,0:T(8,128)(2,1)S(1)} %pad_maximum_fusion.11), channel_id=1, source_target_pairs={{0,2},{1,3},{2,0},{3,1},{4,6},{5,7},{6,4},{7,5},{8,10},{9,11},{10,... | collective-permute-start | bytes 245768 | tf_op jit(solution)/shard_map/ppermute | solution.py:1437
  284.8 5.1 %collective-permute-start.50 = (bf16[2,10,16,128]{3,2,1,0:T(8,128)(2,1)S(1)}, bf16[2,10,16,128]{3,2,1,0:T(8,128)(2,1)S(1)}, u32[]{:S(2)}, u32[]{:S(2)}) collective-permute-start(bf16[2,10,16,128]{3,2,1,0:T(8,128)(2,1)S(1)} %pad_maximum_fusion.12), channel_id=1, source_target_pairs={{0,4},{1,5},{2,6},{3,7},{4,0},{5,1},{6,2},{7,3},{8,12},{9,13},{10,... | collective-permute-start | bytes 245768 | tf_op jit(solution)/shard_map/ppermute | solution.py:1437
  286.3 5.2 %collective-permute-start.51 = (bf16[2,10,16,128]{3,2,1,0:T(8,128)(2,1)S(1)}, bf16[2,10,16,128]{3,2,1,0:T(8,128)(2,1)S(1)}, u32[]{:S(2)}, u32[]{:S(2)}) collective-permute-start(bf16[2,10,16,128]{3,2,1,0:T(8,128)(2,1)S(1)} %pad_maximum_fusion.13), channel_id=1, source_target_pairs={{0,6},{1,7},{2,4},{3,5},{4,2},{5,3},{6,0},{7,1},{8,14},{9,15},{10,... | collective-permute-start | bytes 245768 | tf_op jit(solution)/shard_map/ppermute | solution.py:1437
  294.7 19.0 %collective-permute-start.53 = (f32[128,128]{1,0:T(8,128)}, f32[128,128]{1,0:T(8,128)S(1)}, u32[]{:S(2)}, u32[]{:S(2)}) collective-permute-start(f32[128,128]{1,0:T(8,128)} %get-tuple-element.278), channel_id=1, source_target_pairs={{1,0},{2,1},{3,2},{4,3},{5,4},{6,5},{7,6},{8,7},{9,8},{10,9},{11,1... | collective-permute-start | bytes 196616 | tf_op jit(solution)/shard_map/ppermute | solution.py:1442
  305.6 8.2 %collective-permute-start.52 = (f32[72,128]{1,0:T(8,128)}, f32[72,128]{1,0:T(8,128)S(1)}, u32[]{:S(2)}, u32[]{:S(2)}) collective-permute-start(f32[72,128]{1,0:T(8,128)} %get-tuple-element.277), channel_id=1, source_target_pairs={{0,1},{1,2},{2,3},{3,4},{4,5},{5,6},{6,7},{7,8},{8,9},{9,10},{10,1... | collective-permute-start | bytes 110600 | tf_op jit(solution)/shard_map/ppermute | solution.py:1442
  (45 other events, 301.9 us)
where the time goes:
time: 321 us; the launch traced here: 317 us
  Pallas kernels  139 us (43%)
  waiting for transfers between devices  72.2 us (22%)
  starting transfers between devices  69.5 us (22%)
  local copies, waits for them, and re-layouts  18 us (6%)
  other arithmetic  15.6 us (5%)
    ppermute x50, waiting for transfers between devices, exchange(): return lax.ppermute(values, AXES, [(d, d ^ bit) for d in range(BLOCKS)])  64.4 us
    ppermute x50, starting transfers between devices, exchange(): return lax.ppermute(values, AXES, [(d, d ^ bit) for d in range(BLOCKS)])  47.3 us
    pallas_call x1, Pallas kernels, feed_forward(): pl.pallas_call(mlp_kernel, out_shape=(shape((rows, FF), BF16), shape((row...  35.2 us
    pallas_call x2, Pallas kernels, attend_back(): pl.pallas_call(partial(attend_back_kernel, group), out_shape=shape((rows,...  26 us
    ppermute x4, starting transfers between devices, shifted(): return lax.ppermute(values, AXES, pairs)  22.2 us
    pallas_call x1, Pallas kernels, attend(): pl.pallas_call(attend_kernel, out_shape=(shape((rows, width), BF16), shap...  17.9 us
    pallas_call x1, Pallas kernels, split(): pl.pallas_call(split_kernel, out_shape=(shape((rows, width), F32), shape(...  16.2 us
    pallas_call x1, Pallas kernels, qkv_back(): pl.pallas_call(qkv_back_kernel, out_shape=(shape((rows, width), F32), hal...  12.9 us
  transfers between devices with their start and end apart: 54, of which 28 were waited for; matrix products, arithmetic and copies ran while one was open for 3% of the time, Pallas kernels for 31%

commit v1 on v0

--- a/solution.py
+++ b/solution.py
@@ -197,12 +197,12 @@
 def pack_kernel(att_rows, me_ref, own, tails, heads, att, mlp, win_a, win_m, table):
     me = me_ref[0]
     mlp_rows = own.shape[0] - att_rows
-    win_a[0:ATT_BEFORE, :] = tails[0:ATT_BEFORE, :]
+    win_a[0:ATT_BEFORE, :] = tails[0:ATT_BEFORE, :].astype(F32)
     win_a[ATT_BEFORE : ATT_BEFORE + att_rows, :] = own[0:att_rows, :]
-    win_a[ATT_BEFORE + att_rows :, :] = heads[0:ATT_AFTER, :]
-    win_m[0:MLP_BEFORE, :] = tails[ATT_BEFORE:, :]
+    win_a[ATT_BEFORE + att_rows :, :] = heads[0:ATT_AFTER, :].astype(F32)
+    win_m[0:MLP_BEFORE, :] = tails[ATT_BEFORE:, :].astype(F32)
     win_m[MLP_BEFORE : MLP_BEFORE + mlp_rows, :] = own[att_rows:, :]
-    win_m[MLP_BEFORE + mlp_rows :, :] = heads[ATT_AFTER:, :]
+    win_m[MLP_BEFORE + mlp_rows :, :] = heads[ATT_AFTER:, :].astype(F32)
     att_off, mlp_off = window_offsets(me, att_rows, mlp_rows)
 
     def tile(name, rt, ct, first, stride):
@@ -1163,19 +1163,26 @@
     rows = pl.ds(pl.multiple_of(b * QB, QB), QB)
     at = pl.ds(start, width)
     mask = jnp.concatenate([bias[0:width, :]] * 2, axis=1)
+    pairs = []
     for p in range(GROUP):
         lanes = slice(LANES * p, LANES * p + LANES)
         place = b * PAIRS + GROUP * group + p
         queries = head_masked(q[rows, lanes] * 0.125)
         grads = head_masked(da[rows, lanes])
+        keys, values = k[at, lanes], v[at, lanes]
+        scores = mm(keys, queries, NT)
+        dweight = mm(values, grads, NT)
+        pairs.append((lanes, place, queries, grads, keys, scores, dweight))
+    later = []
+    for lanes, place, queries, grads, keys, scores, dweight in pairs:
         highest = stats[place, 0:1, :]
         inverse = stats[place, 1:2, :]
-        keys, values = k[at, lanes], v[at, lanes]
-        weight = jnp.exp(mm(keys, queries, NT) + mask - highest) * inverse
-        dweight = mm(values, grads, NT)
+        weight = jnp.exp(scores + mask - highest) * inverse
         inner_sum = total(fold8(weight * dweight))
         dvalues[at, lanes] += mm(weight.astype(BF16), grads, NN)
         dscore = (weight * (dweight - inner_sum)).astype(BF16)
+        later.append((lanes, queries, keys, dscore))
+    for lanes, queries, keys, dscore in later:
         dkeys[at, lanes] += mm(dscore, queries, NN)
         both = mm(keys, dscore, TN)
         dq[rows, lanes] = (pick_heads(both) * 0.125).T.astype(BF16)
@@ -1647,7 +1654,7 @@
     me = lax.axis_index(AXES).astype(jnp.int32).reshape(1)
     tails = jnp.concatenate([params[att_rows - ATT_BEFORE : att_rows], params[-MLP_BEFORE:]])
     heads = jnp.concatenate([params[:ATT_AFTER], params[att_rows : att_rows + MLP_AFTER]])
-    tails, heads = shifted(tails, 1), shifted(heads, -1)
+    tails, heads = shifted(tails.astype(BF16), 1), shifted(heads.astype(BF16), -1)
     att_own, mlp_own = pack(me, params, tails, heads, att_rows)
 
     got = [exchange(att_own, k * Z0) for k in range(1, 4)]

time: 321 us -> 316 us (0.984)
  the two profiles are of different devices: /device:TPU:1 before, /device:TPU:2 now
where the time goes in v1:
time: 316 us; the launch traced here: 311 us
  Pallas kernels  135 us (43%)
  waiting for transfers between devices  82 us (26%)
  starting transfers between devices  60.8 us (19%)
  other arithmetic  15.8 us (5%)
  local copies, waits for them, and re-layouts  15.1 us (5%)
    ppermute x50, waiting for transfers between devices, exchange(): return lax.ppermute(values, AXES, [(d, d ^ bit) for d in range(BLOCKS)])  74.2 us
    ppermute x50, starting transfers between devices, exchange(): return lax.ppermute(values, AXES, [(d, d ^ bit) for d in range(BLOCKS)])  47.2 us
    pallas_call x1, Pallas kernels, feed_forward(): pl.pallas_call(mlp_kernel, out_shape=(shape((rows, FF), BF16), shape((row...  35.2 us
    pallas_call x2, Pallas kernels, attend_back(): pl.pallas_call(partial(attend_back_kernel, group), out_shape=shape((rows,...  22.2 us
    pallas_call x1, Pallas kernels, attend(): pl.pallas_call(attend_kernel, out_shape=(shape((rows, width), BF16), shap...  17.6 us
    pallas_call x1, Pallas kernels, split(): pl.pallas_call(split_kernel, out_shape=(shape((rows, width), F32), shape(...  16.1 us
    ppermute x4, starting transfers between devices, shifted(): return lax.ppermute(values, AXES, pairs)  13.6 us
    pallas_call x1, Pallas kernels, qkv_back(): pl.pallas_call(qkv_back_kernel, out_shape=(shape((rows, width), F32), hal...  12.9 us
  transfers between devices with their start and end apart: 54, of which 29 were waited for; matrix products, arithmetic and copies ran while one was open for 3% of the time, Pallas kernels for 30%

profile of v1, /device:TPU:2, one launch (start us, length us, event | category | flops | bytes accessed | tf_op | source)
XLA Modules:
  0.0 311.4 jit_solution(13377405130910790728)
XLA Ops:
  1.9 5.9 %collective-permute-start.1 = (bf16[72,128]{1,0:T(8,128)(2,1)S(1)}, bf16[72,128]{1,0:T(8,128)(2,1)S(1)}, u32[]{:S(2)}, u32[]{:S(2)}) collective-permute-start(bf16[72,128]{1,0:T(8,128)(2,1)S(1)} %pad_maximum_fusion.19), channel_id=1, source_target_pairs={{1,0},{2,1},{3,2},{4,3},{5,4},{6,5},{7,6},{8,7},{9,8},{10,9},{11,1... | collective-permute-start | bytes 55304 | tf_op jit(solution)/shard_map/ppermute | solution.py:1449
  7.8 1.9 collective-permute-start
  12.0 1.3 convert_bitcast_fusion
  14.5 2.4 collective-permute-done.tails
  17.6 2.1 pack.1
  19.8 4.3 %collective-permute-start.2 = (bf16[2,19,16,128]{3,2,1,0:T(8,128)(2,1)}, bf16[2,19,16,128]{3,2,1,0:T(8,128)(2,1)S(1)}, u32[]{:S(2)}, u32[]{:S(2)}) collective-permute-start(bf16[2,19,16,128]{3,2,1,0:T(8,128)(2,1)} %get-tuple-element.141), channel_id=1, source_target_pairs={{0,2},{1,3},{2,0},{3,1},{4,6},{5,7},{6,4},{7,5},{8,10},{9,11},{10,... | collective-permute-start | bytes 466952 | tf_op jit(solution)/shard_map/ppermute | solution.py:1444
  25.1 3.7 %collective-permute-done.4 = bf16[2,19,16,128]{3,2,1,0:T(8,128)(2,1)S(1)} collective-permute-done((bf16[2,19,16,128]{3,2,1,0:T(8,128)(2,1)}, bf16[2,19,16,128]{3,2,1,0:T(8,128)(2,1)S(1)}, u32[]{:S(2)}, u32[]{:S(2)}) %collective-permute-start.4) | collective-permute-done | bytes 155680 | tf_op jit(solution)/shard_map/ppermute | solution.py:1444
  28.7 4.5 %collective-permute-done.3 = bf16[2,19,16,128]{3,2,1,0:T(8,128)(2,1)S(1)} collective-permute-done((bf16[2,19,16,128]{3,2,1,0:T(8,128)(2,1)}, bf16[2,19,16,128]{3,2,1,0:T(8,128)(2,1)S(1)}, u32[]{:S(2)}, u32[]{:S(2)}) %collective-permute-start.3) | collective-permute-done | bytes 155680 | tf_op jit(solution)/shard_map/ppermute | solution.py:1444
  33.5 1.9 collective-permute-start.6
  35.5 2.7 collective-permute-start.8
  38.2 3.7 %collective-permute-done.5 = bf16[4,19,16,128]{3,2,1,0:T(8,128)(2,1)S(1)} collective-permute-done((bf16[4,19,16,128]{3,2,1,0:T(8,128)(2,1)S(1)}, bf16[4,19,16,128]{3,2,1,0:T(8,128)(2,1)S(1)}, u32[]{:S(2)}, u32[]{:S(2)}) %collective-permute-start.5) | collective-permute-done | bytes 311328 | tf_op jit(solution)/shard_map/ppermute | solution.py:1444
  42.8 4.4 %collective-permute-done.8 = bf16[2,36,16,128]{3,2,1,0:T(8,128)(2,1)S(1)} collective-permute-done((bf16[2,36,16,128]{3,2,1,0:T(8,128)(2,1)S(1)}, bf16[2,36,16,128]{3,2,1,0:T(8,128)(2,1)S(1)}, u32[]{:S(2)}, u32[]{:S(2)}) %collective-permute-start.8) | collective-permute-done | bytes 294944 | tf_op jit(solution)/shard_map/ppermute | solution.py:1444
  47.2 4.9 %collective-permute-done.7 = bf16[2,36,16,128]{3,2,1,0:T(8,128)(2,1)S(1)} collective-permute-done((bf16[2,36,16,128]{3,2,1,0:T(8,128)(2,1)S(1)}, bf16[2,36,16,128]{3,2,1,0:T(8,128)(2,1)S(1)}, u32[]{:S(2)}, u32[]{:S(2)}) %collective-permute-start.7) | collective-permute-done | bytes 294944 | tf_op jit(solution)/shard_map/ppermute | solution.py:1444
  54.2 13.1 %collective-permute-done.13 = bf16[2,36,16,128]{3,2,1,0:T(8,128)(2,1)S(1)} collective-permute-done((bf16[2,36,16,128]{3,2,1,0:T(8,128)(2,1)S(1)}, bf16[2,36,16,128]{3,2,1,0:T(8,128)(2,1)S(1)}, u32[]{:S(2)}, u32[]{:S(2)}) %collective-permute-start.13) | collective-permute-done | bytes 294944 | tf_op jit(solution)/shard_map/ppermute | solution.py:1444
  67.5 1.6 collective-permute-done.9.refs_1_.refs_9_
  70.0 1.5 collective-permute-done.14.refs_3_.refs_11_
  74.5 10.2 %qkv_forward.1 = (bf16[1024,768]{1,0:T(8,128)(2,1)}, bf16[1024,2304]{1,0:T(8,128)(2,1)}, f32[88,128]{1,0:T(8,128)}) custom-call(s32[1]{0:T(128)} %bitcast.me_ref, bf16[1024,768]{1,0:T(8,128)(2,1)} %tokens_in.1, bf16[8,19,16,128]{3,2,1,0:T(8,128)(2,1)} %copy-done.4, bf16[8,19,16,128]{3,2,1,0:T(8,128)(2,1)} %copy-done.19, bf16[8,19,16,128]{3,2,1,0:T(8,128)(2,1)} %copy-done.17, ...), custom_call_target="tpu_custom_call" | custom-call | flops 3623878656 | bytes 9437184 | tf_op jit(solution)/shard_map/qkv_forward/pallas_call | solution.py:430
  84.7 3.1 %collective-permute-done.16 = bf16[4,36,16,128]{3,2,1,0:T(8,128)(2,1)} collective-permute-done((bf16[4,36,16,128]{3,2,1,0:T(8,128)(2,1)S(1)}, bf16[4,36,16,128]{3,2,1,0:T(8,128)(2,1)}, u32[]{:S(2)}, u32[]{:S(2)}) %collective-permute-start.16) | collective-permute-done | bytes 589856 | tf_op jit(solution)/shard_map/ppermute | solution.py:1444
  89.3 1.8 collective-permute-start.18
  91.7 17.6 %attend_forward.1 = (bf16[1024,768]{1,0:T(8,128)(2,1)}, f32[1024,768]{1,0:T(8,128)}, bf16[1024,768]{1,0:T(8,128)(2,1)}, bf16[1024,768]{1,0:T(8,128)(2,1)}, bf16[...) custom-call(s32[1]{0:T(128)} %bitcast.me_ref, s32[3,8]{1,0:T(4,128)} %pad_add_fusion.windows, ...), custom_call_target="tpu_custom_call" | custom-call | flops 1610612736 | bytes 15728640 | tf_op jit(solution)/shard_map/attend_forward/pallas_call | solution.py:635
  109.4 8.3 %collective-permute-done.18.refs_1_ = bf16[8,36,16,128]{3,2,1,0:T(8,128)(2,1)S(1)} collective-permute-done((bf16[8,36,16,128]{3,2,1,0:T(8,128)(2,1)S(1)}, bf16[8,36,16,128]{3,2,1,0:T(8,128)(2,1)S(1)}, u32[]{:S(2)}, u32[]{:S(2)}) %collective-permute-start.18) | collective-permute-done | bytes 1179680 | tf_op jit(solution)/shard_map/ppermute | solution.py:1444
  117.7 1.9 collective-permute-done.19.refs_5_
  120.1 4.0 %collective-permute-done.22.refs_3_ = bf16[8,36,16,128]{3,2,1,0:T(8,128)(2,1)S(1)} collective-permute-done((bf16[8,36,16,128]{3,2,1,0:T(8,128)(2,1)S(1)}, bf16[8,36,16,128]{3,2,1,0:T(8,128)(2,1)S(1)}, u32[]{:S(2)}, u32[]{:S(2)}) %collective-permute-start.22) | collective-permute-done | bytes 1179680 | tf_op jit(solution)/shard_map/ppermute | solution.py:1444
  124.3 2.0 copy-done.34
  126.3 35.2 %feed_forward.1 = (bf16[1024,3072]{1,0:T(8,128)(2,1)}, bf16[1024,3072]{1,0:T(8,128)(2,1)}, f32[24,128]{1,0:T(8,128)S(1)}, bf16[16,36,16,128]{3,2,1,0:T(8,128)(2,...) custom-call(s32[1]{0:T(128)} %bitcast.me_ref, ...), custom_call_target="tpu_custom_call" | custom-call | flops 19327352832 | bytes 41943040 | tf_op jit(solution)/shard_map/feed_forward/pallas_call | solution.py:883
  162.2 2.8 copy-done.3
  165.0 1.3 copy-done.14
  166.2 1.3 copy-done.16
  167.5 10.9 %feed_forward_out.1 = (bf16[1024,768]{1,0:T(8,128)(2,1)}, f32[6,128]{1,0:T(8,128)S(1)}) custom-call(s32[1]{0:T(128)} %bitcast.me_ref, bf16[1024,3072]{1,0:T(8,128)(2,1)S(1)} %copy-done.3, f32[1024,768]{1,0:T(8,128)S(1)} %copy-done.1, bf16[1024,768]{1,0:T(8,128)(2,1)S(1)} %copy-done, f32[88,128]{1,0:T(8,128)S(1)} %copy-done.30, ...), custom_call_target="tpu_custom_call" | custom-call | flops 4831838208 | bytes 20971520 | tf_op jit(solution)/shard_map/feed_forward_out/pallas_call | solution.py:1005
  178.6 1.3 add_convert_fusion.1
  181.0 1.4 collective-permute-start.27
  183.5 16.1 %feed_forward_in.1 = (f32[1024,768]{1,0:T(8,128)}, bf16[1024,768]{1,0:T(8,128)(2,1)}, bf16[2,8,9,16,128]{4,3,2,1,0:T(8,128)(2,1)S(1)}, bf16[2,8,9,16,128]{4,3,2,1,0:T(8,128)(2,1)S(1)}, f32[24,128]{1,0:T(8,128)S(1)}) custom-call(s32[1]{0:T(128)} %bitcast.me_ref, bf16[1024,3072]{1,0:T(8,128)(2,1)} %get-tuple-element.197.dz_in, ...), custom_call_target="tpu_custom_call" | custom-call | flops 7247757312 | bytes 41943040 | tf_op jit(solution)/shard_map/feed_forward_in/pallas_call | solution.py:1119
  199.8 1.4 copy-done.33
  201.2 11.0 %attend_backward.2.dqkv_in.dqkv0_in = bf16[1024,1152]{1,0:T(8,128)(2,1)S(1)} custom-call(s32[3,8]{1,0:T(4,128)S(1)} %copy-done.32, bf16[1024,2304]{1,0:T(8,128)(2,1)S(1)} %bitcast.17, bf16[1024,768]{1,0:T(8,128)(2,1)S(1)} %copy-done.33, f32[48,2,256]{2,1,0:T(2,128)S(1)} %copy-done.35, f32[8,128]{1,0:T(8,128)S(1)} %copy-done.31), custom_call_target="tpu_custom_call" | custom-call | flops 3221225472 | bytes 14680064 | tf_op jit(solution)/shard_map/attend_backward/pallas_call | solution.py:1234
  212.2 3.2 %qkv_weight_grad.1 = (bf16[16,9,16,128]{3,2,1,0:T(8,128)(2,1)S(1)}, bf16[16,9,16,128]{3,2,1,0:T(8,128)(2,1)S(1)}, bf16[16,9,16,128]{3,2,1,0:T(8,128)(2,1)S(1)}, bf16[16,9,16,128]{3,2,1,0:T(8,128)(2,1)S(1)}) custom-call(s32[1]{0:T(128)} %bitcast.me_ref, bf16[1024,768]{1,0:T(8,128)(2,1)S(1)} %copy-done.37, ...), custom_call_target="tpu_custom_call" | custom-call | flops 1811939328 | bytes 7864320 | tf_op jit(solution)/shard_map/qkv_weight_grad/pallas_call | solution.py:1294
  215.5 1.5 add_convert_fusion.3
  217.3 1.3 add_convert_fusion.2
  218.7 1.3 collective-permute-start.29
  220.5 11.2 %attend_backward.3.dqkv1_in = bf16[1024,1152]{1,0:T(8,128)(2,1)S(1)} custom-call(s32[3,8]{1,0:T(4,128)S(1)} %copy-done.32, bf16[1024,2304]{1,0:T(8,128)(2,1)S(1)} %bitcast.17, bf16[1024,768]{1,0:T(8,128)(2,1)S(1)} %copy-done.33, f32[48,2,256]{2,1,0:T(2,128)S(1)} %copy-done.35, f32[8,128]{1,0:T(8,128)S(1)} %copy-done.31), custom_call_target="tpu_custom_call" | custom-call | flops 3221225472 | bytes 14680064 | tf_op jit(solution)/shard_map/attend_backward/pallas_call | solution.py:1234
  231.8 1.9 collective-permute-done.28
  233.7 1.4 convert_add_fusion
  235.2 1.4 convert_add_fusion.1
  236.9 1.3 collective-permute-start.32
  240.2 1.6 collective-permute-start.35
  241.8 12.9 %qkv_backward.1 = (f32[1024,768]{1,0:T(8,128)}, bf16[16,10,16,128]{3,2,1,0:T(8,128)(2,1)S(1)}, bf16[16,10,16,128]{3,2,1,0:T(8,128)(2,1)S(1)}, bf16[16,10,16,128]...) custom-call(s32[1]{0:T(128)} %bitcast.me_ref, bf16[1024,768]{1,0:T(8,128)(2,1)} %tokens_in.1, ...), custom_call_target="tpu_custom_call" | custom-call | flops 5435817984 | bytes 23592960 | tf_op jit(solution)/shard_map/qkv_backward/pallas_call | solution.py:1410
  255.8 3.0 collective-permute-start.40
  258.9 1.5 collective-permute-start.37
  261.0 3.0 collective-permute-done.37
  264.4 1.6 collective-permute-start.41
  266.0 1.5 collective-permute-start.42
  267.6 1.8 collective-permute-start.44
  269.4 2.5 collective-permute-start.45
  271.9 1.5 collective-permute-done.41
  273.7 2.0 collective-permute-done.45
  275.7 2.5 collective-permute-start.46
  279.9 3.0 collective-permute-done.46
  284.3 3.5 %collective-permute-start.50 = (bf16[2,10,16,128]{3,2,1,0:T(8,128)(2,1)S(1)}, bf16[2,10,16,128]{3,2,1,0:T(8,128)(2,1)S(1)}, u32[]{:S(2)}, u32[]{:S(2)}) collective-permute-start(bf16[2,10,16,128]{3,2,1,0:T(8,128)(2,1)S(1)} %pad_maximum_fusion.12), channel_id=1, source_target_pairs={{0,4},{1,5},{2,6},{3,7},{4,0},{5,1},{6,2},{7,3},{8,12},{9,13},{10,... | collective-permute-start | bytes 245768 | tf_op jit(solution)/shard_map/ppermute | solution.py:1444
  288.7 1.5 collective-permute-done.50
  290.2 3.8 %collective-permute-done.51 = bf16[2,10,16,128]{3,2,1,0:T(8,128)(2,1)S(1)} collective-permute-done((bf16[2,10,16,128]{3,2,1,0:T(8,128)(2,1)S(1)}, bf16[2,10,16,128]{3,2,1,0:T(8,128)(2,1)S(1)}, u32[]{:S(2)}, u32[]{:S(2)}) %collective-permute-start.51) | collective-permute-done | bytes 81952 | tf_op jit(solution)/shard_map/ppermute | solution.py:1444
  294.7 2.4 spread.1
  297.1 1.9 collective-permute-start.53
  299.0 3.9 %collective-permute-start.52 = (f32[72,128]{1,0:T(8,128)}, f32[72,128]{1,0:T(8,128)S(1)}, u32[]{:S(2)}, u32[]{:S(2)}) collective-permute-start(f32[72,128]{1,0:T(8,128)} %get-tuple-element.277), channel_id=1, source_target_pairs={{0,1},{1,2},{2,3},{3,4},{4,5},{5,6},{6,7},{7,8},{8,9},{9,10},{10,1... | collective-permute-start | bytes 110600 | tf_op jit(solution)/shard_map/ppermute | solution.py:1449
  303.0 5.4 %collective-permute-done.52.below = f32[72,128]{1,0:T(8,128)S(1)} collective-permute-done((f32[72,128]{1,0:T(8,128)}, f32[72,128]{1,0:T(8,128)S(1)}, u32[]{:S(2)}, u32[]{:S(2)}) %collective-permute-start.52) | collective-permute-done | bytes 36896 | tf_op jit(solution)/shard_map/ppermute | solution.py:1449
  309.0 2.2 close.1
  (237 shorter events, 29.6 us)
Async XLA Ops:
  1.9 12.6 %collective-permute-start.1 = (bf16[72,128]{1,0:T(8,128)(2,1)S(1)}, bf16[72,128]{1,0:T(8,128)(2,1)S(1)}, u32[]{:S(2)}, u32[]{:S(2)}) collective-permute-start(bf16[72,128]{1,0:T(8,128)(2,1)S(1)} %pad_maximum_fusion.19), channel_id=1, source_target_pairs={{1,0},{2,1},{3,2},{4,3},{5,4},{6,5},{7,6},{8,7},{9,8},{10,9},{11,1... | collective-permute-start | bytes 55304 | tf_op jit(solution)/shard_map/ppermute | solution.py:1449
  7.8 9.2 %collective-permute-start = (bf16[128,128]{1,0:T(8,128)(2,1)S(1)}, bf16[128,128]{1,0:T(8,128)(2,1)S(1)}, u32[]{:S(2)}, u32[]{:S(2)}) collective-permute-start(bf16[128,128]{1,0:T(8,128)(2,1)S(1)} %pad_maximum_fusion.17), channel_id=1, source_target_pairs={{0,1},{1,2},{2,3},{3,4},{4,5},{5,6},{6,7},{7,8},{8,9},{9,10},{10,1... | collective-permute-start | bytes 98312 | tf_op jit(solution)/shard_map/ppermute | solution.py:1449
  19.7 9.0 %collective-permute-start.4 = (bf16[2,19,16,128]{3,2,1,0:T(8,128)(2,1)}, bf16[2,19,16,128]{3,2,1,0:T(8,128)(2,1)S(1)}, u32[]{:S(2)}, u32[]{:S(2)}) collective-permute-start(bf16[2,19,16,128]{3,2,1,0:T(8,128)(2,1)} %get-tuple-element.141), channel_id=1, source_target_pairs={{0,6},{1,7},{2,4},{3,5},{4,2},{5,3},{6,0},{7,1},{8,14},{9,15},{10,... | collective-permute-start | bytes 466952 | tf_op jit(solution)/shard_map/ppermute | solution.py:1444
  19.7 13.6 %collective-permute-start.3 = (bf16[2,19,16,128]{3,2,1,0:T(8,128)(2,1)}, bf16[2,19,16,128]{3,2,1,0:T(8,128)(2,1)S(1)}, u32[]{:S(2)}, u32[]{:S(2)}) collective-permute-start(bf16[2,19,16,128]{3,2,1,0:T(8,128)(2,1)} %get-tuple-element.141), channel_id=1, source_target_pairs={{0,4},{1,5},{2,6},{3,7},{4,0},{5,1},{6,2},{7,3},{8,12},{9,13},{10,... | collective-permute-start | bytes 466952 | tf_op jit(solution)/shard_map/ppermute | solution.py:1444
  19.8 13.5 %collective-permute-start.2 = (bf16[2,19,16,128]{3,2,1,0:T(8,128)(2,1)}, bf16[2,19,16,128]{3,2,1,0:T(8,128)(2,1)S(1)}, u32[]{:S(2)}, u32[]{:S(2)}) collective-permute-start(bf16[2,19,16,128]{3,2,1,0:T(8,128)(2,1)} %get-tuple-element.141), channel_id=1, source_target_pairs={{0,2},{1,3},{2,0},{3,1},{4,6},{5,7},{6,4},{7,5},{8,10},{9,11},{10,... | collective-permute-start | bytes 466952 | tf_op jit(solution)/shard_map/ppermute | solution.py:1444
  33.4 8.5 %collective-permute-start.5 = (bf16[4,19,16,128]{3,2,1,0:T(8,128)(2,1)S(1)}, bf16[4,19,16,128]{3,2,1,0:T(8,128)(2,1)S(1)}, u32[]{:S(2)}, u32[]{:S(2)}) collective-permute-start(bf16[4,19,16,128]{3,2,1,0:T(8,128)(2,1)S(1)} %get-tuple-element.143), channel_id=1, source_target_pairs={{0,16},{1,17},{2,18},{3,19},{4,20},{5,21},{6,22},{7,23},{8,24},{9,... | collective-permute-start | bytes 933896 | tf_op jit(solution)/shard_map/ppermute | solution.py:1444
  33.5 9.3 %collective-permute-start.6 = (bf16[4,19,16,128]{3,2,1,0:T(8,128)(2,1)S(1)}, bf16[4,19,16,128]{3,2,1,0:T(8,128)(2,1)S(1)}, u32[]{:S(2)}, u32[]{:S(2)}) collective-permute-start(bf16[4,19,16,128]{3,2,1,0:T(8,128)(2,1)S(1)} %get-tuple-element.144), channel_id=1, source_target_pairs={{0,1},{1,0},{2,3},{3,2},{4,5},{5,4},{6,7},{7,6},{8,9},{9,8},{10,11... | collective-permute-start | bytes 933896 | tf_op jit(solution)/shard_map/ppermute | solution.py:1444
  35.5 11.8 %collective-permute-start.8 = (bf16[2,36,16,128]{3,2,1,0:T(8,128)(2,1)S(1)}, bf16[2,36,16,128]{3,2,1,0:T(8,128)(2,1)S(1)}, u32[]{:S(2)}, u32[]{:S(2)}) collective-permute-start(bf16[2,36,16,128]{3,2,1,0:T(8,128)(2,1)S(1)} %copy-done.47), channel_id=1, source_target_pairs={{0,6},{1,7},{2,4},{3,5},{4,2},{5,3},{6,0},{7,1},{8,14},{9,15},{10,... | collective-permute-start | bytes 884744 | tf_op jit(solution)/shard_map/ppermute | solution.py:1444
  38.2 13.9 %collective-permute-start.7 = (bf16[2,36,16,128]{3,2,1,0:T(8,128)(2,1)S(1)}, bf16[2,36,16,128]{3,2,1,0:T(8,128)(2,1)S(1)}, u32[]{:S(2)}, u32[]{:S(2)}) collective-permute-start(bf16[2,36,16,128]{3,2,1,0:T(8,128)(2,1)S(1)} %copy-done.47), channel_id=1, source_target_pairs={{0,2},{1,3},{2,0},{3,1},{4,6},{5,7},{6,4},{7,5},{8,10},{9,11},{10,... | collective-permute-start | bytes 884744 | tf_op jit(solution)/shard_map/ppermute | solution.py:1444
  42.0 25.4 %copy-start.4 = (bf16[8,19,16,128]{3,2,1,0:T(8,128)(2,1)}, bf16[8,19,16,128]{3,2,1,0:T(8,128)(2,1)S(1)}, u32[]{:S(2)}) copy-start(bf16[8,19,16,128]{3,2,1,0:T(8,128)(2,1)S(1)} %pad_maximum_fusion.2.refs_0_.refs_8_) | copy-start | bytes 1867780
  52.1 15.2 %collective-permute-start.13 = (bf16[2,36,16,128]{3,2,1,0:T(8,128)(2,1)S(1)}, bf16[2,36,16,128]{3,2,1,0:T(8,128)(2,1)S(1)}, u32[]{:S(2)}, u32[]{:S(2)}) collective-permute-start(bf16[2,36,16,128]{3,2,1,0:T(8,128)(2,1)S(1)} %copy-done.47), channel_id=1, source_target_pairs={{0,4},{1,5},{2,6},{3,7},{4,0},{5,1},{6,2},{7,3},{8,12},{9,13},{10,... | collective-permute-start | bytes 884744 | tf_op jit(solution)/shard_map/ppermute | solution.py:1444
  52.7 14.8 %collective-permute-start.11 = (bf16[8,19,16,128]{3,2,1,0:T(8,128)(2,1)S(1)}, bf16[8,19,16,128]{3,2,1,0:T(8,128)(2,1)S(1)}, u32[]{:S(2)}, u32[]{:S(2)}) collective-permute-start(bf16[8,19,16,128]{3,2,1,0:T(8,128)(2,1)S(1)} %pad_maximum_fusion.2.refs_0_.refs_8_), channel_id=1, source_target_pairs={{0,8},{1,9},{2,10},{3,11},{4,12},{5,13},{6,14},{7,15},{8,0},{9,1},... | collective-permute-start | bytes 1867784 | tf_op jit(solution)/shard_map/ppermute | solution.py:1444
  52.7 16.4 %collective-permute-start.9 = (bf16[8,19,16,128]{3,2,1,0:T(8,128)(2,1)S(1)}, bf16[8,19,16,128]{3,2,1,0:T(8,128)(2,1)S(1)}, u32[]{:S(2)}, u32[]{:S(2)}) collective-permute-start(bf16[8,19,16,128]{3,2,1,0:T(8,128)(2,1)S(1)} %pad_maximum_fusion.2.refs_0_.refs_8_), channel_id=1, source_target_pairs={{0,1},{1,0},{2,3},{3,2},{4,5},{5,4},{6,7},{7,6},{8,9},{9,8},{10,11... | collective-permute-start | bytes 1867784 | tf_op jit(solution)/shard_map/ppermute | solution.py:1444
  53.0 16.2 %collective-permute-start.12 = (bf16[8,19,16,128]{3,2,1,0:T(8,128)(2,1)S(1)}, bf16[8,19,16,128]{3,2,1,0:T(8,128)(2,1)S(1)}, u32[]{:S(2)}, u32[]{:S(2)}) collective-permute-start(bf16[8,19,16,128]{3,2,1,0:T(8,128)(2,1)S(1)} %pad_maximum_fusion.3.refs_4_.refs_12_), channel_id=1, source_target_pairs={{0,8},{1,9},{2,10},{3,11},{4,12},{5,13},{6,14},{7,15},{8,0},{9,1},... | collective-permute-start | bytes 1867784 | tf_op jit(solution)/shard_map/ppermute | solution.py:1444
  53.2 16.2 %collective-permute-start.10 = (bf16[8,19,16,128]{3,2,1,0:T(8,128)(2,1)S(1)}, bf16[8,19,16,128]{3,2,1,0:T(8,128)(2,1)S(1)}, u32[]{:S(2)}, u32[]{:S(2)}) collective-permute-start(bf16[8,19,16,128]{3,2,1,0:T(8,128)(2,1)S(1)} %pad_maximum_fusion.3.refs_4_.refs_12_), channel_id=1, source_target_pairs={{0,16},{1,17},{2,18},{3,19},{4,20},{5,21},{6,22},{7,23},{8,24},{9,... | collective-permute-start | bytes 1867784 | tf_op jit(solution)/shard_map/ppermute | solution.py:1444
  69.5 2.1 collective-permute-start.14
  69.5 2.9 collective-permute-start.15
  72.4 15.5 %collective-permute-start.16 = (bf16[4,36,16,128]{3,2,1,0:T(8,128)(2,1)S(1)}, bf16[4,36,16,128]{3,2,1,0:T(8,128)(2,1)}, u32[]{:S(2)}, u32[]{:S(2)}) collective-permute-start(bf16[4,36,16,128]{3,2,1,0:T(8,128)(2,1)S(1)} %pad_maximum_fusion.4), channel_id=1, source_target_pairs={{0,16},{1,17},{2,18},{3,19},{4,20},{5,21},{6,22},{7,23},{8,24},{9,... | collective-permute-start | bytes 1769480 | tf_op jit(solution)/shard_map/ppermute | solution.py:1444
  73.3 15.8 %collective-permute-start.17 = (bf16[4,36,16,128]{3,2,1,0:T(8,128)(2,1)S(1)}, bf16[4,36,16,128]{3,2,1,0:T(8,128)(2,1)S(1)}, u32[]{:S(2)}, u32[]{:S(2)}) collective-permute-start(bf16[4,36,16,128]{3,2,1,0:T(8,128)(2,1)S(1)} %pad_maximum_fusion.5), channel_id=1, source_target_pairs={{0,1},{1,0},{2,3},{3,2},{4,5},{5,4},{6,7},{7,6},{8,9},{9,8},{10,11... | collective-permute-start | bytes 1769480 | tf_op jit(solution)/shard_map/ppermute | solution.py:1444
  89.2 73.0 %copy-start.2 = (bf16[8,36,16,128]{3,2,1,0:T(8,128)(2,1)}, bf16[8,36,16,128]{3,2,1,0:T(8,128)(2,1)S(1)}, u32[]{:S(2)}) copy-start(bf16[8,36,16,128]{3,2,1,0:T(8,128)(2,1)S(1)} %pad_maximum_fusion.1.refs_4_) | copy-start | bytes 3538948
  89.2 20.1 %collective-permute-start.20 = (bf16[8,36,16,128]{3,2,1,0:T(8,128)(2,1)S(1)}, bf16[8,36,16,128]{3,2,1,0:T(8,128)(2,1)S(1)}, u32[]{:S(2)}, u32[]{:S(2)}) collective-permute-start(bf16[8,36,16,128]{3,2,1,0:T(8,128)(2,1)S(1)} %pad_maximum_fusion.refs_0_), channel_id=1, source_target_pairs={{0,8},{1,9},{2,10},{3,11},{4,12},{5,13},{6,14},{7,15},{8,0},{9,1},... | collective-permute-start | bytes 3538952 | tf_op jit(solution)/shard_map/ppermute | solution.py:1444
  89.3 28.4 %collective-permute-start.18 = (bf16[8,36,16,128]{3,2,1,0:T(8,128)(2,1)S(1)}, bf16[8,36,16,128]{3,2,1,0:T(8,128)(2,1)S(1)}, u32[]{:S(2)}, u32[]{:S(2)}) collective-permute-start(bf16[8,36,16,128]{3,2,1,0:T(8,128)(2,1)S(1)} %pad_maximum_fusion.refs_0_), channel_id=1, source_target_pairs={{0,1},{1,0},{2,3},{3,2},{4,5},{5,4},{6,7},{7,6},{8,9},{9,8},{10,11... | collective-permute-start | bytes 3538952 | tf_op jit(solution)/shard_map/ppermute | solution.py:1444
  91.1 26.6 %collective-permute-start.21 = (bf16[8,36,16,128]{3,2,1,0:T(8,128)(2,1)S(1)}, bf16[8,36,16,128]{3,2,1,0:T(8,128)(2,1)S(1)}, u32[]{:S(2)}, u32[]{:S(2)}) collective-permute-start(bf16[8,36,16,128]{3,2,1,0:T(8,128)(2,1)S(1)} %pad_maximum_fusion.1.refs_4_), channel_id=1, source_target_pairs={{0,8},{1,9},{2,10},{3,11},{4,12},{5,13},{6,14},{7,15},{8,0},{9,1},... | collective-permute-start | bytes 3538952 | tf_op jit(solution)/shard_map/ppermute | solution.py:1444
  91.2 28.3 %collective-permute-start.19 = (bf16[8,36,16,128]{3,2,1,0:T(8,128)(2,1)S(1)}, bf16[8,36,16,128]{3,2,1,0:T(8,128)(2,1)}, u32[]{:S(2)}, u32[]{:S(2)}) collective-permute-start(bf16[8,36,16,128]{3,2,1,0:T(8,128)(2,1)S(1)} %pad_maximum_fusion.1.refs_4_), channel_id=1, source_target_pairs={{0,16},{1,17},{2,18},{3,19},{4,20},{5,21},{6,22},{7,23},{8,24},{9,... | collective-permute-start | bytes 3538952 | tf_op jit(solution)/shard_map/ppermute | solution.py:1444
  91.7 32.6 %copy-start.30 = (f32[88,128]{1,0:T(8,128)S(1)}, f32[88,128]{1,0:T(8,128)}, u32[]{:S(2)}) copy-start(f32[88,128]{1,0:T(8,128)} %get-tuple-element.174.small) | copy-start | bytes 135172
  109.3 52.8 %copy-start.8 = (bf16[8,36,16,128]{3,2,1,0:T(8,128)(2,1)}, bf16[8,36,16,128]{3,2,1,0:T(8,128)(2,1)S(1)}, u32[]{:S(2)}) copy-start(bf16[8,36,16,128]{3,2,1,0:T(8,128)(2,1)S(1)} %collective-permute-done.20.refs_2_) | copy-start | bytes 3538948
  117.7 44.5 %copy-start.10 = (bf16[8,36,16,128]{3,2,1,0:T(8,128)(2,1)}, bf16[8,36,16,128]{3,2,1,0:T(8,128)(2,1)S(1)}, u32[]{:S(2)}) copy-start(bf16[8,36,16,128]{3,2,1,0:T(8,128)(2,1)S(1)} %collective-permute-done.18.refs_1_) | copy-start | bytes 3538948
  117.7 44.5 %copy-start.12 = (bf16[8,36,16,128]{3,2,1,0:T(8,128)(2,1)}, bf16[8,36,16,128]{3,2,1,0:T(8,128)(2,1)S(1)}, u32[]{:S(2)}) copy-start(bf16[8,36,16,128]{3,2,1,0:T(8,128)(2,1)S(1)} %collective-permute-done.21.refs_6_) | copy-start | bytes 3538948
  119.6 4.5 %collective-permute-start.22 = (bf16[8,36,16,128]{3,2,1,0:T(8,128)(2,1)S(1)}, bf16[8,36,16,128]{3,2,1,0:T(8,128)(2,1)S(1)}, u32[]{:S(2)}, u32[]{:S(2)}) collective-permute-start(bf16[8,36,16,128]{3,2,1,0:T(8,128)(2,1)S(1)} %collective-permute-done.18.refs_1_), channel_id=1, source_target_pairs={{0,8},{1,9},{2,10},{3,11},{4,12},{5,13},{6,14},{7,15},{8,0},{9,1},... | collective-permute-start | bytes 3538952 | tf_op jit(solution)/shard_map/ppermute | solution.py:1444
  119.6 4.7 %collective-permute-start.23 = (bf16[8,36,16,128]{3,2,1,0:T(8,128)(2,1)}, bf16[8,36,16,128]{3,2,1,0:T(8,128)(2,1)S(1)}, u32[]{:S(2)}, u32[]{:S(2)}) collective-permute-start(bf16[8,36,16,128]{3,2,1,0:T(8,128)(2,1)} %collective-permute-done.19.refs_5_), channel_id=1, source_target_pairs={{0,8},{1,9},{2,10},{3,11},{4,12},{5,13},{6,14},{7,15},{8,0},{9,1},... | collective-permute-start | bytes 3538952 | tf_op jit(solution)/shard_map/ppermute | solution.py:1444
  124.1 37.5 %copy-start.13 = (bf16[8,36,16,128]{3,2,1,0:T(8,128)(2,1)}, bf16[8,36,16,128]{3,2,1,0:T(8,128)(2,1)S(1)}, u32[]{:S(2)}) copy-start(bf16[8,36,16,128]{3,2,1,0:T(8,128)(2,1)S(1)} %collective-permute-done.22.refs_3_) | copy-start | bytes 3538948
  124.3 37.2 %copy-start.15 = (bf16[8,36,16,128]{3,2,1,0:T(8,128)(2,1)}, bf16[8,36,16,128]{3,2,1,0:T(8,128)(2,1)S(1)}, u32[]{:S(2)}) copy-start(bf16[8,36,16,128]{3,2,1,0:T(8,128)(2,1)S(1)} %collective-permute-done.23.refs_7_) | copy-start | bytes 3538948
  126.3 35.8 %copy-start = (bf16[1024,768]{1,0:T(8,128)(2,1)S(1)}, bf16[1024,768]{1,0:T(8,128)(2,1)}, u32[]{:S(2)}) copy-start(bf16[1024,768]{1,0:T(8,128)(2,1)} %cot_in.3) | copy-start | bytes 4718596
  126.3 35.8 %copy-start.1 = (f32[1024,768]{1,0:T(8,128)S(1)}, f32[1024,768]{1,0:T(8,128)}, u32[]{:S(2)}) copy-start(f32[1024,768]{1,0:T(8,128)} %get-tuple-element.185.x1_in) | copy-start | bytes 9437188
  161.6 16.9 %collective-permute-start.24 = (bf16[16,36,16,128]{3,2,1,0:T(8,128)(2,1)}, bf16[16,36,16,128]{3,2,1,0:T(8,128)(2,1)S(1)}, u32[]{:S(2)}, u32[]{:S(2)}) collective-permute-start(bf16[16,36,16,128]{3,2,1,0:T(8,128)(2,1)} %get-tuple-element.189), channel_id=1, source_target_pairs={{0,8},{1,9},{2,10},{3,11},{4,12},{5,13},{6,14},{7,15},{8,0},{9,1},... | collective-permute-start | bytes 7077896 | tf_op jit(solution)/shard_map/ppermute | solution.py:1444
  161.8 16.7 %collective-permute-start.25 = (bf16[16,36,16,128]{3,2,1,0:T(8,128)(2,1)}, bf16[16,36,16,128]{3,2,1,0:T(8,128)(2,1)S(1)}, u32[]{:S(2)}, u32[]{:S(2)}) collective-permute-start(bf16[16,36,16,128]{3,2,1,0:T(8,128)(2,1)} %get-tuple-element.190), channel_id=1, source_target_pairs={{0,8},{1,9},{2,10},{3,11},{4,12},{5,13},{6,14},{7,15},{8,0},{9,1},... | collective-permute-start | bytes 7077896 | tf_op jit(solution)/shard_map/ppermute | solution.py:1444
  180.7 34.8 %collective-permute-start.26 = (bf16[8,36,16,128]{3,2,1,0:T(8,128)(2,1)}, bf16[8,36,16,128]{3,2,1,0:T(8,128)(2,1)}, u32[]{:S(2)}, u32[]{:S(2)}) collective-permute-start(bf16[8,36,16,128]{3,2,1,0:T(8,128)(2,1)} %add_convert_fusion.1), channel_id=1, source_target_pairs={{0,1},{1,0},{2,3},{3,2},{4,5},{5,4},{6,7},{7,6},{8,9},{9,8},{10,11... | collective-permute-start | bytes 3538952 | tf_op jit(solution)/shard_map/ppermute | solution.py:1444
  181.0 34.5 %collective-permute-start.27 = (bf16[8,36,16,128]{3,2,1,0:T(8,128)(2,1)S(1)}, bf16[8,36,16,128]{3,2,1,0:T(8,128)(2,1)}, u32[]{:S(2)}, u32[]{:S(2)}) collective-permute-start(bf16[8,36,16,128]{3,2,1,0:T(8,128)(2,1)S(1)} %add_convert_fusion), channel_id=1, source_target_pairs={{0,16},{1,17},{2,18},{3,19},{4,20},{5,21},{6,22},{7,23},{8,24},{9,... | collective-permute-start | bytes 3538952 | tf_op jit(solution)/shard_map/ppermute | solution.py:1444
  218.6 15.0 %collective-permute-start.28 = (bf16[4,36,16,128]{3,2,1,0:T(8,128)(2,1)S(1)}, bf16[4,36,16,128]{3,2,1,0:T(8,128)(2,1)S(1)}, u32[]{:S(2)}, u32[]{:S(2)}) collective-permute-start(bf16[4,36,16,128]{3,2,1,0:T(8,128)(2,1)S(1)} %add_convert_fusion.3), channel_id=1, source_target_pairs={{0,16},{1,17},{2,18},{3,19},{4,20},{5,21},{6,22},{7,23},{8,24},{9,... | collective-permute-start | bytes 1769480 | tf_op jit(solution)/shard_map/ppermute | solution.py:1444
  218.7 15.0 %collective-permute-start.29 = (bf16[4,36,16,128]{3,2,1,0:T(8,128)(2,1)S(1)}, bf16[4,36,16,128]{3,2,1,0:T(8,128)(2,1)S(1)}, u32[]{:S(2)}, u32[]{:S(2)}) collective-permute-start(bf16[4,36,16,128]{3,2,1,0:T(8,128)(2,1)S(1)} %add_convert_fusion.2), channel_id=1, source_target_pairs={{0,1},{1,0},{2,3},{3,2},{4,5},{5,4},{6,7},{7,6},{8,9},{9,8},{10,11... | collective-permute-start | bytes 1769480 | tf_op jit(solution)/shard_map/ppermute | solution.py:1444
  220.0 13.7 %collective-permute-start.30 = (bf16[16,9,16,128]{3,2,1,0:T(8,128)(2,1)S(1)}, bf16[16,9,16,128]{3,2,1,0:T(8,128)(2,1)S(1)}, u32[]{:S(2)}, u32[]{:S(2)}) collective-permute-start(bf16[16,9,16,128]{3,2,1,0:T(8,128)(2,1)S(1)} %get-tuple-element.220), channel_id=1, source_target_pairs={{0,8},{1,9},{2,10},{3,11},{4,12},{5,13},{6,14},{7,15},{8,0},{9,1},... | collective-permute-start | bytes 1769480 | tf_op jit(solution)/shard_map/ppermute | solution.py:1444
  220.0 13.7 %collective-permute-start.31 = (bf16[16,9,16,128]{3,2,1,0:T(8,128)(2,1)S(1)}, bf16[16,9,16,128]{3,2,1,0:T(8,128)(2,1)S(1)}, u32[]{:S(2)}, u32[]{:S(2)}) collective-permute-start(bf16[16,9,16,128]{3,2,1,0:T(8,128)(2,1)S(1)} %get-tuple-element.221), channel_id=1, source_target_pairs={{0,8},{1,9},{2,10},{3,11},{4,12},{5,13},{6,14},{7,15},{8,0},{9,1},... | collective-permute-start | bytes 1769480 | tf_op jit(solution)/shard_map/ppermute | solution.py:1444
  236.9 17.7 %collective-permute-start.32 = (bf16[8,9,16,128]{3,2,1,0:T(8,128)(2,1)S(1)}, bf16[8,9,16,128]{3,2,1,0:T(8,128)(2,1)S(1)}, u32[]{:S(2)}, u32[]{:S(2)}) collective-permute-start(bf16[8,9,16,128]{3,2,1,0:T(8,128)(2,1)S(1)} %add_convert_fusion.7), channel_id=1, source_target_pairs={{0,1},{1,0},{2,3},{3,2},{4,5},{5,4},{6,7},{7,6},{8,9},{9,8},{10,11... | collective-permute-start | bytes 884744 | tf_op jit(solution)/shard_map/ppermute | solution.py:1444
  238.3 16.4 %collective-permute-start.33 = (bf16[8,9,16,128]{3,2,1,0:T(8,128)(2,1)S(1)}, bf16[8,9,16,128]{3,2,1,0:T(8,128)(2,1)S(1)}, u32[]{:S(2)}, u32[]{:S(2)}) collective-permute-start(bf16[8,9,16,128]{3,2,1,0:T(8,128)(2,1)S(1)} %add_convert_fusion.6), channel_id=1, source_target_pairs={{0,16},{1,17},{2,18},{3,19},{4,20},{5,21},{6,22},{7,23},{8,24},{9,... | collective-permute-start | bytes 884744 | tf_op jit(solution)/shard_map/ppermute | solution.py:1444
  238.9 15.8 %collective-permute-start.34 = (bf16[2,36,16,128]{3,2,1,0:T(8,128)(2,1)S(1)}, bf16[2,36,16,128]{3,2,1,0:T(8,128)(2,1)S(1)}, u32[]{:S(2)}, u32[]{:S(2)}) collective-permute-start(bf16[2,36,16,128]{3,2,1,0:T(8,128)(2,1)S(1)} %pad_maximum_fusion.8), channel_id=1, source_target_pairs={{0,2},{1,3},{2,0},{3,1},{4,6},{5,7},{6,4},{7,5},{8,10},{9,11},{10,... | collective-permute-start | bytes 884744 | tf_op jit(solution)/shard_map/ppermute | solution.py:1444
  240.2 14.5 %collective-permute-start.35 = (bf16[2,36,16,128]{3,2,1,0:T(8,128)(2,1)S(1)}, bf16[2,36,16,128]{3,2,1,0:T(8,128)(2,1)S(1)}, u32[]{:S(2)}, u32[]{:S(2)}) collective-permute-start(bf16[2,36,16,128]{3,2,1,0:T(8,128)(2,1)S(1)} %pad_maximum_fusion.9), channel_id=1, source_target_pairs={{0,4},{1,5},{2,6},{3,7},{4,0},{5,1},{6,2},{7,3},{8,12},{9,13},{10,... | collective-permute-start | bytes 884744 | tf_op jit(solution)/shard_map/ppermute | solution.py:1444
  254.9 6.1 %collective-permute-start.36 = (bf16[4,9,16,128]{3,2,1,0:T(8,128)(2,1)S(1)}, bf16[4,9,16,128]{3,2,1,0:T(8,128)(2,1)S(1)}, u32[]{:S(2)}, u32[]{:S(2)}) collective-permute-start(bf16[4,9,16,128]{3,2,1,0:T(8,128)(2,1)S(1)} %add_convert_fusion.11), channel_id=1, source_target_pairs={{0,16},{1,17},{2,18},{3,19},{4,20},{5,21},{6,22},{7,23},{8,24},{9,... | collective-permute-start | bytes 442376 | tf_op jit(solution)/shard_map/ppermute | solution.py:1444
  255.8 8.5 %collective-permute-start.40 = (bf16[36,16,128]{2,1,0:T(8,128)(2,1)S(1)}, bf16[36,16,128]{2,1,0:T(8,128)(2,1)S(1)}, u32[]{:S(2)}, u32[]{:S(2)}) collective-permute-start(bf16[36,16,128]{2,1,0:T(8,128)(2,1)S(1)} %slice_bitcast_fusion.1), channel_id=1, source_target_pairs={{0,6},{1,7},{2,4},{3,5},{4,2},{5,3},{6,0},{7,1},{8,14},{9,15},{10,... | collective-permute-start | bytes 442376 | tf_op jit(solution)/shard_map/ppermute | solution.py:1444
  258.9 5.1 %collective-permute-start.37 = (bf16[4,9,16,128]{3,2,1,0:T(8,128)(2,1)S(1)}, bf16[4,9,16,128]{3,2,1,0:T(8,128)(2,1)S(1)}, u32[]{:S(2)}, u32[]{:S(2)}) collective-permute-start(bf16[4,9,16,128]{3,2,1,0:T(8,128)(2,1)S(1)} %add_convert_fusion.10), channel_id=1, source_target_pairs={{0,1},{1,0},{2,3},{3,2},{4,5},{5,4},{6,7},{7,6},{8,9},{9,8},{10,11... | collective-permute-start | bytes 442376 | tf_op jit(solution)/shard_map/ppermute | solution.py:1444
  260.4 3.8 %collective-permute-start.38 = (bf16[16,10,16,128]{3,2,1,0:T(8,128)(2,1)S(1)}, bf16[16,10,16,128]{3,2,1,0:T(8,128)(2,1)S(1)}, u32[]{:S(2)}, u32[]{:S(2)}) collective-permute-start(bf16[16,10,16,128]{3,2,1,0:T(8,128)(2,1)S(1)} %get-tuple-element.252), channel_id=1, source_target_pairs={{0,8},{1,9},{2,10},{3,11},{4,12},{5,13},{6,14},{7,15},{8,0},{9,1},... | collective-permute-start | bytes 1966088 | tf_op jit(solution)/shard_map/ppermute | solution.py:1444
  260.4 3.9 %collective-permute-start.39 = (bf16[16,10,16,128]{3,2,1,0:T(8,128)(2,1)S(1)}, bf16[16,10,16,128]{3,2,1,0:T(8,128)(2,1)S(1)}, u32[]{:S(2)}, u32[]{:S(2)}) collective-permute-start(bf16[16,10,16,128]{3,2,1,0:T(8,128)(2,1)S(1)} %get-tuple-element.254), channel_id=1, source_target_pairs={{0,8},{1,9},{2,10},{3,11},{4,12},{5,13},{6,14},{7,15},{8,0},{9,1},... | collective-permute-start | bytes 1966088 | tf_op jit(solution)/shard_map/ppermute | solution.py:1444
  264.4 9.0 %collective-permute-start.41 = (bf16[8,10,16,128]{3,2,1,0:T(8,128)(2,1)S(1)}, bf16[8,10,16,128]{3,2,1,0:T(8,128)(2,1)S(1)}, u32[]{:S(2)}, u32[]{:S(2)}) collective-permute-start(bf16[8,10,16,128]{3,2,1,0:T(8,128)(2,1)S(1)} %add_convert_fusion.5), channel_id=1, source_target_pairs={{0,1},{1,0},{2,3},{3,2},{4,5},{5,4},{6,7},{7,6},{8,9},{9,8},{10,11... | collective-permute-start | bytes 983048 | tf_op jit(solution)/shard_map/ppermute | solution.py:1444
  266.0 7.6 %collective-permute-start.42 = (bf16[8,10,16,128]{3,2,1,0:T(8,128)(2,1)S(1)}, bf16[8,10,16,128]{3,2,1,0:T(8,128)(2,1)S(1)}, u32[]{:S(2)}, u32[]{:S(2)}) collective-permute-start(bf16[8,10,16,128]{3,2,1,0:T(8,128)(2,1)S(1)} %add_convert_fusion.4), channel_id=1, source_target_pairs={{0,16},{1,17},{2,18},{3,19},{4,20},{5,21},{6,22},{7,23},{8,24},{9,... | collective-permute-start | bytes 983048 | tf_op jit(solution)/shard_map/ppermute | solution.py:1444
  267.5 6.2 %collective-permute-start.43 = (bf16[2,9,16,128]{3,2,1,0:T(8,128)(2,1)S(1)}, bf16[2,9,16,128]{3,2,1,0:T(8,128)(2,1)S(1)}, u32[]{:S(2)}, u32[]{:S(2)}) collective-permute-start(bf16[2,9,16,128]{3,2,1,0:T(8,128)(2,1)S(1)} %pad_maximum_fusion.14), channel_id=1, source_target_pairs={{0,2},{1,3},{2,0},{3,1},{4,6},{5,7},{6,4},{7,5},{8,10},{9,11},{10,... | collective-permute-start | bytes 221192 | tf_op jit(solution)/shard_map/ppermute | solution.py:1444
  267.6 6.1 %collective-permute-start.44 = (bf16[2,9,16,128]{3,2,1,0:T(8,128)(2,1)S(1)}, bf16[2,9,16,128]{3,2,1,0:T(8,128)(2,1)S(1)}, u32[]{:S(2)}, u32[]{:S(2)}) collective-permute-start(bf16[2,9,16,128]{3,2,1,0:T(8,128)(2,1)S(1)} %pad_maximum_fusion.15), channel_id=1, source_target_pairs={{0,4},{1,5},{2,6},{3,7},{4,0},{5,1},{6,2},{7,3},{8,12},{9,13},{10,... | collective-permute-start | bytes 221192 | tf_op jit(solution)/shard_map/ppermute | solution.py:1444
  269.4 6.3 %collective-permute-start.45 = (bf16[2,9,16,128]{3,2,1,0:T(8,128)(2,1)S(1)}, bf16[2,9,16,128]{3,2,1,0:T(8,128)(2,1)S(1)}, u32[]{:S(2)}, u32[]{:S(2)}) collective-permute-start(bf16[2,9,16,128]{3,2,1,0:T(8,128)(2,1)S(1)} %pad_maximum_fusion.16), channel_id=1, source_target_pairs={{0,6},{1,7},{2,4},{3,5},{4,2},{5,3},{6,0},{7,1},{8,14},{9,15},{10,... | collective-permute-start | bytes 221192 | tf_op jit(solution)/shard_map/ppermute | solution.py:1444
  275.7 7.2 %collective-permute-start.46 = (bf16[36,16,128]{2,1,0:T(8,128)(2,1)S(1)}, bf16[36,16,128]{2,1,0:T(8,128)(2,1)S(1)}, u32[]{:S(2)}, u32[]{:S(2)}) collective-permute-start(bf16[36,16,128]{2,1,0:T(8,128)(2,1)S(1)} %slice_bitcast_fusion), channel_id=1, source_target_pairs={{0,6},{1,7},{2,4},{3,5},{4,2},{5,3},{6,0},{7,1},{8,14},{9,15},{10,... | collective-permute-start | bytes 442376 | tf_op jit(solution)/shard_map/ppermute | solution.py:1444
  278.2 5.6 %collective-permute-start.47 = (bf16[4,10,16,128]{3,2,1,0:T(8,128)(2,1)S(1)}, bf16[4,10,16,128]{3,2,1,0:T(8,128)(2,1)S(1)}, u32[]{:S(2)}, u32[]{:S(2)}) collective-permute-start(bf16[4,10,16,128]{3,2,1,0:T(8,128)(2,1)S(1)} %add_convert_fusion.9), channel_id=1, source_target_pairs={{0,16},{1,17},{2,18},{3,19},{4,20},{5,21},{6,22},{7,23},{8,24},{9,... | collective-permute-start | bytes 491528 | tf_op jit(solution)/shard_map/ppermute | solution.py:1444
  278.7 5.3 %collective-permute-start.48 = (bf16[4,10,16,128]{3,2,1,0:T(8,128)(2,1)S(1)}, bf16[4,10,16,128]{3,2,1,0:T(8,128)(2,1)S(1)}, u32[]{:S(2)}, u32[]{:S(2)}) collective-permute-start(bf16[4,10,16,128]{3,2,1,0:T(8,128)(2,1)S(1)} %add_convert_fusion.8), channel_id=1, source_target_pairs={{0,1},{1,0},{2,3},{3,2},{4,5},{5,4},{6,7},{7,6},{8,9},{9,8},{10,11... | collective-permute-start | bytes 491528 | tf_op jit(solution)/shard_map/ppermute | solution.py:1444
  284.2 4.5 %collective-permute-start.49 = (bf16[2,10,16,128]{3,2,1,0:T(8,128)(2,1)S(1)}, bf16[2,10,16,128]{3,2,1,0:T(8,128)(2,1)S(1)}, u32[]{:S(2)}, u32[]{:S(2)}) collective-permute-start(bf16[2,10,16,128]{3,2,1,0:T(8,128)(2,1)S(1)} %pad_maximum_fusion.11), channel_id=1, source_target_pairs={{0,2},{1,3},{2,0},{3,1},{4,6},{5,7},{6,4},{7,5},{8,10},{9,11},{10,... | collective-permute-start | bytes 245768 | tf_op jit(solution)/shard_map/ppermute | solution.py:1444
  284.3 5.9 %collective-permute-start.50 = (bf16[2,10,16,128]{3,2,1,0:T(8,128)(2,1)S(1)}, bf16[2,10,16,128]{3,2,1,0:T(8,128)(2,1)S(1)}, u32[]{:S(2)}, u32[]{:S(2)}) collective-permute-start(bf16[2,10,16,128]{3,2,1,0:T(8,128)(2,1)S(1)} %pad_maximum_fusion.12), channel_id=1, source_target_pairs={{0,4},{1,5},{2,6},{3,7},{4,0},{5,1},{6,2},{7,3},{8,12},{9,13},{10,... | collective-permute-start | bytes 245768 | tf_op jit(solution)/shard_map/ppermute | solution.py:1444
  287.8 6.2 %collective-permute-start.51 = (bf16[2,10,16,128]{3,2,1,0:T(8,128)(2,1)S(1)}, bf16[2,10,16,128]{3,2,1,0:T(8,128)(2,1)S(1)}, u32[]{:S(2)}, u32[]{:S(2)}) collective-permute-start(bf16[2,10,16,128]{3,2,1,0:T(8,128)(2,1)S(1)} %pad_maximum_fusion.13), channel_id=1, source_target_pairs={{0,6},{1,7},{2,4},{3,5},{4,2},{5,3},{6,0},{7,1},{8,14},{9,15},{10,... | collective-permute-start | bytes 245768 | tf_op jit(solution)/shard_map/ppermute | solution.py:1444
  297.1 11.2 %collective-permute-start.53 = (f32[128,128]{1,0:T(8,128)}, f32[128,128]{1,0:T(8,128)S(1)}, u32[]{:S(2)}, u32[]{:S(2)}) collective-permute-start(f32[128,128]{1,0:T(8,128)} %get-tuple-element.278), channel_id=1, source_target_pairs={{1,0},{2,1},{3,2},{4,3},{5,4},{6,5},{7,6},{8,7},{9,8},{10,9},{11,1... | collective-permute-start | bytes 196616 | tf_op jit(solution)/shard_map/ppermute | solution.py:1449
  299.0 9.3 %collective-permute-start.52 = (f32[72,128]{1,0:T(8,128)}, f32[72,128]{1,0:T(8,128)S(1)}, u32[]{:S(2)}, u32[]{:S(2)}) collective-permute-start(f32[72,128]{1,0:T(8,128)} %get-tuple-element.277), channel_id=1, source_target_pairs={{0,1},{1,2},{2,3},{3,4},{4,5},{5,6},{6,7},{7,8},{8,9},{9,10},{10,1... | collective-permute-start | bytes 110600 | tf_op jit(solution)/shard_map/ppermute | solution.py:1449
  (46 other events, 309.6 us)

commit v2 on v1

--- a/solution.py
+++ b/solution.py
@@ -1444,9 +1444,19 @@
     return lax.ppermute(values, AXES, [(d, d ^ bit) for d in range(BLOCKS)])
 
 
-def shifted(values, by):
-    pairs = [(d, d + by) for d in range(BLOCKS) if 0 <= d + by < BLOCKS]
-    return lax.ppermute(values, AXES, pairs)
+def overhangs(att_rows, mlp_rows):
+    before, after = [], []
+    for d in range(BLOCKS):
+        att = 12 + d * (576 - att_rows) + (0 if d < QKV_BLOCKS else 12)
+        mlp = 12 + d * (1152 - mlp_rows) + (0 if d < W1_BLOCKS else 24)
+        ahead = 12 if d == 0 else 0
+        att_end = att + 576 + (12 if d in (QKV_BLOCKS - 1, BLOCKS - 1) else 0)
+        mlp_end = mlp + 1152 + (24 if d == W1_BLOCKS - 1 else 12 if d == BLOCKS - 1 else 0)
+        if min(att, mlp) < ahead:
+            before.append(d)
+        if att_end > att_rows or mlp_end > mlp_rows:
+            after.append(d)
+    return before, after
 
 
 def together(*values):
@@ -1654,7 +1664,9 @@
     me = lax.axis_index(AXES).astype(jnp.int32).reshape(1)
     tails = jnp.concatenate([params[att_rows - ATT_BEFORE : att_rows], params[-MLP_BEFORE:]])
     heads = jnp.concatenate([params[:ATT_AFTER], params[att_rows : att_rows + MLP_AFTER]])
-    tails, heads = shifted(tails.astype(BF16), 1), shifted(heads.astype(BF16), -1)
+    before, beyond = overhangs(att_rows, mlp_rows)
+    heads = lax.ppermute(heads.astype(BF16), AXES, [(d + 1, d) for d in beyond])
+    tails = lax.ppermute(tails.astype(BF16), AXES, [(d - 1, d) for d in before])
     att_own, mlp_own = pack(me, params, tails, heads, att_rows)
 
     got = [exchange(att_own, k * Z0) for k in range(1, 4)]
@@ -1739,7 +1751,9 @@
     got = [exchange(part, (k + 1) * Z0) for k, part in enumerate(sends)]
     group1 = sum_terms([z_part(c, d, 0)] + got)
     mine, to_before, to_after = spread(me, group0, group1, m_own, att_rows, mlp_rows, scale)
-    grad_params = close(mine, shifted(to_after, 1), shifted(to_before, -1), att_rows)
+    below = lax.ppermute(to_after, AXES, [(d, d + 1) for d in beyond])
+    above = lax.ppermute(to_before, AXES, [(d, d - 1) for d in before])
+    grad_params = close(mine, below, above, att_rows)
     return output, grad_input, grad_params
 
 

time: 316 us -> 311 us (0.984)
  transfers between devices with their start and end apart: 54 -> 54, of which waited for: 29 -> 28; matrix products, arithmetic and copies ran while one was open for 3% -> 3% of each run, Pallas kernels for 30% -> 30%
where the time goes in v2:
time: 311 us; the launch traced here: 308 us
  Pallas kernels  133 us (43%)
  waiting for transfers between devices  80.7 us (26%)
  starting transfers between devices  60.3 us (19%)
  other arithmetic  15.8 us (5%)
  local copies, waits for them, and re-layouts  15.6 us (5%)
    ppermute x50, waiting for transfers between devices, exchange(): return lax.ppermute(values, AXES, [(d, d ^ bit) for d in range(BLOCKS)])  73.4 us
    ppermute x50, starting transfers between devices, exchange(): return lax.ppermute(values, AXES, [(d, d ^ bit) for d in range(BLOCKS)])  46.7 us
    pallas_call x1, Pallas kernels, feed_forward(): pl.pallas_call(mlp_kernel, out_shape=(shape((rows, FF), BF16), shape((row...  35.2 us
    pallas_call x2, Pallas kernels, attend_back(): pl.pallas_call(partial(attend_back_kernel, group), out_shape=shape((rows,...  21.4 us
    pallas_call x1, Pallas kernels, attend(): pl.pallas_call(attend_kernel, out_shape=(shape((rows, width), BF16), shap...  16.4 us
    pallas_call x1, Pallas kernels, split(): pl.pallas_call(split_kernel, out_shape=(shape((rows, width), F32), shape(...  16.2 us
    pallas_call x1, Pallas kernels, qkv_back(): pl.pallas_call(qkv_back_kernel, out_shape=(shape((rows, width), F32), hal...  12.9 us
    unnamed x112, local copies, waits for them, and re-layouts  12.5 us
  transfers between devices with their start and end apart: 54, of which 28 were waited for; matrix products, arithmetic and copies ran while one was open for 3% of the time, Pallas kernels for 30%

profile of v2, /device:TPU:2, one launch (start us, length us, event | category | flops | bytes accessed | tf_op | source)
XLA Modules:
  0.0 307.9 jit_solution(1221557484521558064)
XLA Ops:
  1.9 5.9 %collective-permute-start.1 = (bf16[72,128]{1,0:T(8,128)(2,1)S(1)}, bf16[72,128]{1,0:T(8,128)(2,1)S(1)}, u32[]{:S(2)}, u32[]{:S(2)}) collective-permute-start(bf16[72,128]{1,0:T(8,128)(2,1)S(1)} %pad_maximum_fusion.19), channel_id=1, source_target_pairs={{1,0},{2,1},{3,2},{4,3},{5,4},{16,15},{17,16}} | collective-permute-start | bytes 55304 | tf_op jit(solution)/shard_map/ppermute | solution.py:1668
  7.8 1.9 collective-permute-start
  12.0 1.3 convert_bitcast_fusion
  14.5 2.1 collective-permute-done.tails
  17.3 2.1 pack.1
  19.4 4.3 %collective-permute-start.2 = (bf16[2,19,16,128]{3,2,1,0:T(8,128)(2,1)}, bf16[2,19,16,128]{3,2,1,0:T(8,128)(2,1)S(1)}, u32[]{:S(2)}, u32[]{:S(2)}) collective-permute-start(bf16[2,19,16,128]{3,2,1,0:T(8,128)(2,1)} %get-tuple-element.141), channel_id=1, source_target_pairs={{0,2},{1,3},{2,0},{3,1},{4,6},{5,7},{6,4},{7,5},{8,10},{9,11},{10,... | collective-permute-start | bytes 466952 | tf_op jit(solution)/shard_map/ppermute | solution.py:1444
  24.7 2.1 collective-permute-done.4
  26.8 3.5 %collective-permute-done.3 = bf16[2,19,16,128]{3,2,1,0:T(8,128)(2,1)S(1)} collective-permute-done((bf16[2,19,16,128]{3,2,1,0:T(8,128)(2,1)}, bf16[2,19,16,128]{3,2,1,0:T(8,128)(2,1)S(1)}, u32[]{:S(2)}, u32[]{:S(2)}) %collective-permute-start.3) | collective-permute-done | bytes 155680 | tf_op jit(solution)/shard_map/ppermute | solution.py:1444
  31.1 1.5 collective-permute-start.6
  32.6 2.5 collective-permute-start.8
  35.1 3.5 %collective-permute-done.5 = bf16[4,19,16,128]{3,2,1,0:T(8,128)(2,1)S(1)} collective-permute-done((bf16[4,19,16,128]{3,2,1,0:T(8,128)(2,1)S(1)}, bf16[4,19,16,128]{3,2,1,0:T(8,128)(2,1)S(1)}, u32[]{:S(2)}, u32[]{:S(2)}) %collective-permute-start.5) | collective-permute-done | bytes 311328 | tf_op jit(solution)/shard_map/ppermute | solution.py:1444
  38.6 1.3 collective-permute-done.6
  40.0 4.4 %collective-permute-done.8 = bf16[2,36,16,128]{3,2,1,0:T(8,128)(2,1)S(1)} collective-permute-done((bf16[2,36,16,128]{3,2,1,0:T(8,128)(2,1)S(1)}, bf16[2,36,16,128]{3,2,1,0:T(8,128)(2,1)S(1)}, u32[]{:S(2)}, u32[]{:S(2)}) %collective-permute-start.8) | collective-permute-done | bytes 294944 | tf_op jit(solution)/shard_map/ppermute | solution.py:1444
  44.4 4.9 %collective-permute-done.7 = bf16[2,36,16,128]{3,2,1,0:T(8,128)(2,1)S(1)} collective-permute-done((bf16[2,36,16,128]{3,2,1,0:T(8,128)(2,1)S(1)}, bf16[2,36,16,128]{3,2,1,0:T(8,128)(2,1)S(1)}, u32[]{:S(2)}, u32[]{:S(2)}) %collective-permute-start.7) | collective-permute-done | bytes 294944 | tf_op jit(solution)/shard_map/ppermute | solution.py:1444
  51.0 13.5 %collective-permute-done.13 = bf16[2,36,16,128]{3,2,1,0:T(8,128)(2,1)S(1)} collective-permute-done((bf16[2,36,16,128]{3,2,1,0:T(8,128)(2,1)S(1)}, bf16[2,36,16,128]{3,2,1,0:T(8,128)(2,1)S(1)}, u32[]{:S(2)}, u32[]{:S(2)}) %collective-permute-start.13) | collective-permute-done | bytes 294944 | tf_op jit(solution)/shard_map/ppermute | solution.py:1444
  64.7 1.6 collective-permute-done.9.refs_1_.refs_9_
  67.1 1.5 collective-permute-done.14.refs_3_.refs_11_
  70.1 1.8 collective-permute-start.17
  71.9 10.2 %qkv_forward.1 = (bf16[1024,768]{1,0:T(8,128)(2,1)}, bf16[1024,2304]{1,0:T(8,128)(2,1)}, f32[88,128]{1,0:T(8,128)}) custom-call(s32[1]{0:T(128)} %bitcast.me_ref, bf16[1024,768]{1,0:T(8,128)(2,1)} %tokens_in.1, bf16[8,19,16,128]{3,2,1,0:T(8,128)(2,1)} %copy-done.4, bf16[8,19,16,128]{3,2,1,0:T(8,128)(2,1)} %copy-done.19, bf16[8,19,16,128]{3,2,1,0:T(8,128)(2,1)} %copy-done.17, ...), custom_call_target="tpu_custom_call" | custom-call | flops 3623878656 | bytes 9437184 | tf_op jit(solution)/shard_map/qkv_forward/pallas_call | solution.py:430
  82.1 3.0 collective-permute-done.16
  86.4 1.8 collective-permute-start.18
  88.9 16.4 %attend_forward.1 = (bf16[1024,768]{1,0:T(8,128)(2,1)}, f32[1024,768]{1,0:T(8,128)}, bf16[1024,768]{1,0:T(8,128)(2,1)}, bf16[1024,768]{1,0:T(8,128)(2,1)}, bf16[...) custom-call(s32[1]{0:T(128)} %bitcast.me_ref, s32[3,8]{1,0:T(4,128)} %pad_add_fusion.windows, ...), custom_call_target="tpu_custom_call" | custom-call | flops 1610612736 | bytes 15728640 | tf_op jit(solution)/shard_map/attend_forward/pallas_call | solution.py:635
  105.4 9.4 %collective-permute-done.18.refs_1_ = bf16[8,36,16,128]{3,2,1,0:T(8,128)(2,1)S(1)} collective-permute-done((bf16[8,36,16,128]{3,2,1,0:T(8,128)(2,1)S(1)}, bf16[8,36,16,128]{3,2,1,0:T(8,128)(2,1)S(1)}, u32[]{:S(2)}, u32[]{:S(2)}) %collective-permute-start.18) | collective-permute-done | bytes 1179680 | tf_op jit(solution)/shard_map/ppermute | solution.py:1444
  114.8 1.9 collective-permute-done.19.refs_5_
  117.2 4.0 %collective-permute-done.22.refs_3_ = bf16[8,36,16,128]{3,2,1,0:T(8,128)(2,1)S(1)} collective-permute-done((bf16[8,36,16,128]{3,2,1,0:T(8,128)(2,1)S(1)}, bf16[8,36,16,128]{3,2,1,0:T(8,128)(2,1)S(1)}, u32[]{:S(2)}, u32[]{:S(2)}) %collective-permute-start.22) | collective-permute-done | bytes 1179680 | tf_op jit(solution)/shard_map/ppermute | solution.py:1444
  121.5 2.0 copy-done.34
  123.5 35.2 %feed_forward.1 = (bf16[1024,3072]{1,0:T(8,128)(2,1)}, bf16[1024,3072]{1,0:T(8,128)(2,1)}, f32[24,128]{1,0:T(8,128)S(1)}, bf16[16,36,16,128]{3,2,1,0:T(8,128)(2,...) custom-call(s32[1]{0:T(128)} %bitcast.me_ref, ...), custom_call_target="tpu_custom_call" | custom-call | flops 19327352832 | bytes 41943040 | tf_op jit(solution)/shard_map/feed_forward/pallas_call | solution.py:883
  159.3 2.8 copy-done.3
  164.7 10.9 %feed_forward_out.1 = (bf16[1024,768]{1,0:T(8,128)(2,1)}, f32[6,128]{1,0:T(8,128)S(1)}) custom-call(s32[1]{0:T(128)} %bitcast.me_ref, bf16[1024,3072]{1,0:T(8,128)(2,1)S(1)} %copy-done.3, f32[1024,768]{1,0:T(8,128)S(1)} %copy-done.1, bf16[1024,768]{1,0:T(8,128)(2,1)S(1)} %copy-done, f32[88,128]{1,0:T(8,128)S(1)} %copy-done.30, ...), custom_call_target="tpu_custom_call" | custom-call | flops 4831838208 | bytes 20971520 | tf_op jit(solution)/shard_map/feed_forward_out/pallas_call | solution.py:1005
  175.7 1.3 add_convert_fusion.1
  180.7 16.2 %feed_forward_in.1 = (f32[1024,768]{1,0:T(8,128)}, bf16[1024,768]{1,0:T(8,128)(2,1)}, bf16[2,8,9,16,128]{4,3,2,1,0:T(8,128)(2,1)S(1)}, bf16[2,8,9,16,128]{4,3,2,1,0:T(8,128)(2,1)S(1)}, f32[24,128]{1,0:T(8,128)S(1)}) custom-call(s32[1]{0:T(128)} %bitcast.me_ref, bf16[1024,3072]{1,0:T(8,128)(2,1)} %get-tuple-element.197.dz_in, ...), custom_call_target="tpu_custom_call" | custom-call | flops 7247757312 | bytes 41943040 | tf_op jit(solution)/shard_map/feed_forward_in/pallas_call | solution.py:1119
  196.9 1.4 copy-done.33
  198.3 10.6 %attend_backward.2.dqkv_in.dqkv0_in = bf16[1024,1152]{1,0:T(8,128)(2,1)S(1)} custom-call(s32[3,8]{1,0:T(4,128)S(1)} %copy-done.32, bf16[1024,2304]{1,0:T(8,128)(2,1)S(1)} %bitcast.17, bf16[1024,768]{1,0:T(8,128)(2,1)S(1)} %copy-done.33, f32[48,2,256]{2,1,0:T(2,128)S(1)} %copy-done.35, f32[8,128]{1,0:T(8,128)S(1)} %copy-done.31), custom_call_target="tpu_custom_call" | custom-call | flops 3221225472 | bytes 14680064 | tf_op jit(solution)/shard_map/attend_backward/pallas_call | solution.py:1234
  209.0 3.2 %qkv_weight_grad.1 = (bf16[16,9,16,128]{3,2,1,0:T(8,128)(2,1)S(1)}, bf16[16,9,16,128]{3,2,1,0:T(8,128)(2,1)S(1)}, bf16[16,9,16,128]{3,2,1,0:T(8,128)(2,1)S(1)}, bf16[16,9,16,128]{3,2,1,0:T(8,128)(2,1)S(1)}) custom-call(s32[1]{0:T(128)} %bitcast.me_ref, bf16[1024,768]{1,0:T(8,128)(2,1)S(1)} %copy-done.37, ...), custom_call_target="tpu_custom_call" | custom-call | flops 1811939328 | bytes 7864320 | tf_op jit(solution)/shard_map/qkv_weight_grad/pallas_call | solution.py:1294
  212.3 1.5 add_convert_fusion.3
  214.1 1.3 add_convert_fusion.2
  215.5 1.5 collective-permute-start.29
  217.5 10.8 %attend_backward.3.dqkv1_in = bf16[1024,1152]{1,0:T(8,128)(2,1)S(1)} custom-call(s32[3,8]{1,0:T(4,128)S(1)} %copy-done.32, bf16[1024,2304]{1,0:T(8,128)(2,1)S(1)} %bitcast.17, bf16[1024,768]{1,0:T(8,128)(2,1)S(1)} %copy-done.33, f32[48,2,256]{2,1,0:T(2,128)S(1)} %copy-done.35, f32[8,128]{1,0:T(8,128)S(1)} %copy-done.31), custom_call_target="tpu_custom_call" | custom-call | flops 3221225472 | bytes 14680064 | tf_op jit(solution)/shard_map/attend_backward/pallas_call | solution.py:1234
  228.3 2.4 collective-permute-done.28
  231.2 1.4 convert_add_fusion
  232.7 1.4 convert_add_fusion.1
  236.0 1.7 collective-permute-start.34
  237.6 1.5 collective-permute-start.35
  239.1 12.9 %qkv_backward.1 = (f32[1024,768]{1,0:T(8,128)}, bf16[16,10,16,128]{3,2,1,0:T(8,128)(2,1)S(1)}, bf16[16,10,16,128]{3,2,1,0:T(8,128)(2,1)S(1)}, bf16[16,10,16,128]...) custom-call(s32[1]{0:T(128)} %bitcast.me_ref, bf16[1024,768]{1,0:T(8,128)(2,1)} %tokens_in.1, ...), custom_call_target="tpu_custom_call" | custom-call | flops 5435817984 | bytes 23592960 | tf_op jit(solution)/shard_map/qkv_backward/pallas_call | solution.py:1410
  252.2 1.5 collective-permute-start.36
  253.7 2.4 collective-permute-start.40
  256.2 1.7 collective-permute-start.37
  258.4 2.9 collective-permute-done.37
  261.7 1.7 collective-permute-start.41
  263.4 1.5 collective-permute-start.42
  265.0 1.8 collective-permute-start.44
  266.8 2.5 collective-permute-start.45
  269.3 1.5 collective-permute-done.41
  271.0 2.1 collective-permute-done.45
  273.1 2.6 collective-permute-start.46
  277.1 3.1 collective-permute-done.46
  281.7 2.8 collective-permute-start.50
  284.5 1.6 collective-permute-start.51
  287.1 3.6 %collective-permute-done.51 = bf16[2,10,16,128]{3,2,1,0:T(8,128)(2,1)S(1)} collective-permute-done((bf16[2,10,16,128]{3,2,1,0:T(8,128)(2,1)S(1)}, bf16[2,10,16,128]{3,2,1,0:T(8,128)(2,1)S(1)}, u32[]{:S(2)}, u32[]{:S(2)}) %collective-permute-start.51) | collective-permute-done | bytes 81952 | tf_op jit(solution)/shard_map/ppermute | solution.py:1444
  291.4 2.4 spread.1
  293.9 1.9 collective-permute-start.53
  295.8 3.9 %collective-permute-start.52 = (f32[72,128]{1,0:T(8,128)}, f32[72,128]{1,0:T(8,128)S(1)}, u32[]{:S(2)}, u32[]{:S(2)}) collective-permute-start(f32[72,128]{1,0:T(8,128)} %get-tuple-element.277), channel_id=1, source_target_pairs={{0,1},{1,2},{2,3},{3,4},{4,5},{15,16},{16,17}} | collective-permute-start | bytes 110600 | tf_op jit(solution)/shard_map/ppermute | solution.py:1754
  299.7 5.2 %collective-permute-done.52.below = f32[72,128]{1,0:T(8,128)S(1)} collective-permute-done((f32[72,128]{1,0:T(8,128)}, f32[72,128]{1,0:T(8,128)S(1)}, u32[]{:S(2)}, u32[]{:S(2)}) %collective-permute-start.52) | collective-permute-done | bytes 36896 | tf_op jit(solution)/shard_map/ppermute | solution.py:1754
  305.5 2.2 close.1
  (237 shorter events, 30.3 us)
Async XLA Ops:
  1.9 12.6 %collective-permute-start.1 = (bf16[72,128]{1,0:T(8,128)(2,1)S(1)}, bf16[72,128]{1,0:T(8,128)(2,1)S(1)}, u32[]{:S(2)}, u32[]{:S(2)}) collective-permute-start(bf16[72,128]{1,0:T(8,128)(2,1)S(1)} %pad_maximum_fusion.19), channel_id=1, source_target_pairs={{1,0},{2,1},{3,2},{4,3},{5,4},{16,15},{17,16}} | collective-permute-start | bytes 55304 | tf_op jit(solution)/shard_map/ppermute | solution.py:1668
  7.8 8.8 %collective-permute-start = (bf16[128,128]{1,0:T(8,128)(2,1)S(1)}, bf16[128,128]{1,0:T(8,128)(2,1)S(1)}, u32[]{:S(2)}, u32[]{:S(2)}) collective-permute-start(bf16[128,128]{1,0:T(8,128)(2,1)S(1)} %pad_maximum_fusion.17), channel_id=1, source_target_pairs={{6,7},{7,8},{8,9},{9,10},{10,11},{11,12},{12,13},{13,14},{14,15},{... | collective-permute-start | bytes 98312 | tf_op jit(solution)/shard_map/ppermute | solution.py:1669
  19.4 7.4 %collective-permute-start.4 = (bf16[2,19,16,128]{3,2,1,0:T(8,128)(2,1)}, bf16[2,19,16,128]{3,2,1,0:T(8,128)(2,1)S(1)}, u32[]{:S(2)}, u32[]{:S(2)}) collective-permute-start(bf16[2,19,16,128]{3,2,1,0:T(8,128)(2,1)} %get-tuple-element.141), channel_id=1, source_target_pairs={{0,6},{1,7},{2,4},{3,5},{4,2},{5,3},{6,0},{7,1},{8,14},{9,15},{10,... | collective-permute-start | bytes 466952 | tf_op jit(solution)/shard_map/ppermute | solution.py:1444
  19.4 10.9 %collective-permute-start.3 = (bf16[2,19,16,128]{3,2,1,0:T(8,128)(2,1)}, bf16[2,19,16,128]{3,2,1,0:T(8,128)(2,1)S(1)}, u32[]{:S(2)}, u32[]{:S(2)}) collective-permute-start(bf16[2,19,16,128]{3,2,1,0:T(8,128)(2,1)} %get-tuple-element.141), channel_id=1, source_target_pairs={{0,4},{1,5},{2,6},{3,7},{4,0},{5,1},{6,2},{7,3},{8,12},{9,13},{10,... | collective-permute-start | bytes 466952 | tf_op jit(solution)/shard_map/ppermute | solution.py:1444
  19.4 10.9 %collective-permute-start.2 = (bf16[2,19,16,128]{3,2,1,0:T(8,128)(2,1)}, bf16[2,19,16,128]{3,2,1,0:T(8,128)(2,1)S(1)}, u32[]{:S(2)}, u32[]{:S(2)}) collective-permute-start(bf16[2,19,16,128]{3,2,1,0:T(8,128)(2,1)} %get-tuple-element.141), channel_id=1, source_target_pairs={{0,2},{1,3},{2,0},{3,1},{4,6},{5,7},{6,4},{7,5},{8,10},{9,11},{10,... | collective-permute-start | bytes 466952 | tf_op jit(solution)/shard_map/ppermute | solution.py:1444
  30.4 8.1 %collective-permute-start.5 = (bf16[4,19,16,128]{3,2,1,0:T(8,128)(2,1)S(1)}, bf16[4,19,16,128]{3,2,1,0:T(8,128)(2,1)S(1)}, u32[]{:S(2)}, u32[]{:S(2)}) collective-permute-start(bf16[4,19,16,128]{3,2,1,0:T(8,128)(2,1)S(1)} %get-tuple-element.143), channel_id=1, source_target_pairs={{0,16},{1,17},{2,18},{3,19},{4,20},{5,21},{6,22},{7,23},{8,24},{9,... | collective-permute-start | bytes 933896 | tf_op jit(solution)/shard_map/ppermute | solution.py:1444
  31.1 8.9 %collective-permute-start.6 = (bf16[4,19,16,128]{3,2,1,0:T(8,128)(2,1)S(1)}, bf16[4,19,16,128]{3,2,1,0:T(8,128)(2,1)S(1)}, u32[]{:S(2)}, u32[]{:S(2)}) collective-permute-start(bf16[4,19,16,128]{3,2,1,0:T(8,128)(2,1)S(1)} %get-tuple-element.144), channel_id=1, source_target_pairs={{0,1},{1,0},{2,3},{3,2},{4,5},{5,4},{6,7},{7,6},{8,9},{9,8},{10,11... | collective-permute-start | bytes 933896 | tf_op jit(solution)/shard_map/ppermute | solution.py:1444
  32.6 11.8 %collective-permute-start.8 = (bf16[2,36,16,128]{3,2,1,0:T(8,128)(2,1)S(1)}, bf16[2,36,16,128]{3,2,1,0:T(8,128)(2,1)S(1)}, u32[]{:S(2)}, u32[]{:S(2)}) collective-permute-start(bf16[2,36,16,128]{3,2,1,0:T(8,128)(2,1)S(1)} %copy-done.47), channel_id=1, source_target_pairs={{0,6},{1,7},{2,4},{3,5},{4,2},{5,3},{6,0},{7,1},{8,14},{9,15},{10,... | collective-permute-start | bytes 884744 | tf_op jit(solution)/shard_map/ppermute | solution.py:1444
  35.1 14.2 %collective-permute-start.7 = (bf16[2,36,16,128]{3,2,1,0:T(8,128)(2,1)S(1)}, bf16[2,36,16,128]{3,2,1,0:T(8,128)(2,1)S(1)}, u32[]{:S(2)}, u32[]{:S(2)}) collective-permute-start(bf16[2,36,16,128]{3,2,1,0:T(8,128)(2,1)S(1)} %copy-done.47), channel_id=1, source_target_pairs={{0,2},{1,3},{2,0},{3,1},{4,6},{5,7},{6,4},{7,5},{8,10},{9,11},{10,... | collective-permute-start | bytes 884744 | tf_op jit(solution)/shard_map/ppermute | solution.py:1444
  38.6 25.9 %copy-start.4 = (bf16[8,19,16,128]{3,2,1,0:T(8,128)(2,1)}, bf16[8,19,16,128]{3,2,1,0:T(8,128)(2,1)S(1)}, u32[]{:S(2)}) copy-start(bf16[8,19,16,128]{3,2,1,0:T(8,128)(2,1)S(1)} %pad_maximum_fusion.2.refs_0_.refs_8_) | copy-start | bytes 1867780
  49.3 15.2 %collective-permute-start.13 = (bf16[2,36,16,128]{3,2,1,0:T(8,128)(2,1)S(1)}, bf16[2,36,16,128]{3,2,1,0:T(8,128)(2,1)S(1)}, u32[]{:S(2)}, u32[]{:S(2)}) collective-permute-start(bf16[2,36,16,128]{3,2,1,0:T(8,128)(2,1)S(1)} %copy-done.47), channel_id=1, source_target_pairs={{0,4},{1,5},{2,6},{3,7},{4,0},{5,1},{6,2},{7,3},{8,12},{9,13},{10,... | collective-permute-start | bytes 884744 | tf_op jit(solution)/shard_map/ppermute | solution.py:1444
  49.9 14.8 %collective-permute-start.11 = (bf16[8,19,16,128]{3,2,1,0:T(8,128)(2,1)S(1)}, bf16[8,19,16,128]{3,2,1,0:T(8,128)(2,1)S(1)}, u32[]{:S(2)}, u32[]{:S(2)}) collective-permute-start(bf16[8,19,16,128]{3,2,1,0:T(8,128)(2,1)S(1)} %pad_maximum_fusion.2.refs_0_.refs_8_), channel_id=1, source_target_pairs={{0,8},{1,9},{2,10},{3,11},{4,12},{5,13},{6,14},{7,15},{8,0},{9,1},... | collective-permute-start | bytes 1867784 | tf_op jit(solution)/shard_map/ppermute | solution.py:1444
  49.9 16.4 %collective-permute-start.9 = (bf16[8,19,16,128]{3,2,1,0:T(8,128)(2,1)S(1)}, bf16[8,19,16,128]{3,2,1,0:T(8,128)(2,1)S(1)}, u32[]{:S(2)}, u32[]{:S(2)}) collective-permute-start(bf16[8,19,16,128]{3,2,1,0:T(8,128)(2,1)S(1)} %pad_maximum_fusion.2.refs_0_.refs_8_), channel_id=1, source_target_pairs={{0,1},{1,0},{2,3},{3,2},{4,5},{5,4},{6,7},{7,6},{8,9},{9,8},{10,11... | collective-permute-start | bytes 1867784 | tf_op jit(solution)/shard_map/ppermute | solution.py:1444
  50.2 16.2 %collective-permute-start.12 = (bf16[8,19,16,128]{3,2,1,0:T(8,128)(2,1)S(1)}, bf16[8,19,16,128]{3,2,1,0:T(8,128)(2,1)S(1)}, u32[]{:S(2)}, u32[]{:S(2)}) collective-permute-start(bf16[8,19,16,128]{3,2,1,0:T(8,128)(2,1)S(1)} %pad_maximum_fusion.3.refs_4_.refs_12_), channel_id=1, source_target_pairs={{0,8},{1,9},{2,10},{3,11},{4,12},{5,13},{6,14},{7,15},{8,0},{9,1},... | collective-permute-start | bytes 1867784 | tf_op jit(solution)/shard_map/ppermute | solution.py:1444
  50.4 16.2 %collective-permute-start.10 = (bf16[8,19,16,128]{3,2,1,0:T(8,128)(2,1)S(1)}, bf16[8,19,16,128]{3,2,1,0:T(8,128)(2,1)S(1)}, u32[]{:S(2)}, u32[]{:S(2)}) collective-permute-start(bf16[8,19,16,128]{3,2,1,0:T(8,128)(2,1)S(1)} %pad_maximum_fusion.3.refs_4_.refs_12_), channel_id=1, source_target_pairs={{0,16},{1,17},{2,18},{3,19},{4,20},{5,21},{6,22},{7,23},{8,24},{9,... | collective-permute-start | bytes 1867784 | tf_op jit(solution)/shard_map/ppermute | solution.py:1444
  66.6 2.1 collective-permute-start.14
  66.6 2.9 collective-permute-start.15
  69.6 15.5 %collective-permute-start.16 = (bf16[4,36,16,128]{3,2,1,0:T(8,128)(2,1)S(1)}, bf16[4,36,16,128]{3,2,1,0:T(8,128)(2,1)}, u32[]{:S(2)}, u32[]{:S(2)}) collective-permute-start(bf16[4,36,16,128]{3,2,1,0:T(8,128)(2,1)S(1)} %pad_maximum_fusion.4), channel_id=1, source_target_pairs={{0,16},{1,17},{2,18},{3,19},{4,20},{5,21},{6,22},{7,23},{8,24},{9,... | collective-permute-start | bytes 1769480 | tf_op jit(solution)/shard_map/ppermute | solution.py:1444
  70.1 16.2 %collective-permute-start.17 = (bf16[4,36,16,128]{3,2,1,0:T(8,128)(2,1)S(1)}, bf16[4,36,16,128]{3,2,1,0:T(8,128)(2,1)S(1)}, u32[]{:S(2)}, u32[]{:S(2)}) collective-permute-start(bf16[4,36,16,128]{3,2,1,0:T(8,128)(2,1)S(1)} %pad_maximum_fusion.5), channel_id=1, source_target_pairs={{0,1},{1,0},{2,3},{3,2},{4,5},{5,4},{6,7},{7,6},{8,9},{9,8},{10,11... | collective-permute-start | bytes 1769480 | tf_op jit(solution)/shard_map/ppermute | solution.py:1444
  86.4 73.0 %copy-start.2 = (bf16[8,36,16,128]{3,2,1,0:T(8,128)(2,1)}, bf16[8,36,16,128]{3,2,1,0:T(8,128)(2,1)S(1)}, u32[]{:S(2)}) copy-start(bf16[8,36,16,128]{3,2,1,0:T(8,128)(2,1)S(1)} %pad_maximum_fusion.1.refs_4_) | copy-start | bytes 3538948
  86.4 19.0 %collective-permute-start.20 = (bf16[8,36,16,128]{3,2,1,0:T(8,128)(2,1)S(1)}, bf16[8,36,16,128]{3,2,1,0:T(8,128)(2,1)S(1)}, u32[]{:S(2)}, u32[]{:S(2)}) collective-permute-start(bf16[8,36,16,128]{3,2,1,0:T(8,128)(2,1)S(1)} %pad_maximum_fusion.refs_0_), channel_id=1, source_target_pairs={{0,8},{1,9},{2,10},{3,11},{4,12},{5,13},{6,14},{7,15},{8,0},{9,1},... | collective-permute-start | bytes 3538952 | tf_op jit(solution)/shard_map/ppermute | solution.py:1444
  86.4 28.4 %collective-permute-start.18 = (bf16[8,36,16,128]{3,2,1,0:T(8,128)(2,1)S(1)}, bf16[8,36,16,128]{3,2,1,0:T(8,128)(2,1)S(1)}, u32[]{:S(2)}, u32[]{:S(2)}) collective-permute-start(bf16[8,36,16,128]{3,2,1,0:T(8,128)(2,1)S(1)} %pad_maximum_fusion.refs_0_), channel_id=1, source_target_pairs={{0,1},{1,0},{2,3},{3,2},{4,5},{5,4},{6,7},{7,6},{8,9},{9,8},{10,11... | collective-permute-start | bytes 3538952 | tf_op jit(solution)/shard_map/ppermute | solution.py:1444
  88.2 26.6 %collective-permute-start.21 = (bf16[8,36,16,128]{3,2,1,0:T(8,128)(2,1)S(1)}, bf16[8,36,16,128]{3,2,1,0:T(8,128)(2,1)S(1)}, u32[]{:S(2)}, u32[]{:S(2)}) collective-permute-start(bf16[8,36,16,128]{3,2,1,0:T(8,128)(2,1)S(1)} %pad_maximum_fusion.1.refs_4_), channel_id=1, source_target_pairs={{0,8},{1,9},{2,10},{3,11},{4,12},{5,13},{6,14},{7,15},{8,0},{9,1},... | collective-permute-start | bytes 3538952 | tf_op jit(solution)/shard_map/ppermute | solution.py:1444
  88.4 28.3 %collective-permute-start.19 = (bf16[8,36,16,128]{3,2,1,0:T(8,128)(2,1)S(1)}, bf16[8,36,16,128]{3,2,1,0:T(8,128)(2,1)}, u32[]{:S(2)}, u32[]{:S(2)}) collective-permute-start(bf16[8,36,16,128]{3,2,1,0:T(8,128)(2,1)S(1)} %pad_maximum_fusion.1.refs_4_), channel_id=1, source_target_pairs={{0,16},{1,17},{2,18},{3,19},{4,20},{5,21},{6,22},{7,23},{8,24},{9,... | collective-permute-start | bytes 3538952 | tf_op jit(solution)/shard_map/ppermute | solution.py:1444
  88.9 32.6 %copy-start.30 = (f32[88,128]{1,0:T(8,128)S(1)}, f32[88,128]{1,0:T(8,128)}, u32[]{:S(2)}) copy-start(f32[88,128]{1,0:T(8,128)} %get-tuple-element.174.small) | copy-start | bytes 135172
  105.4 53.9 %copy-start.8 = (bf16[8,36,16,128]{3,2,1,0:T(8,128)(2,1)}, bf16[8,36,16,128]{3,2,1,0:T(8,128)(2,1)S(1)}, u32[]{:S(2)}) copy-start(bf16[8,36,16,128]{3,2,1,0:T(8,128)(2,1)S(1)} %collective-permute-done.20.refs_2_) | copy-start | bytes 3538948
  114.8 44.5 %copy-start.10 = (bf16[8,36,16,128]{3,2,1,0:T(8,128)(2,1)}, bf16[8,36,16,128]{3,2,1,0:T(8,128)(2,1)S(1)}, u32[]{:S(2)}) copy-start(bf16[8,36,16,128]{3,2,1,0:T(8,128)(2,1)S(1)} %collective-permute-done.18.refs_1_) | copy-start | bytes 3538948
  114.8 44.5 %copy-start.12 = (bf16[8,36,16,128]{3,2,1,0:T(8,128)(2,1)}, bf16[8,36,16,128]{3,2,1,0:T(8,128)(2,1)S(1)}, u32[]{:S(2)}) copy-start(bf16[8,36,16,128]{3,2,1,0:T(8,128)(2,1)S(1)} %collective-permute-done.21.refs_6_) | copy-start | bytes 3538948
  116.7 4.5 %collective-permute-start.22 = (bf16[8,36,16,128]{3,2,1,0:T(8,128)(2,1)S(1)}, bf16[8,36,16,128]{3,2,1,0:T(8,128)(2,1)S(1)}, u32[]{:S(2)}, u32[]{:S(2)}) collective-permute-start(bf16[8,36,16,128]{3,2,1,0:T(8,128)(2,1)S(1)} %collective-permute-done.18.refs_1_), channel_id=1, source_target_pairs={{0,8},{1,9},{2,10},{3,11},{4,12},{5,13},{6,14},{7,15},{8,0},{9,1},... | collective-permute-start | bytes 3538952 | tf_op jit(solution)/shard_map/ppermute | solution.py:1444
  116.7 4.7 %collective-permute-start.23 = (bf16[8,36,16,128]{3,2,1,0:T(8,128)(2,1)}, bf16[8,36,16,128]{3,2,1,0:T(8,128)(2,1)S(1)}, u32[]{:S(2)}, u32[]{:S(2)}) collective-permute-start(bf16[8,36,16,128]{3,2,1,0:T(8,128)(2,1)} %collective-permute-done.19.refs_5_), channel_id=1, source_target_pairs={{0,8},{1,9},{2,10},{3,11},{4,12},{5,13},{6,14},{7,15},{8,0},{9,1},... | collective-permute-start | bytes 3538952 | tf_op jit(solution)/shard_map/ppermute | solution.py:1444
  121.2 37.5 %copy-start.13 = (bf16[8,36,16,128]{3,2,1,0:T(8,128)(2,1)}, bf16[8,36,16,128]{3,2,1,0:T(8,128)(2,1)S(1)}, u32[]{:S(2)}) copy-start(bf16[8,36,16,128]{3,2,1,0:T(8,128)(2,1)S(1)} %collective-permute-done.22.refs_3_) | copy-start | bytes 3538948
  121.5 37.2 %copy-start.15 = (bf16[8,36,16,128]{3,2,1,0:T(8,128)(2,1)}, bf16[8,36,16,128]{3,2,1,0:T(8,128)(2,1)S(1)}, u32[]{:S(2)}) copy-start(bf16[8,36,16,128]{3,2,1,0:T(8,128)(2,1)S(1)} %collective-permute-done.23.refs_7_) | copy-start | bytes 3538948
  123.5 35.8 %copy-start = (bf16[1024,768]{1,0:T(8,128)(2,1)S(1)}, bf16[1024,768]{1,0:T(8,128)(2,1)}, u32[]{:S(2)}) copy-start(bf16[1024,768]{1,0:T(8,128)(2,1)} %cot_in.3) | copy-start | bytes 4718596
  123.5 35.8 %copy-start.1 = (f32[1024,768]{1,0:T(8,128)S(1)}, f32[1024,768]{1,0:T(8,128)}, u32[]{:S(2)}) copy-start(f32[1024,768]{1,0:T(8,128)} %get-tuple-element.185.x1_in) | copy-start | bytes 9437188
  158.7 16.9 %collective-permute-start.24 = (bf16[16,36,16,128]{3,2,1,0:T(8,128)(2,1)}, bf16[16,36,16,128]{3,2,1,0:T(8,128)(2,1)S(1)}, u32[]{:S(2)}, u32[]{:S(2)}) collective-permute-start(bf16[16,36,16,128]{3,2,1,0:T(8,128)(2,1)} %get-tuple-element.189), channel_id=1, source_target_pairs={{0,8},{1,9},{2,10},{3,11},{4,12},{5,13},{6,14},{7,15},{8,0},{9,1},... | collective-permute-start | bytes 7077896 | tf_op jit(solution)/shard_map/ppermute | solution.py:1444
  159.0 16.6 %collective-permute-start.25 = (bf16[16,36,16,128]{3,2,1,0:T(8,128)(2,1)}, bf16[16,36,16,128]{3,2,1,0:T(8,128)(2,1)S(1)}, u32[]{:S(2)}, u32[]{:S(2)}) collective-permute-start(bf16[16,36,16,128]{3,2,1,0:T(8,128)(2,1)} %get-tuple-element.190), channel_id=1, source_target_pairs={{0,8},{1,9},{2,10},{3,11},{4,12},{5,13},{6,14},{7,15},{8,0},{9,1},... | collective-permute-start | bytes 7077896 | tf_op jit(solution)/shard_map/ppermute | solution.py:1444
  177.8 34.4 %collective-permute-start.26 = (bf16[8,36,16,128]{3,2,1,0:T(8,128)(2,1)}, bf16[8,36,16,128]{3,2,1,0:T(8,128)(2,1)}, u32[]{:S(2)}, u32[]{:S(2)}) collective-permute-start(bf16[8,36,16,128]{3,2,1,0:T(8,128)(2,1)} %add_convert_fusion.1), channel_id=1, source_target_pairs={{0,1},{1,0},{2,3},{3,2},{4,5},{5,4},{6,7},{7,6},{8,9},{9,8},{10,11... | collective-permute-start | bytes 3538952 | tf_op jit(solution)/shard_map/ppermute | solution.py:1444
  178.2 34.1 %collective-permute-start.27 = (bf16[8,36,16,128]{3,2,1,0:T(8,128)(2,1)S(1)}, bf16[8,36,16,128]{3,2,1,0:T(8,128)(2,1)}, u32[]{:S(2)}, u32[]{:S(2)}) collective-permute-start(bf16[8,36,16,128]{3,2,1,0:T(8,128)(2,1)S(1)} %add_convert_fusion), channel_id=1, source_target_pairs={{0,16},{1,17},{2,18},{3,19},{4,20},{5,21},{6,22},{7,23},{8,24},{9,... | collective-permute-start | bytes 3538952 | tf_op jit(solution)/shard_map/ppermute | solution.py:1444
  215.4 15.3 %collective-permute-start.28 = (bf16[4,36,16,128]{3,2,1,0:T(8,128)(2,1)S(1)}, bf16[4,36,16,128]{3,2,1,0:T(8,128)(2,1)S(1)}, u32[]{:S(2)}, u32[]{:S(2)}) collective-permute-start(bf16[4,36,16,128]{3,2,1,0:T(8,128)(2,1)S(1)} %add_convert_fusion.3), channel_id=1, source_target_pairs={{0,16},{1,17},{2,18},{3,19},{4,20},{5,21},{6,22},{7,23},{8,24},{9,... | collective-permute-start | bytes 1769480 | tf_op jit(solution)/shard_map/ppermute | solution.py:1444
  215.5 15.7 %collective-permute-start.29 = (bf16[4,36,16,128]{3,2,1,0:T(8,128)(2,1)S(1)}, bf16[4,36,16,128]{3,2,1,0:T(8,128)(2,1)S(1)}, u32[]{:S(2)}, u32[]{:S(2)}) collective-permute-start(bf16[4,36,16,128]{3,2,1,0:T(8,128)(2,1)S(1)} %add_convert_fusion.2), channel_id=1, source_target_pairs={{0,1},{1,0},{2,3},{3,2},{4,5},{5,4},{6,7},{7,6},{8,9},{9,8},{10,11... | collective-permute-start | bytes 1769480 | tf_op jit(solution)/shard_map/ppermute | solution.py:1444
  217.0 14.3 %collective-permute-start.30 = (bf16[16,9,16,128]{3,2,1,0:T(8,128)(2,1)S(1)}, bf16[16,9,16,128]{3,2,1,0:T(8,128)(2,1)S(1)}, u32[]{:S(2)}, u32[]{:S(2)}) collective-permute-start(bf16[16,9,16,128]{3,2,1,0:T(8,128)(2,1)S(1)} %get-tuple-element.220), channel_id=1, source_target_pairs={{0,8},{1,9},{2,10},{3,11},{4,12},{5,13},{6,14},{7,15},{8,0},{9,1},... | collective-permute-start | bytes 1769480 | tf_op jit(solution)/shard_map/ppermute | solution.py:1444
  217.0 14.3 %collective-permute-start.31 = (bf16[16,9,16,128]{3,2,1,0:T(8,128)(2,1)S(1)}, bf16[16,9,16,128]{3,2,1,0:T(8,128)(2,1)S(1)}, u32[]{:S(2)}, u32[]{:S(2)}) collective-permute-start(bf16[16,9,16,128]{3,2,1,0:T(8,128)(2,1)S(1)} %get-tuple-element.221), channel_id=1, source_target_pairs={{0,8},{1,9},{2,10},{3,11},{4,12},{5,13},{6,14},{7,15},{8,0},{9,1},... | collective-permute-start | bytes 1769480 | tf_op jit(solution)/shard_map/ppermute | solution.py:1444
  234.4 17.6 %collective-permute-start.32 = (bf16[8,9,16,128]{3,2,1,0:T(8,128)(2,1)S(1)}, bf16[8,9,16,128]{3,2,1,0:T(8,128)(2,1)S(1)}, u32[]{:S(2)}, u32[]{:S(2)}) collective-permute-start(bf16[8,9,16,128]{3,2,1,0:T(8,128)(2,1)S(1)} %add_convert_fusion.7), channel_id=1, source_target_pairs={{0,1},{1,0},{2,3},{3,2},{4,5},{5,4},{6,7},{7,6},{8,9},{9,8},{10,11... | collective-permute-start | bytes 884744 | tf_op jit(solution)/shard_map/ppermute | solution.py:1444
  235.3 16.8 %collective-permute-start.33 = (bf16[8,9,16,128]{3,2,1,0:T(8,128)(2,1)S(1)}, bf16[8,9,16,128]{3,2,1,0:T(8,128)(2,1)S(1)}, u32[]{:S(2)}, u32[]{:S(2)}) collective-permute-start(bf16[8,9,16,128]{3,2,1,0:T(8,128)(2,1)S(1)} %add_convert_fusion.6), channel_id=1, source_target_pairs={{0,16},{1,17},{2,18},{3,19},{4,20},{5,21},{6,22},{7,23},{8,24},{9,... | collective-permute-start | bytes 884744 | tf_op jit(solution)/shard_map/ppermute | solution.py:1444
  236.0 16.0 %collective-permute-start.34 = (bf16[2,36,16,128]{3,2,1,0:T(8,128)(2,1)S(1)}, bf16[2,36,16,128]{3,2,1,0:T(8,128)(2,1)S(1)}, u32[]{:S(2)}, u32[]{:S(2)}) collective-permute-start(bf16[2,36,16,128]{3,2,1,0:T(8,128)(2,1)S(1)} %pad_maximum_fusion.8), channel_id=1, source_target_pairs={{0,2},{1,3},{2,0},{3,1},{4,6},{5,7},{6,4},{7,5},{8,10},{9,11},{10,... | collective-permute-start | bytes 884744 | tf_op jit(solution)/shard_map/ppermute | solution.py:1444
  237.6 14.4 %collective-permute-start.35 = (bf16[2,36,16,128]{3,2,1,0:T(8,128)(2,1)S(1)}, bf16[2,36,16,128]{3,2,1,0:T(8,128)(2,1)S(1)}, u32[]{:S(2)}, u32[]{:S(2)}) collective-permute-start(bf16[2,36,16,128]{3,2,1,0:T(8,128)(2,1)S(1)} %pad_maximum_fusion.9), channel_id=1, source_target_pairs={{0,4},{1,5},{2,6},{3,7},{4,0},{5,1},{6,2},{7,3},{8,12},{9,13},{10,... | collective-permute-start | bytes 884744 | tf_op jit(solution)/shard_map/ppermute | solution.py:1444
  252.2 6.2 %collective-permute-start.36 = (bf16[4,9,16,128]{3,2,1,0:T(8,128)(2,1)S(1)}, bf16[4,9,16,128]{3,2,1,0:T(8,128)(2,1)S(1)}, u32[]{:S(2)}, u32[]{:S(2)}) collective-permute-start(bf16[4,9,16,128]{3,2,1,0:T(8,128)(2,1)S(1)} %add_convert_fusion.11), channel_id=1, source_target_pairs={{0,16},{1,17},{2,18},{3,19},{4,20},{5,21},{6,22},{7,23},{8,24},{9,... | collective-permute-start | bytes 442376 | tf_op jit(solution)/shard_map/ppermute | solution.py:1444
  253.7 7.9 %collective-permute-start.40 = (bf16[36,16,128]{2,1,0:T(8,128)(2,1)S(1)}, bf16[36,16,128]{2,1,0:T(8,128)(2,1)S(1)}, u32[]{:S(2)}, u32[]{:S(2)}) collective-permute-start(bf16[36,16,128]{2,1,0:T(8,128)(2,1)S(1)} %slice_bitcast_fusion.1), channel_id=1, source_target_pairs={{0,6},{1,7},{2,4},{3,5},{4,2},{5,3},{6,0},{7,1},{8,14},{9,15},{10,... | collective-permute-start | bytes 442376 | tf_op jit(solution)/shard_map/ppermute | solution.py:1444
  256.2 5.1 %collective-permute-start.37 = (bf16[4,9,16,128]{3,2,1,0:T(8,128)(2,1)S(1)}, bf16[4,9,16,128]{3,2,1,0:T(8,128)(2,1)S(1)}, u32[]{:S(2)}, u32[]{:S(2)}) collective-permute-start(bf16[4,9,16,128]{3,2,1,0:T(8,128)(2,1)S(1)} %add_convert_fusion.10), channel_id=1, source_target_pairs={{0,1},{1,0},{2,3},{3,2},{4,5},{5,4},{6,7},{7,6},{8,9},{9,8},{10,11... | collective-permute-start | bytes 442376 | tf_op jit(solution)/shard_map/ppermute | solution.py:1444
  257.8 3.6 %collective-permute-start.38 = (bf16[16,10,16,128]{3,2,1,0:T(8,128)(2,1)S(1)}, bf16[16,10,16,128]{3,2,1,0:T(8,128)(2,1)S(1)}, u32[]{:S(2)}, u32[]{:S(2)}) collective-permute-start(bf16[16,10,16,128]{3,2,1,0:T(8,128)(2,1)S(1)} %get-tuple-element.252), channel_id=1, source_target_pairs={{0,8},{1,9},{2,10},{3,11},{4,12},{5,13},{6,14},{7,15},{8,0},{9,1},... | collective-permute-start | bytes 1966088 | tf_op jit(solution)/shard_map/ppermute | solution.py:1444
  257.8 3.7 %collective-permute-start.39 = (bf16[16,10,16,128]{3,2,1,0:T(8,128)(2,1)S(1)}, bf16[16,10,16,128]{3,2,1,0:T(8,128)(2,1)S(1)}, u32[]{:S(2)}, u32[]{:S(2)}) collective-permute-start(bf16[16,10,16,128]{3,2,1,0:T(8,128)(2,1)S(1)} %get-tuple-element.254), channel_id=1, source_target_pairs={{0,8},{1,9},{2,10},{3,11},{4,12},{5,13},{6,14},{7,15},{8,0},{9,1},... | collective-permute-start | bytes 1966088 | tf_op jit(solution)/shard_map/ppermute | solution.py:1444
  261.7 9.1 %collective-permute-start.41 = (bf16[8,10,16,128]{3,2,1,0:T(8,128)(2,1)S(1)}, bf16[8,10,16,128]{3,2,1,0:T(8,128)(2,1)S(1)}, u32[]{:S(2)}, u32[]{:S(2)}) collective-permute-start(bf16[8,10,16,128]{3,2,1,0:T(8,128)(2,1)S(1)} %add_convert_fusion.5), channel_id=1, source_target_pairs={{0,1},{1,0},{2,3},{3,2},{4,5},{5,4},{6,7},{7,6},{8,9},{9,8},{10,11... | collective-permute-start | bytes 983048 | tf_op jit(solution)/shard_map/ppermute | solution.py:1444
  263.4 7.5 %collective-permute-start.42 = (bf16[8,10,16,128]{3,2,1,0:T(8,128)(2,1)S(1)}, bf16[8,10,16,128]{3,2,1,0:T(8,128)(2,1)S(1)}, u32[]{:S(2)}, u32[]{:S(2)}) collective-permute-start(bf16[8,10,16,128]{3,2,1,0:T(8,128)(2,1)S(1)} %add_convert_fusion.4), channel_id=1, source_target_pairs={{0,16},{1,17},{2,18},{3,19},{4,20},{5,21},{6,22},{7,23},{8,24},{9,... | collective-permute-start | bytes 983048 | tf_op jit(solution)/shard_map/ppermute | solution.py:1444
  264.9 6.1 %collective-permute-start.43 = (bf16[2,9,16,128]{3,2,1,0:T(8,128)(2,1)S(1)}, bf16[2,9,16,128]{3,2,1,0:T(8,128)(2,1)S(1)}, u32[]{:S(2)}, u32[]{:S(2)}) collective-permute-start(bf16[2,9,16,128]{3,2,1,0:T(8,128)(2,1)S(1)} %pad_maximum_fusion.14), channel_id=1, source_target_pairs={{0,2},{1,3},{2,0},{3,1},{4,6},{5,7},{6,4},{7,5},{8,10},{9,11},{10,... | collective-permute-start | bytes 221192 | tf_op jit(solution)/shard_map/ppermute | solution.py:1444
  265.0 6.0 %collective-permute-start.44 = (bf16[2,9,16,128]{3,2,1,0:T(8,128)(2,1)S(1)}, bf16[2,9,16,128]{3,2,1,0:T(8,128)(2,1)S(1)}, u32[]{:S(2)}, u32[]{:S(2)}) collective-permute-start(bf16[2,9,16,128]{3,2,1,0:T(8,128)(2,1)S(1)} %pad_maximum_fusion.15), channel_id=1, source_target_pairs={{0,4},{1,5},{2,6},{3,7},{4,0},{5,1},{6,2},{7,3},{8,12},{9,13},{10,... | collective-permute-start | bytes 221192 | tf_op jit(solution)/shard_map/ppermute | solution.py:1444
  266.8 6.2 %collective-permute-start.45 = (bf16[2,9,16,128]{3,2,1,0:T(8,128)(2,1)S(1)}, bf16[2,9,16,128]{3,2,1,0:T(8,128)(2,1)S(1)}, u32[]{:S(2)}, u32[]{:S(2)}) collective-permute-start(bf16[2,9,16,128]{3,2,1,0:T(8,128)(2,1)S(1)} %pad_maximum_fusion.16), channel_id=1, source_target_pairs={{0,6},{1,7},{2,4},{3,5},{4,2},{5,3},{6,0},{7,1},{8,14},{9,15},{10,... | collective-permute-start | bytes 221192 | tf_op jit(solution)/shard_map/ppermute | solution.py:1444
  273.1 7.1 %collective-permute-start.46 = (bf16[36,16,128]{2,1,0:T(8,128)(2,1)S(1)}, bf16[36,16,128]{2,1,0:T(8,128)(2,1)S(1)}, u32[]{:S(2)}, u32[]{:S(2)}) collective-permute-start(bf16[36,16,128]{2,1,0:T(8,128)(2,1)S(1)} %slice_bitcast_fusion), channel_id=1, source_target_pairs={{0,6},{1,7},{2,4},{3,5},{4,2},{5,3},{6,0},{7,1},{8,14},{9,15},{10,... | collective-permute-start | bytes 442376 | tf_op jit(solution)/shard_map/ppermute | solution.py:1444
  275.6 5.5 %collective-permute-start.47 = (bf16[4,10,16,128]{3,2,1,0:T(8,128)(2,1)S(1)}, bf16[4,10,16,128]{3,2,1,0:T(8,128)(2,1)S(1)}, u32[]{:S(2)}, u32[]{:S(2)}) collective-permute-start(bf16[4,10,16,128]{3,2,1,0:T(8,128)(2,1)S(1)} %add_convert_fusion.9), channel_id=1, source_target_pairs={{0,16},{1,17},{2,18},{3,19},{4,20},{5,21},{6,22},{7,23},{8,24},{9,... | collective-permute-start | bytes 491528 | tf_op jit(solution)/shard_map/ppermute | solution.py:1444
  276.2 5.3 %collective-permute-start.48 = (bf16[4,10,16,128]{3,2,1,0:T(8,128)(2,1)S(1)}, bf16[4,10,16,128]{3,2,1,0:T(8,128)(2,1)S(1)}, u32[]{:S(2)}, u32[]{:S(2)}) collective-permute-start(bf16[4,10,16,128]{3,2,1,0:T(8,128)(2,1)S(1)} %add_convert_fusion.8), channel_id=1, source_target_pairs={{0,1},{1,0},{2,3},{3,2},{4,5},{5,4},{6,7},{7,6},{8,9},{9,8},{10,11... | collective-permute-start | bytes 491528 | tf_op jit(solution)/shard_map/ppermute | solution.py:1444
  281.6 4.5 %collective-permute-start.49 = (bf16[2,10,16,128]{3,2,1,0:T(8,128)(2,1)S(1)}, bf16[2,10,16,128]{3,2,1,0:T(8,128)(2,1)S(1)}, u32[]{:S(2)}, u32[]{:S(2)}) collective-permute-start(bf16[2,10,16,128]{3,2,1,0:T(8,128)(2,1)S(1)} %pad_maximum_fusion.11), channel_id=1, source_target_pairs={{0,2},{1,3},{2,0},{3,1},{4,6},{5,7},{6,4},{7,5},{8,10},{9,11},{10,... | collective-permute-start | bytes 245768 | tf_op jit(solution)/shard_map/ppermute | solution.py:1444
  281.7 5.4 %collective-permute-start.50 = (bf16[2,10,16,128]{3,2,1,0:T(8,128)(2,1)S(1)}, bf16[2,10,16,128]{3,2,1,0:T(8,128)(2,1)S(1)}, u32[]{:S(2)}, u32[]{:S(2)}) collective-permute-start(bf16[2,10,16,128]{3,2,1,0:T(8,128)(2,1)S(1)} %pad_maximum_fusion.12), channel_id=1, source_target_pairs={{0,4},{1,5},{2,6},{3,7},{4,0},{5,1},{6,2},{7,3},{8,12},{9,13},{10,... | collective-permute-start | bytes 245768 | tf_op jit(solution)/shard_map/ppermute | solution.py:1444
  284.5 6.2 %collective-permute-start.51 = (bf16[2,10,16,128]{3,2,1,0:T(8,128)(2,1)S(1)}, bf16[2,10,16,128]{3,2,1,0:T(8,128)(2,1)S(1)}, u32[]{:S(2)}, u32[]{:S(2)}) collective-permute-start(bf16[2,10,16,128]{3,2,1,0:T(8,128)(2,1)S(1)} %pad_maximum_fusion.13), channel_id=1, source_target_pairs={{0,6},{1,7},{2,4},{3,5},{4,2},{5,3},{6,0},{7,1},{8,14},{9,15},{10,... | collective-permute-start | bytes 245768 | tf_op jit(solution)/shard_map/ppermute | solution.py:1444
  293.9 11.0 %collective-permute-start.53 = (f32[128,128]{1,0:T(8,128)}, f32[128,128]{1,0:T(8,128)S(1)}, u32[]{:S(2)}, u32[]{:S(2)}) collective-permute-start(f32[128,128]{1,0:T(8,128)} %get-tuple-element.278), channel_id=1, source_target_pairs={{7,6},{8,7},{9,8},{10,9},{11,10},{12,11},{13,12},{14,13},{15,14},{... | collective-permute-start | bytes 196616 | tf_op jit(solution)/shard_map/ppermute | solution.py:1755
  295.8 9.1 %collective-permute-start.52 = (f32[72,128]{1,0:T(8,128)}, f32[72,128]{1,0:T(8,128)S(1)}, u32[]{:S(2)}, u32[]{:S(2)}) collective-permute-start(f32[72,128]{1,0:T(8,128)} %get-tuple-element.277), channel_id=1, source_target_pairs={{0,1},{1,2},{2,3},{3,4},{4,5},{15,16},{16,17}} | collective-permute-start | bytes 110600 | tf_op jit(solution)/shard_map/ppermute | solution.py:1754
  (46 other events, 306.2 us)

commit v3 on v2

--- a/solution.py
+++ b/solution.py
@@ -1633,12 +1633,13 @@
     paired = (wide, narrow) == (4, 8)
     scale = 1.0 / math.sqrt(rows * devices)
 
-    position = jnp.arange(rows, dtype=jnp.int32)
-    real = (pad_mask > 0) & (position < lengths[0])
-    ids, windows = key_windows(segment_ids, real)
-    query_ids = ids.astype(F32).reshape(rows // QB, QB)
+    def attention_windows(segments, pads, lengths):
+        real = (pads > 0) & (jnp.arange(rows, dtype=jnp.int32) < lengths[0])
+        ids, windows = key_windows(segments, real)
+        return windows, ids.astype(F32).reshape(rows // QB, QB)
 
     if not paired:
+        windows, query_ids = attention_windows(segment_ids, pad_mask, lengths)
         me = jnp.zeros((1,), jnp.int32)
         att, mlp = gather_plainly(params, att_rows, width)
         n1, qkv, small = project_qkv(me, tokens, att)
@@ -1671,11 +1672,14 @@
 
     got = [exchange(att_own, k * Z0) for k in range(1, 4)]
     a, b = along_z(att_own[0], att_own[1], got)
-    a, b, mlp_own, windows, query_ids = together(a, b, mlp_own, windows, query_ids)
+    a, b, mlp_own, *tables = together(a, b, mlp_own, segment_ids, pad_mask, lengths)
+    windows, query_ids = attention_windows(*tables)
     ax, by = exchange(a, X), exchange(b, Y)
     z1, z3 = exchange(mlp_own, Z0), exchange(mlp_own, 3 * Z0)
     a, b = joined(a, ax), joined(b, by)
-    a, b, z1, z3, mlp_own = together(a, b, z1, z3, mlp_own)
+    a, b, z1, z3, mlp_own, windows, query_ids = together(
+        a, b, z1, z3, mlp_own, windows, query_ids
+    )
     ay, bx = exchange(a, Y), exchange(b, X)
     ac, bc = exchange(a, C), exchange(b, C)
     z2 = exchange(mlp_own, 2 * Z0)

time: 311 us -> 307 us (0.987)
  waiting for transfers between devices: 80.7 us -> 76.5 us
    unnamed x112 -> x114, local copies, waits for them, and re-layouts: 12.5 us -> 11 us
  transfers between devices with their start and end apart: 54 -> 54, of which waited for: 28 -> 32; matrix products, arithmetic and copies ran while one was open for 3% -> 2% of each run, Pallas kernels for 30% -> 31%
where the time goes in v3:
time: 307 us; the launch traced here: 304 us
  Pallas kernels  135 us (44%)
  waiting for transfers between devices  76.5 us (25%)
  starting transfers between devices  62.4 us (20%)
  other arithmetic  15 us (5%)
  local copies, waits for them, and re-layouts  12.6 us (4%)
    ppermute x50, waiting for transfers between devices, exchange(): return lax.ppermute(values, AXES, [(d, d ^ bit) for d in range(BLOCKS)])  70.7 us
    ppermute x50, starting transfers between devices, exchange(): return lax.ppermute(values, AXES, [(d, d ^ bit) for d in range(BLOCKS)])  47.4 us
    pallas_call x1, Pallas kernels, feed_forward(): pl.pallas_call(mlp_kernel, out_shape=(shape((rows, FF), BF16), shape((row...  35.2 us
    pallas_call x2, Pallas kernels, attend_back(): pl.pallas_call(partial(attend_back_kernel, group), out_shape=shape((rows,...  21.8 us
    pallas_call x1, Pallas kernels, attend(): pl.pallas_call(attend_kernel, out_shape=(shape((rows, width), BF16), shap...  17.6 us
    pallas_call x1, Pallas kernels, split(): pl.pallas_call(split_kernel, out_shape=(shape((rows, width), F32), shape(...  16.2 us
    pallas_call x1, Pallas kernels, qkv_back(): pl.pallas_call(qkv_back_kernel, out_shape=(shape((rows, width), F32), hal...  12.9 us
    unnamed x114, local copies, waits for them, and re-layouts  11 us
  transfers between devices with their start and end apart: 54, of which 32 were waited for; matrix products, arithmetic and copies ran while one was open for 2% of the time, Pallas kernels for 31%

profile of v3, /device:TPU:2, one launch (start us, length us, event | category | flops | bytes accessed | tf_op | source)
XLA Modules:
  0.0 303.8 jit_solution(18332460103362818575)
XLA Ops:
  1.9 3.4 %collective-permute-start = (bf16[128,128]{1,0:T(8,128)(2,1)S(1)}, bf16[128,128]{1,0:T(8,128)(2,1)S(1)}, u32[]{:S(2)}, u32[]{:S(2)}) collective-permute-start(bf16[128,128]{1,0:T(8,128)(2,1)S(1)} %pad_maximum_fusion.17), channel_id=1, source_target_pairs={{6,7},{7,8},{8,9},{9,10},{10,11},{11,12},{12,13},{13,14},{14,15},{... | collective-permute-start | bytes 98312 | tf_op jit(solution)/shard_map/ppermute | solution.py:1670
  5.4 5.7 %collective-permute-start.1 = (bf16[72,128]{1,0:T(8,128)(2,1)S(1)}, bf16[72,128]{1,0:T(8,128)(2,1)S(1)}, u32[]{:S(2)}, u32[]{:S(2)}) collective-permute-start(bf16[72,128]{1,0:T(8,128)(2,1)S(1)} %pad_maximum_fusion.19), channel_id=1, source_target_pairs={{1,0},{2,1},{3,2},{4,3},{5,4},{16,15},{17,16}} | collective-permute-start | bytes 55304 | tf_op jit(solution)/shard_map/ppermute | solution.py:1669
  13.2 2.1 pack.1
  15.4 4.3 %collective-permute-start.2 = (bf16[2,19,16,128]{3,2,1,0:T(8,128)(2,1)}, bf16[2,19,16,128]{3,2,1,0:T(8,128)(2,1)S(1)}, u32[]{:S(2)}, u32[]{:S(2)}) collective-permute-start(bf16[2,19,16,128]{3,2,1,0:T(8,128)(2,1)} %get-tuple-element.144), channel_id=1, source_target_pairs={{0,2},{1,3},{2,0},{3,1},{4,6},{5,7},{6,4},{7,5},{8,10},{9,11},{10,... | collective-permute-start | bytes 466952 | tf_op jit(solution)/shard_map/ppermute | solution.py:1444
  20.6 3.5 %collective-permute-done.4 = bf16[2,19,16,128]{3,2,1,0:T(8,128)(2,1)S(1)} collective-permute-done((bf16[2,19,16,128]{3,2,1,0:T(8,128)(2,1)}, bf16[2,19,16,128]{3,2,1,0:T(8,128)(2,1)S(1)}, u32[]{:S(2)}, u32[]{:S(2)}) %collective-permute-start.4) | collective-permute-done | bytes 155680 | tf_op jit(solution)/shard_map/ppermute | solution.py:1444
  24.2 3.6 %collective-permute-done.3 = bf16[2,19,16,128]{3,2,1,0:T(8,128)(2,1)S(1)} collective-permute-done((bf16[2,19,16,128]{3,2,1,0:T(8,128)(2,1)}, bf16[2,19,16,128]{3,2,1,0:T(8,128)(2,1)S(1)}, u32[]{:S(2)}, u32[]{:S(2)}) %collective-permute-start.3) | collective-permute-done | bytes 155680 | tf_op jit(solution)/shard_map/ppermute | solution.py:1444
  28.9 2.2 collective-permute-start.8
  32.7 5.9 %collective-permute-done.5 = bf16[4,19,16,128]{3,2,1,0:T(8,128)(2,1)S(1)} collective-permute-done((bf16[4,19,16,128]{3,2,1,0:T(8,128)(2,1)S(1)}, bf16[4,19,16,128]{3,2,1,0:T(8,128)(2,1)S(1)}, u32[]{:S(2)}, u32[]{:S(2)}) %collective-permute-start.5) | collective-permute-done | bytes 311328 | tf_op jit(solution)/shard_map/ppermute | solution.py:1444
  40.7 3.8 %collective-permute-done.7 = bf16[2,36,16,128]{3,2,1,0:T(8,128)(2,1)S(1)} collective-permute-done((bf16[2,36,16,128]{3,2,1,0:T(8,128)(2,1)S(1)}, bf16[2,36,16,128]{3,2,1,0:T(8,128)(2,1)S(1)}, u32[]{:S(2)}, u32[]{:S(2)}) %collective-permute-start.7) | collective-permute-done | bytes 294944 | tf_op jit(solution)/shard_map/ppermute | solution.py:1444
  44.6 1.5 collective-permute-start.13
  46.6 2.9 collective-permute-start.10
  49.5 10.4 %collective-permute-done.13 = bf16[2,36,16,128]{3,2,1,0:T(8,128)(2,1)S(1)} collective-permute-done((bf16[2,36,16,128]{3,2,1,0:T(8,128)(2,1)S(1)}, bf16[2,36,16,128]{3,2,1,0:T(8,128)(2,1)S(1)}, u32[]{:S(2)}, u32[]{:S(2)}) %collective-permute-start.13) | collective-permute-done | bytes 294944 | tf_op jit(solution)/shard_map/ppermute | solution.py:1444
  60.1 2.4 collective-permute-done.9.refs_1_.refs_9_
  62.5 1.4 collective-permute-done.10.refs_5_.refs_13_
  64.4 1.5 collective-permute-done.14.refs_3_.refs_11_
  66.9 1.7 collective-permute-start.16
  68.7 10.2 %qkv_forward.1 = (bf16[1024,768]{1,0:T(8,128)(2,1)}, bf16[1024,2304]{1,0:T(8,128)(2,1)}, f32[88,128]{1,0:T(8,128)}) custom-call(s32[1]{0:T(128)} %bitcast.me_ref, bf16[1024,768]{1,0:T(8,128)(2,1)} %tokens_in.1, bf16[8,19,16,128]{3,2,1,0:T(8,128)(2,1)} %copy-done.4, bf16[8,19,16,128]{3,2,1,0:T(8,128)(2,1)} %copy-done.19, bf16[8,19,16,128]{3,2,1,0:T(8,128)(2,1)} %copy-done.17, ...), custom_call_target="tpu_custom_call" | custom-call | flops 3623878656 | bytes 9437184 | tf_op jit(solution)/shard_map/qkv_forward/pallas_call | solution.py:430
  78.9 3.4 %collective-permute-done.16 = bf16[4,36,16,128]{3,2,1,0:T(8,128)(2,1)} collective-permute-done((bf16[4,36,16,128]{3,2,1,0:T(8,128)(2,1)S(1)}, bf16[4,36,16,128]{3,2,1,0:T(8,128)(2,1)}, u32[]{:S(2)}, u32[]{:S(2)}) %collective-permute-start.16) | collective-permute-done | bytes 589856 | tf_op jit(solution)/shard_map/ppermute | solution.py:1444
  84.6 1.4 collective-permute-start.19
  86.0 17.6 %attend_forward.1 = (bf16[1024,768]{1,0:T(8,128)(2,1)}, f32[1024,768]{1,0:T(8,128)}, bf16[1024,768]{1,0:T(8,128)(2,1)}, bf16[1024,768]{1,0:T(8,128)(2,1)}, bf16[...) custom-call(s32[1]{0:T(128)} %bitcast.me_ref, s32[3,8]{1,0:T(4,128)} %pad_add_fusion.windows, ...), custom_call_target="tpu_custom_call" | custom-call | flops 1610612736 | bytes 15728640 | tf_op jit(solution)/shard_map/attend_forward/pallas_call | solution.py:635
  103.6 8.7 %collective-permute-done.18.refs_1_ = bf16[8,36,16,128]{3,2,1,0:T(8,128)(2,1)S(1)} collective-permute-done((bf16[8,36,16,128]{3,2,1,0:T(8,128)(2,1)S(1)}, bf16[8,36,16,128]{3,2,1,0:T(8,128)(2,1)S(1)}, u32[]{:S(2)}, u32[]{:S(2)}) %collective-permute-start.18) | collective-permute-done | bytes 1179680 | tf_op jit(solution)/shard_map/ppermute | solution.py:1444
  113.4 4.0 %collective-permute-done.22.refs_3_ = bf16[8,36,16,128]{3,2,1,0:T(8,128)(2,1)S(1)} collective-permute-done((bf16[8,36,16,128]{3,2,1,0:T(8,128)(2,1)S(1)}, bf16[8,36,16,128]{3,2,1,0:T(8,128)(2,1)S(1)}, u32[]{:S(2)}, u32[]{:S(2)}) %collective-permute-start.22) | collective-permute-done | bytes 1179680 | tf_op jit(solution)/shard_map/ppermute | solution.py:1444
  117.7 2.0 copy-done.34
  119.7 35.2 %feed_forward.1 = (bf16[1024,3072]{1,0:T(8,128)(2,1)}, bf16[1024,3072]{1,0:T(8,128)(2,1)}, f32[24,128]{1,0:T(8,128)S(1)}, bf16[16,36,16,128]{3,2,1,0:T(8,128)(2,...) custom-call(s32[1]{0:T(128)} %bitcast.me_ref, ...), custom_call_target="tpu_custom_call" | custom-call | flops 19327352832 | bytes 41943040 | tf_op jit(solution)/shard_map/feed_forward/pallas_call | solution.py:883
  155.6 2.8 copy-done.3
  158.3 1.3 copy-done.14
  160.9 10.9 %feed_forward_out.1 = (bf16[1024,768]{1,0:T(8,128)(2,1)}, f32[6,128]{1,0:T(8,128)S(1)}) custom-call(s32[1]{0:T(128)} %bitcast.me_ref, bf16[1024,3072]{1,0:T(8,128)(2,1)S(1)} %copy-done.3, f32[1024,768]{1,0:T(8,128)S(1)} %copy-done.1, bf16[1024,768]{1,0:T(8,128)(2,1)S(1)} %copy-done, f32[88,128]{1,0:T(8,128)S(1)} %copy-done.30, ...), custom_call_target="tpu_custom_call" | custom-call | flops 4831838208 | bytes 20971520 | tf_op jit(solution)/shard_map/feed_forward_out/pallas_call | solution.py:1005
  171.9 1.3 add_convert_fusion.1
  174.0 1.6 collective-permute-start.26
  175.7 2.0 collective-permute-start.27
  177.8 16.2 %feed_forward_in.1 = (f32[1024,768]{1,0:T(8,128)}, bf16[1024,768]{1,0:T(8,128)(2,1)}, bf16[2,8,9,16,128]{4,3,2,1,0:T(8,128)(2,1)S(1)}, bf16[2,8,9,16,128]{4,3,2,1,0:T(8,128)(2,1)S(1)}, f32[24,128]{1,0:T(8,128)S(1)}) custom-call(s32[1]{0:T(128)} %bitcast.me_ref, bf16[1024,3072]{1,0:T(8,128)(2,1)} %get-tuple-element.203.dz_in, ...), custom_call_target="tpu_custom_call" | custom-call | flops 7247757312 | bytes 41943040 | tf_op jit(solution)/shard_map/feed_forward_in/pallas_call | solution.py:1119
  194.0 1.4 copy-done.33
  195.4 10.8 %attend_backward.2.dqkv_in.dqkv0_in = bf16[1024,1152]{1,0:T(8,128)(2,1)S(1)} custom-call(s32[3,8]{1,0:T(4,128)S(1)} %copy-done.32, bf16[1024,2304]{1,0:T(8,128)(2,1)S(1)} %bitcast.17, bf16[1024,768]{1,0:T(8,128)(2,1)S(1)} %copy-done.33, f32[48,2,256]{2,1,0:T(2,128)S(1)} %copy-done.35, f32[8,128]{1,0:T(8,128)S(1)} %copy-done.31), custom_call_target="tpu_custom_call" | custom-call | flops 3221225472 | bytes 14680064 | tf_op jit(solution)/shard_map/attend_backward/pallas_call | solution.py:1234
  206.3 3.2 %qkv_weight_grad.1 = (bf16[16,9,16,128]{3,2,1,0:T(8,128)(2,1)S(1)}, bf16[16,9,16,128]{3,2,1,0:T(8,128)(2,1)S(1)}, bf16[16,9,16,128]{3,2,1,0:T(8,128)(2,1)S(1)}, bf16[16,9,16,128]{3,2,1,0:T(8,128)(2,1)S(1)}) custom-call(s32[1]{0:T(128)} %bitcast.me_ref, bf16[1024,768]{1,0:T(8,128)(2,1)S(1)} %copy-done.37, ...), custom_call_target="tpu_custom_call" | custom-call | flops 1811939328 | bytes 7864320 | tf_op jit(solution)/shard_map/qkv_weight_grad/pallas_call | solution.py:1294
  209.6 1.5 add_convert_fusion.3
  211.4 1.3 add_convert_fusion.2
  212.7 2.5 collective-permute-start.29
  215.8 11.0 %attend_backward.3.dqkv1_in = bf16[1024,1152]{1,0:T(8,128)(2,1)S(1)} custom-call(s32[3,8]{1,0:T(4,128)S(1)} %copy-done.32, bf16[1024,2304]{1,0:T(8,128)(2,1)S(1)} %bitcast.17, bf16[1024,768]{1,0:T(8,128)(2,1)S(1)} %copy-done.33, f32[48,2,256]{2,1,0:T(2,128)S(1)} %copy-done.35, f32[8,128]{1,0:T(8,128)S(1)} %copy-done.31), custom_call_target="tpu_custom_call" | custom-call | flops 3221225472 | bytes 14680064 | tf_op jit(solution)/shard_map/attend_backward/pallas_call | solution.py:1234
  228.5 1.4 convert_add_fusion
  229.9 1.4 convert_add_fusion.1
  231.7 1.8 collective-permute-start.32
  233.8 1.4 collective-permute-start.34
  236.0 12.9 %qkv_backward.1 = (f32[1024,768]{1,0:T(8,128)}, bf16[16,10,16,128]{3,2,1,0:T(8,128)(2,1)S(1)}, bf16[16,10,16,128]{3,2,1,0:T(8,128)(2,1)S(1)}, bf16[16,10,16,128]...) custom-call(s32[1]{0:T(128)} %bitcast.me_ref, bf16[1024,768]{1,0:T(8,128)(2,1)} %tokens_in.1, ...), custom_call_target="tpu_custom_call" | custom-call | flops 5435817984 | bytes 23592960 | tf_op jit(solution)/shard_map/qkv_backward/pallas_call | solution.py:1410
  250.1 1.4 collective-permute-start.36
  251.5 1.6 collective-permute-start.40
  254.0 1.3 collective-permute-done.36
  255.4 2.9 collective-permute-done.37
  259.9 2.7 collective-permute-start.44
  262.6 1.7 collective-permute-start.45
  264.2 2.2 collective-permute-done.41
  266.5 1.3 collective-permute-done.42
  268.7 1.8 collective-permute-start.46
  270.6 1.3 collective-permute-start.47
  271.9 1.6 collective-permute-start.48
  274.2 1.6 collective-permute-done.46
  278.0 2.4 collective-permute-start.50
  280.4 1.4 collective-permute-start.51
  281.8 1.5 collective-permute-done.50
  283.4 3.3 %collective-permute-done.51 = bf16[2,10,16,128]{3,2,1,0:T(8,128)(2,1)S(1)} collective-permute-done((bf16[2,10,16,128]{3,2,1,0:T(8,128)(2,1)S(1)}, bf16[2,10,16,128]{3,2,1,0:T(8,128)(2,1)S(1)}, u32[]{:S(2)}, u32[]{:S(2)}) %collective-permute-start.51) | collective-permute-done | bytes 81952 | tf_op jit(solution)/shard_map/ppermute | solution.py:1444
  287.4 2.4 spread.1
  289.8 1.9 collective-permute-start.53
  291.7 3.9 %collective-permute-start.52 = (f32[72,128]{1,0:T(8,128)}, f32[72,128]{1,0:T(8,128)S(1)}, u32[]{:S(2)}, u32[]{:S(2)}) collective-permute-start(f32[72,128]{1,0:T(8,128)} %get-tuple-element.283), channel_id=1, source_target_pairs={{0,1},{1,2},{2,3},{3,4},{4,5},{15,16},{16,17}} | collective-permute-start | bytes 110600 | tf_op jit(solution)/shard_map/ppermute | solution.py:1758
  295.6 5.2 %collective-permute-done.52.below = f32[72,128]{1,0:T(8,128)S(1)} collective-permute-done((f32[72,128]{1,0:T(8,128)}, f32[72,128]{1,0:T(8,128)S(1)}, u32[]{:S(2)}, u32[]{:S(2)}) %collective-permute-start.52) | collective-permute-done | bytes 36896 | tf_op jit(solution)/shard_map/ppermute | solution.py:1758
  301.4 2.2 close.1
  (239 shorter events, 30.0 us)
Async XLA Ops:
  1.9 10.7 %collective-permute-start = (bf16[128,128]{1,0:T(8,128)(2,1)S(1)}, bf16[128,128]{1,0:T(8,128)(2,1)S(1)}, u32[]{:S(2)}, u32[]{:S(2)}) collective-permute-start(bf16[128,128]{1,0:T(8,128)(2,1)S(1)} %pad_maximum_fusion.17), channel_id=1, source_target_pairs={{6,7},{7,8},{8,9},{9,10},{10,11},{11,12},{12,13},{13,14},{14,15},{... | collective-permute-start | bytes 98312 | tf_op jit(solution)/shard_map/ppermute | solution.py:1670
  5.4 7.2 %collective-permute-start.1 = (bf16[72,128]{1,0:T(8,128)(2,1)S(1)}, bf16[72,128]{1,0:T(8,128)(2,1)S(1)}, u32[]{:S(2)}, u32[]{:S(2)}) collective-permute-start(bf16[72,128]{1,0:T(8,128)(2,1)S(1)} %pad_maximum_fusion.19), channel_id=1, source_target_pairs={{1,0},{2,1},{3,2},{4,3},{5,4},{16,15},{17,16}} | collective-permute-start | bytes 55304 | tf_op jit(solution)/shard_map/ppermute | solution.py:1669
  15.3 8.9 %collective-permute-start.4 = (bf16[2,19,16,128]{3,2,1,0:T(8,128)(2,1)}, bf16[2,19,16,128]{3,2,1,0:T(8,128)(2,1)S(1)}, u32[]{:S(2)}, u32[]{:S(2)}) collective-permute-start(bf16[2,19,16,128]{3,2,1,0:T(8,128)(2,1)} %get-tuple-element.144), channel_id=1, source_target_pairs={{0,6},{1,7},{2,4},{3,5},{4,2},{5,3},{6,0},{7,1},{8,14},{9,15},{10,... | collective-permute-start | bytes 466952 | tf_op jit(solution)/shard_map/ppermute | solution.py:1444
  15.3 12.5 %collective-permute-start.3 = (bf16[2,19,16,128]{3,2,1,0:T(8,128)(2,1)}, bf16[2,19,16,128]{3,2,1,0:T(8,128)(2,1)S(1)}, u32[]{:S(2)}, u32[]{:S(2)}) collective-permute-start(bf16[2,19,16,128]{3,2,1,0:T(8,128)(2,1)} %get-tuple-element.144), channel_id=1, source_target_pairs={{0,4},{1,5},{2,6},{3,7},{4,0},{5,1},{6,2},{7,3},{8,12},{9,13},{10,... | collective-permute-start | bytes 466952 | tf_op jit(solution)/shard_map/ppermute | solution.py:1444
  15.4 12.5 %collective-permute-start.2 = (bf16[2,19,16,128]{3,2,1,0:T(8,128)(2,1)}, bf16[2,19,16,128]{3,2,1,0:T(8,128)(2,1)S(1)}, u32[]{:S(2)}, u32[]{:S(2)}) collective-permute-start(bf16[2,19,16,128]{3,2,1,0:T(8,128)(2,1)} %get-tuple-element.144), channel_id=1, source_target_pairs={{0,2},{1,3},{2,0},{3,1},{4,6},{5,7},{6,4},{7,5},{8,10},{9,11},{10,... | collective-permute-start | bytes 466952 | tf_op jit(solution)/shard_map/ppermute | solution.py:1444
  28.9 11.8 %collective-permute-start.8 = (bf16[2,36,16,128]{3,2,1,0:T(8,128)(2,1)S(1)}, bf16[2,36,16,128]{3,2,1,0:T(8,128)(2,1)S(1)}, u32[]{:S(2)}, u32[]{:S(2)}) collective-permute-start(bf16[2,36,16,128]{3,2,1,0:T(8,128)(2,1)S(1)} %copy-done.47), channel_id=1, source_target_pairs={{0,6},{1,7},{2,4},{3,5},{4,2},{5,3},{6,0},{7,1},{8,14},{9,15},{10,... | collective-permute-start | bytes 884744 | tf_op jit(solution)/shard_map/ppermute | solution.py:1444
  31.1 13.5 %collective-permute-start.7 = (bf16[2,36,16,128]{3,2,1,0:T(8,128)(2,1)S(1)}, bf16[2,36,16,128]{3,2,1,0:T(8,128)(2,1)S(1)}, u32[]{:S(2)}, u32[]{:S(2)}) collective-permute-start(bf16[2,36,16,128]{3,2,1,0:T(8,128)(2,1)S(1)} %copy-done.47), channel_id=1, source_target_pairs={{0,2},{1,3},{2,0},{3,1},{4,6},{5,7},{6,4},{7,5},{8,10},{9,11},{10,... | collective-permute-start | bytes 884744 | tf_op jit(solution)/shard_map/ppermute | solution.py:1444
  31.1 7.5 %collective-permute-start.5 = (bf16[4,19,16,128]{3,2,1,0:T(8,128)(2,1)S(1)}, bf16[4,19,16,128]{3,2,1,0:T(8,128)(2,1)S(1)}, u32[]{:S(2)}, u32[]{:S(2)}) collective-permute-start(bf16[4,19,16,128]{3,2,1,0:T(8,128)(2,1)S(1)} %get-tuple-element.146), channel_id=1, source_target_pairs={{0,16},{1,17},{2,18},{3,19},{4,20},{5,21},{6,22},{7,23},{8,24},{9,... | collective-permute-start | bytes 933896 | tf_op jit(solution)/shard_map/ppermute | solution.py:1444
  31.7 8.0 %collective-permute-start.6 = (bf16[4,19,16,128]{3,2,1,0:T(8,128)(2,1)S(1)}, bf16[4,19,16,128]{3,2,1,0:T(8,128)(2,1)S(1)}, u32[]{:S(2)}, u32[]{:S(2)}) collective-permute-start(bf16[4,19,16,128]{3,2,1,0:T(8,128)(2,1)S(1)} %get-tuple-element.147), channel_id=1, source_target_pairs={{0,1},{1,0},{2,3},{3,2},{4,5},{5,4},{6,7},{7,6},{8,9},{9,8},{10,11... | collective-permute-start | bytes 933896 | tf_op jit(solution)/shard_map/ppermute | solution.py:1444
  38.7 21.3 %copy-start.4 = (bf16[8,19,16,128]{3,2,1,0:T(8,128)(2,1)}, bf16[8,19,16,128]{3,2,1,0:T(8,128)(2,1)S(1)}, u32[]{:S(2)}) copy-start(bf16[8,19,16,128]{3,2,1,0:T(8,128)(2,1)S(1)} %pad_maximum_fusion.2.refs_0_.refs_8_) | copy-start | bytes 1867780
  44.6 15.3 %collective-permute-start.13 = (bf16[2,36,16,128]{3,2,1,0:T(8,128)(2,1)S(1)}, bf16[2,36,16,128]{3,2,1,0:T(8,128)(2,1)S(1)}, u32[]{:S(2)}, u32[]{:S(2)}) collective-permute-start(bf16[2,36,16,128]{3,2,1,0:T(8,128)(2,1)S(1)} %copy-done.47), channel_id=1, source_target_pairs={{0,4},{1,5},{2,6},{3,7},{4,0},{5,1},{6,2},{7,3},{8,12},{9,13},{10,... | collective-permute-start | bytes 884744 | tf_op jit(solution)/shard_map/ppermute | solution.py:1444
  46.1 14.0 %collective-permute-start.11 = (bf16[8,19,16,128]{3,2,1,0:T(8,128)(2,1)S(1)}, bf16[8,19,16,128]{3,2,1,0:T(8,128)(2,1)S(1)}, u32[]{:S(2)}, u32[]{:S(2)}) collective-permute-start(bf16[8,19,16,128]{3,2,1,0:T(8,128)(2,1)S(1)} %pad_maximum_fusion.2.refs_0_.refs_8_), channel_id=1, source_target_pairs={{0,8},{1,9},{2,10},{3,11},{4,12},{5,13},{6,14},{7,15},{8,0},{9,1},... | collective-permute-start | bytes 1867784 | tf_op jit(solution)/shard_map/ppermute | solution.py:1444
  46.1 16.4 %collective-permute-start.9 = (bf16[8,19,16,128]{3,2,1,0:T(8,128)(2,1)S(1)}, bf16[8,19,16,128]{3,2,1,0:T(8,128)(2,1)S(1)}, u32[]{:S(2)}, u32[]{:S(2)}) collective-permute-start(bf16[8,19,16,128]{3,2,1,0:T(8,128)(2,1)S(1)} %pad_maximum_fusion.2.refs_0_.refs_8_), channel_id=1, source_target_pairs={{0,1},{1,0},{2,3},{3,2},{4,5},{5,4},{6,7},{7,6},{8,9},{9,8},{10,11... | collective-permute-start | bytes 1867784 | tf_op jit(solution)/shard_map/ppermute | solution.py:1444
  46.1 16.4 %collective-permute-start.12 = (bf16[8,19,16,128]{3,2,1,0:T(8,128)(2,1)S(1)}, bf16[8,19,16,128]{3,2,1,0:T(8,128)(2,1)S(1)}, u32[]{:S(2)}, u32[]{:S(2)}) collective-permute-start(bf16[8,19,16,128]{3,2,1,0:T(8,128)(2,1)S(1)} %pad_maximum_fusion.3.refs_4_.refs_12_), channel_id=1, source_target_pairs={{0,8},{1,9},{2,10},{3,11},{4,12},{5,13},{6,14},{7,15},{8,0},{9,1},... | collective-permute-start | bytes 1867784 | tf_op jit(solution)/shard_map/ppermute | solution.py:1444
  46.6 17.3 %collective-permute-start.10 = (bf16[8,19,16,128]{3,2,1,0:T(8,128)(2,1)S(1)}, bf16[8,19,16,128]{3,2,1,0:T(8,128)(2,1)S(1)}, u32[]{:S(2)}, u32[]{:S(2)}) collective-permute-start(bf16[8,19,16,128]{3,2,1,0:T(8,128)(2,1)S(1)} %pad_maximum_fusion.3.refs_4_.refs_12_), channel_id=1, source_target_pairs={{0,16},{1,17},{2,18},{3,19},{4,20},{5,21},{6,22},{7,23},{8,24},{9,... | collective-permute-start | bytes 1867784 | tf_op jit(solution)/shard_map/ppermute | solution.py:1444
  63.9 2.1 collective-permute-start.14
  63.9 2.9 collective-permute-start.15
  66.9 15.5 %collective-permute-start.16 = (bf16[4,36,16,128]{3,2,1,0:T(8,128)(2,1)S(1)}, bf16[4,36,16,128]{3,2,1,0:T(8,128)(2,1)}, u32[]{:S(2)}, u32[]{:S(2)}) collective-permute-start(bf16[4,36,16,128]{3,2,1,0:T(8,128)(2,1)S(1)} %pad_maximum_fusion.4), channel_id=1, source_target_pairs={{0,16},{1,17},{2,18},{3,19},{4,20},{5,21},{6,22},{7,23},{8,24},{9,... | collective-permute-start | bytes 1769480 | tf_op jit(solution)/shard_map/ppermute | solution.py:1444
  68.6 15.1 %collective-permute-start.17 = (bf16[4,36,16,128]{3,2,1,0:T(8,128)(2,1)S(1)}, bf16[4,36,16,128]{3,2,1,0:T(8,128)(2,1)S(1)}, u32[]{:S(2)}, u32[]{:S(2)}) collective-permute-start(bf16[4,36,16,128]{3,2,1,0:T(8,128)(2,1)S(1)} %pad_maximum_fusion.5), channel_id=1, source_target_pairs={{0,1},{1,0},{2,3},{3,2},{4,5},{5,4},{6,7},{7,6},{8,9},{9,8},{10,11... | collective-permute-start | bytes 1769480 | tf_op jit(solution)/shard_map/ppermute | solution.py:1444
  83.8 71.7 %copy-start.2 = (bf16[8,36,16,128]{3,2,1,0:T(8,128)(2,1)}, bf16[8,36,16,128]{3,2,1,0:T(8,128)(2,1)S(1)}, u32[]{:S(2)}) copy-start(bf16[8,36,16,128]{3,2,1,0:T(8,128)(2,1)S(1)} %pad_maximum_fusion.1.refs_4_) | copy-start | bytes 3538948
  83.8 19.8 %collective-permute-start.20 = (bf16[8,36,16,128]{3,2,1,0:T(8,128)(2,1)S(1)}, bf16[8,36,16,128]{3,2,1,0:T(8,128)(2,1)S(1)}, u32[]{:S(2)}, u32[]{:S(2)}) collective-permute-start(bf16[8,36,16,128]{3,2,1,0:T(8,128)(2,1)S(1)} %pad_maximum_fusion.refs_0_), channel_id=1, source_target_pairs={{0,8},{1,9},{2,10},{3,11},{4,12},{5,13},{6,14},{7,15},{8,0},{9,1},... | collective-permute-start | bytes 3538952 | tf_op jit(solution)/shard_map/ppermute | solution.py:1444
  83.9 28.4 %collective-permute-start.18 = (bf16[8,36,16,128]{3,2,1,0:T(8,128)(2,1)S(1)}, bf16[8,36,16,128]{3,2,1,0:T(8,128)(2,1)S(1)}, u32[]{:S(2)}, u32[]{:S(2)}) collective-permute-start(bf16[8,36,16,128]{3,2,1,0:T(8,128)(2,1)S(1)} %pad_maximum_fusion.refs_0_), channel_id=1, source_target_pairs={{0,1},{1,0},{2,3},{3,2},{4,5},{5,4},{6,7},{7,6},{8,9},{9,8},{10,11... | collective-permute-start | bytes 3538952 | tf_op jit(solution)/shard_map/ppermute | solution.py:1444
  84.4 27.9 %collective-permute-start.21 = (bf16[8,36,16,128]{3,2,1,0:T(8,128)(2,1)S(1)}, bf16[8,36,16,128]{3,2,1,0:T(8,128)(2,1)S(1)}, u32[]{:S(2)}, u32[]{:S(2)}) collective-permute-start(bf16[8,36,16,128]{3,2,1,0:T(8,128)(2,1)S(1)} %pad_maximum_fusion.1.refs_4_), channel_id=1, source_target_pairs={{0,8},{1,9},{2,10},{3,11},{4,12},{5,13},{6,14},{7,15},{8,0},{9,1},... | collective-permute-start | bytes 3538952 | tf_op jit(solution)/shard_map/ppermute | solution.py:1444
  84.6 28.3 %collective-permute-start.19 = (bf16[8,36,16,128]{3,2,1,0:T(8,128)(2,1)S(1)}, bf16[8,36,16,128]{3,2,1,0:T(8,128)(2,1)}, u32[]{:S(2)}, u32[]{:S(2)}) collective-permute-start(bf16[8,36,16,128]{3,2,1,0:T(8,128)(2,1)S(1)} %pad_maximum_fusion.1.refs_4_), channel_id=1, source_target_pairs={{0,16},{1,17},{2,18},{3,19},{4,20},{5,21},{6,22},{7,23},{8,24},{9,... | collective-permute-start | bytes 3538952 | tf_op jit(solution)/shard_map/ppermute | solution.py:1444
  86.0 31.7 %copy-start.30 = (f32[88,128]{1,0:T(8,128)S(1)}, f32[88,128]{1,0:T(8,128)}, u32[]{:S(2)}) copy-start(f32[88,128]{1,0:T(8,128)} %get-tuple-element.180.small) | copy-start | bytes 135172
  103.6 51.9 %copy-start.8 = (bf16[8,36,16,128]{3,2,1,0:T(8,128)(2,1)}, bf16[8,36,16,128]{3,2,1,0:T(8,128)(2,1)S(1)}, u32[]{:S(2)}) copy-start(bf16[8,36,16,128]{3,2,1,0:T(8,128)(2,1)S(1)} %collective-permute-done.20.refs_2_) | copy-start | bytes 3538948
  112.3 43.2 %copy-start.10 = (bf16[8,36,16,128]{3,2,1,0:T(8,128)(2,1)}, bf16[8,36,16,128]{3,2,1,0:T(8,128)(2,1)S(1)}, u32[]{:S(2)}) copy-start(bf16[8,36,16,128]{3,2,1,0:T(8,128)(2,1)S(1)} %collective-permute-done.18.refs_1_) | copy-start | bytes 3538948
  112.3 43.2 %copy-start.12 = (bf16[8,36,16,128]{3,2,1,0:T(8,128)(2,1)}, bf16[8,36,16,128]{3,2,1,0:T(8,128)(2,1)S(1)}, u32[]{:S(2)}) copy-start(bf16[8,36,16,128]{3,2,1,0:T(8,128)(2,1)S(1)} %collective-permute-done.21.refs_6_) | copy-start | bytes 3538948
  112.9 4.5 %collective-permute-start.22 = (bf16[8,36,16,128]{3,2,1,0:T(8,128)(2,1)S(1)}, bf16[8,36,16,128]{3,2,1,0:T(8,128)(2,1)S(1)}, u32[]{:S(2)}, u32[]{:S(2)}) collective-permute-start(bf16[8,36,16,128]{3,2,1,0:T(8,128)(2,1)S(1)} %collective-permute-done.18.refs_1_), channel_id=1, source_target_pairs={{0,8},{1,9},{2,10},{3,11},{4,12},{5,13},{6,14},{7,15},{8,0},{9,1},... | collective-permute-start | bytes 3538952 | tf_op jit(solution)/shard_map/ppermute | solution.py:1444
  112.9 4.7 %collective-permute-start.23 = (bf16[8,36,16,128]{3,2,1,0:T(8,128)(2,1)}, bf16[8,36,16,128]{3,2,1,0:T(8,128)(2,1)S(1)}, u32[]{:S(2)}, u32[]{:S(2)}) collective-permute-start(bf16[8,36,16,128]{3,2,1,0:T(8,128)(2,1)} %collective-permute-done.19.refs_5_), channel_id=1, source_target_pairs={{0,8},{1,9},{2,10},{3,11},{4,12},{5,13},{6,14},{7,15},{8,0},{9,1},... | collective-permute-start | bytes 3538952 | tf_op jit(solution)/shard_map/ppermute | solution.py:1444
  117.4 37.5 %copy-start.13 = (bf16[8,36,16,128]{3,2,1,0:T(8,128)(2,1)}, bf16[8,36,16,128]{3,2,1,0:T(8,128)(2,1)S(1)}, u32[]{:S(2)}) copy-start(bf16[8,36,16,128]{3,2,1,0:T(8,128)(2,1)S(1)} %collective-permute-done.22.refs_3_) | copy-start | bytes 3538948
  117.7 37.3 %copy-start.15 = (bf16[8,36,16,128]{3,2,1,0:T(8,128)(2,1)}, bf16[8,36,16,128]{3,2,1,0:T(8,128)(2,1)S(1)}, u32[]{:S(2)}) copy-start(bf16[8,36,16,128]{3,2,1,0:T(8,128)(2,1)S(1)} %collective-permute-done.23.refs_7_) | copy-start | bytes 3538948
  119.7 35.9 %copy-start = (bf16[1024,768]{1,0:T(8,128)(2,1)S(1)}, bf16[1024,768]{1,0:T(8,128)(2,1)}, u32[]{:S(2)}) copy-start(bf16[1024,768]{1,0:T(8,128)(2,1)} %cot_in.3) | copy-start | bytes 4718596
  119.7 35.9 %copy-start.1 = (f32[1024,768]{1,0:T(8,128)S(1)}, f32[1024,768]{1,0:T(8,128)}, u32[]{:S(2)}) copy-start(f32[1024,768]{1,0:T(8,128)} %get-tuple-element.191.x1_in) | copy-start | bytes 9437188
  154.9 16.9 %collective-permute-start.24 = (bf16[16,36,16,128]{3,2,1,0:T(8,128)(2,1)}, bf16[16,36,16,128]{3,2,1,0:T(8,128)(2,1)S(1)}, u32[]{:S(2)}, u32[]{:S(2)}) collective-permute-start(bf16[16,36,16,128]{3,2,1,0:T(8,128)(2,1)} %get-tuple-element.195), channel_id=1, source_target_pairs={{0,8},{1,9},{2,10},{3,11},{4,12},{5,13},{6,14},{7,15},{8,0},{9,1},... | collective-permute-start | bytes 7077896 | tf_op jit(solution)/shard_map/ppermute | solution.py:1444
  155.1 16.7 %collective-permute-start.25 = (bf16[16,36,16,128]{3,2,1,0:T(8,128)(2,1)}, bf16[16,36,16,128]{3,2,1,0:T(8,128)(2,1)S(1)}, u32[]{:S(2)}, u32[]{:S(2)}) collective-permute-start(bf16[16,36,16,128]{3,2,1,0:T(8,128)(2,1)} %get-tuple-element.196), channel_id=1, source_target_pairs={{0,8},{1,9},{2,10},{3,11},{4,12},{5,13},{6,14},{7,15},{8,0},{9,1},... | collective-permute-start | bytes 7077896 | tf_op jit(solution)/shard_map/ppermute | solution.py:1444
  174.0 35.5 %collective-permute-start.26 = (bf16[8,36,16,128]{3,2,1,0:T(8,128)(2,1)}, bf16[8,36,16,128]{3,2,1,0:T(8,128)(2,1)}, u32[]{:S(2)}, u32[]{:S(2)}) collective-permute-start(bf16[8,36,16,128]{3,2,1,0:T(8,128)(2,1)} %add_convert_fusion.1), channel_id=1, source_target_pairs={{0,1},{1,0},{2,3},{3,2},{4,5},{5,4},{6,7},{7,6},{8,9},{9,8},{10,11... | collective-permute-start | bytes 3538952 | tf_op jit(solution)/shard_map/ppermute | solution.py:1444
  175.7 33.9 %collective-permute-start.27 = (bf16[8,36,16,128]{3,2,1,0:T(8,128)(2,1)S(1)}, bf16[8,36,16,128]{3,2,1,0:T(8,128)(2,1)}, u32[]{:S(2)}, u32[]{:S(2)}) collective-permute-start(bf16[8,36,16,128]{3,2,1,0:T(8,128)(2,1)S(1)} %add_convert_fusion), channel_id=1, source_target_pairs={{0,16},{1,17},{2,18},{3,19},{4,20},{5,21},{6,22},{7,23},{8,24},{9,... | collective-permute-start | bytes 3538952 | tf_op jit(solution)/shard_map/ppermute | solution.py:1444
  212.7 14.9 %collective-permute-start.28 = (bf16[4,36,16,128]{3,2,1,0:T(8,128)(2,1)S(1)}, bf16[4,36,16,128]{3,2,1,0:T(8,128)(2,1)S(1)}, u32[]{:S(2)}, u32[]{:S(2)}) collective-permute-start(bf16[4,36,16,128]{3,2,1,0:T(8,128)(2,1)S(1)} %add_convert_fusion.3), channel_id=1, source_target_pairs={{0,16},{1,17},{2,18},{3,19},{4,20},{5,21},{6,22},{7,23},{8,24},{9,... | collective-permute-start | bytes 1769480 | tf_op jit(solution)/shard_map/ppermute | solution.py:1444
  212.7 15.7 %collective-permute-start.29 = (bf16[4,36,16,128]{3,2,1,0:T(8,128)(2,1)S(1)}, bf16[4,36,16,128]{3,2,1,0:T(8,128)(2,1)S(1)}, u32[]{:S(2)}, u32[]{:S(2)}) collective-permute-start(bf16[4,36,16,128]{3,2,1,0:T(8,128)(2,1)S(1)} %add_convert_fusion.2), channel_id=1, source_target_pairs={{0,1},{1,0},{2,3},{3,2},{4,5},{5,4},{6,7},{7,6},{8,9},{9,8},{10,11... | collective-permute-start | bytes 1769480 | tf_op jit(solution)/shard_map/ppermute | solution.py:1444
  215.2 13.2 %collective-permute-start.30 = (bf16[16,9,16,128]{3,2,1,0:T(8,128)(2,1)S(1)}, bf16[16,9,16,128]{3,2,1,0:T(8,128)(2,1)S(1)}, u32[]{:S(2)}, u32[]{:S(2)}) collective-permute-start(bf16[16,9,16,128]{3,2,1,0:T(8,128)(2,1)S(1)} %get-tuple-element.226), channel_id=1, source_target_pairs={{0,8},{1,9},{2,10},{3,11},{4,12},{5,13},{6,14},{7,15},{8,0},{9,1},... | collective-permute-start | bytes 1769480 | tf_op jit(solution)/shard_map/ppermute | solution.py:1444
  215.2 13.2 %collective-permute-start.31 = (bf16[16,9,16,128]{3,2,1,0:T(8,128)(2,1)S(1)}, bf16[16,9,16,128]{3,2,1,0:T(8,128)(2,1)S(1)}, u32[]{:S(2)}, u32[]{:S(2)}) collective-permute-start(bf16[16,9,16,128]{3,2,1,0:T(8,128)(2,1)S(1)} %get-tuple-element.227), channel_id=1, source_target_pairs={{0,8},{1,9},{2,10},{3,11},{4,12},{5,13},{6,14},{7,15},{8,0},{9,1},... | collective-permute-start | bytes 1769480 | tf_op jit(solution)/shard_map/ppermute | solution.py:1444
  231.7 17.2 %collective-permute-start.32 = (bf16[8,9,16,128]{3,2,1,0:T(8,128)(2,1)S(1)}, bf16[8,9,16,128]{3,2,1,0:T(8,128)(2,1)S(1)}, u32[]{:S(2)}, u32[]{:S(2)}) collective-permute-start(bf16[8,9,16,128]{3,2,1,0:T(8,128)(2,1)S(1)} %add_convert_fusion.7), channel_id=1, source_target_pairs={{0,1},{1,0},{2,3},{3,2},{4,5},{5,4},{6,7},{7,6},{8,9},{9,8},{10,11... | collective-permute-start | bytes 884744 | tf_op jit(solution)/shard_map/ppermute | solution.py:1444
  233.5 15.4 %collective-permute-start.33 = (bf16[8,9,16,128]{3,2,1,0:T(8,128)(2,1)S(1)}, bf16[8,9,16,128]{3,2,1,0:T(8,128)(2,1)S(1)}, u32[]{:S(2)}, u32[]{:S(2)}) collective-permute-start(bf16[8,9,16,128]{3,2,1,0:T(8,128)(2,1)S(1)} %add_convert_fusion.6), channel_id=1, source_target_pairs={{0,16},{1,17},{2,18},{3,19},{4,20},{5,21},{6,22},{7,23},{8,24},{9,... | collective-permute-start | bytes 884744 | tf_op jit(solution)/shard_map/ppermute | solution.py:1444
  233.8 15.1 %collective-permute-start.34 = (bf16[2,36,16,128]{3,2,1,0:T(8,128)(2,1)S(1)}, bf16[2,36,16,128]{3,2,1,0:T(8,128)(2,1)S(1)}, u32[]{:S(2)}, u32[]{:S(2)}) collective-permute-start(bf16[2,36,16,128]{3,2,1,0:T(8,128)(2,1)S(1)} %pad_maximum_fusion.8), channel_id=1, source_target_pairs={{0,2},{1,3},{2,0},{3,1},{4,6},{5,7},{6,4},{7,5},{8,10},{9,11},{10,... | collective-permute-start | bytes 884744 | tf_op jit(solution)/shard_map/ppermute | solution.py:1444
  235.3 14.7 %collective-permute-start.35 = (bf16[2,36,16,128]{3,2,1,0:T(8,128)(2,1)S(1)}, bf16[2,36,16,128]{3,2,1,0:T(8,128)(2,1)S(1)}, u32[]{:S(2)}, u32[]{:S(2)}) collective-permute-start(bf16[2,36,16,128]{3,2,1,0:T(8,128)(2,1)S(1)} %pad_maximum_fusion.9), channel_id=1, source_target_pairs={{0,4},{1,5},{2,6},{3,7},{4,0},{5,1},{6,2},{7,3},{8,12},{9,13},{10,... | collective-permute-start | bytes 884744 | tf_op jit(solution)/shard_map/ppermute | solution.py:1444
  250.1 5.2 %collective-permute-start.36 = (bf16[4,9,16,128]{3,2,1,0:T(8,128)(2,1)S(1)}, bf16[4,9,16,128]{3,2,1,0:T(8,128)(2,1)S(1)}, u32[]{:S(2)}, u32[]{:S(2)}) collective-permute-start(bf16[4,9,16,128]{3,2,1,0:T(8,128)(2,1)S(1)} %add_convert_fusion.11), channel_id=1, source_target_pairs={{0,16},{1,17},{2,18},{3,19},{4,20},{5,21},{6,22},{7,23},{8,24},{9,... | collective-permute-start | bytes 442376 | tf_op jit(solution)/shard_map/ppermute | solution.py:1444
  251.5 7.1 %collective-permute-start.40 = (bf16[36,16,128]{2,1,0:T(8,128)(2,1)S(1)}, bf16[36,16,128]{2,1,0:T(8,128)(2,1)S(1)}, u32[]{:S(2)}, u32[]{:S(2)}) collective-permute-start(bf16[36,16,128]{2,1,0:T(8,128)(2,1)S(1)} %slice_bitcast_fusion.1), channel_id=1, source_target_pairs={{0,6},{1,7},{2,4},{3,5},{4,2},{5,3},{6,0},{7,1},{8,14},{9,15},{10,... | collective-permute-start | bytes 442376 | tf_op jit(solution)/shard_map/ppermute | solution.py:1444
  253.1 5.1 %collective-permute-start.37 = (bf16[4,9,16,128]{3,2,1,0:T(8,128)(2,1)S(1)}, bf16[4,9,16,128]{3,2,1,0:T(8,128)(2,1)S(1)}, u32[]{:S(2)}, u32[]{:S(2)}) collective-permute-start(bf16[4,9,16,128]{3,2,1,0:T(8,128)(2,1)S(1)} %add_convert_fusion.10), channel_id=1, source_target_pairs={{0,1},{1,0},{2,3},{3,2},{4,5},{5,4},{6,7},{7,6},{8,9},{9,8},{10,11... | collective-permute-start | bytes 442376 | tf_op jit(solution)/shard_map/ppermute | solution.py:1444
  253.5 4.9 %collective-permute-start.38 = (bf16[16,10,16,128]{3,2,1,0:T(8,128)(2,1)S(1)}, bf16[16,10,16,128]{3,2,1,0:T(8,128)(2,1)S(1)}, u32[]{:S(2)}, u32[]{:S(2)}) collective-permute-start(bf16[16,10,16,128]{3,2,1,0:T(8,128)(2,1)S(1)} %get-tuple-element.258), channel_id=1, source_target_pairs={{0,8},{1,9},{2,10},{3,11},{4,12},{5,13},{6,14},{7,15},{8,0},{9,1},... | collective-permute-start | bytes 1966088 | tf_op jit(solution)/shard_map/ppermute | solution.py:1444
  253.5 5.0 %collective-permute-start.39 = (bf16[16,10,16,128]{3,2,1,0:T(8,128)(2,1)S(1)}, bf16[16,10,16,128]{3,2,1,0:T(8,128)(2,1)S(1)}, u32[]{:S(2)}, u32[]{:S(2)}) collective-permute-start(bf16[16,10,16,128]{3,2,1,0:T(8,128)(2,1)S(1)} %get-tuple-element.260), channel_id=1, source_target_pairs={{0,8},{1,9},{2,10},{3,11},{4,12},{5,13},{6,14},{7,15},{8,0},{9,1},... | collective-permute-start | bytes 1966088 | tf_op jit(solution)/shard_map/ppermute | solution.py:1444
  258.6 7.8 %collective-permute-start.41 = (bf16[8,10,16,128]{3,2,1,0:T(8,128)(2,1)S(1)}, bf16[8,10,16,128]{3,2,1,0:T(8,128)(2,1)S(1)}, u32[]{:S(2)}, u32[]{:S(2)}) collective-permute-start(bf16[8,10,16,128]{3,2,1,0:T(8,128)(2,1)S(1)} %add_convert_fusion.5), channel_id=1, source_target_pairs={{0,1},{1,0},{2,3},{3,2},{4,5},{5,4},{6,7},{7,6},{8,9},{9,8},{10,11... | collective-permute-start | bytes 983048 | tf_op jit(solution)/shard_map/ppermute | solution.py:1444
  259.1 8.7 %collective-permute-start.42 = (bf16[8,10,16,128]{3,2,1,0:T(8,128)(2,1)S(1)}, bf16[8,10,16,128]{3,2,1,0:T(8,128)(2,1)S(1)}, u32[]{:S(2)}, u32[]{:S(2)}) collective-permute-start(bf16[8,10,16,128]{3,2,1,0:T(8,128)(2,1)S(1)} %add_convert_fusion.4), channel_id=1, source_target_pairs={{0,16},{1,17},{2,18},{3,19},{4,20},{5,21},{6,22},{7,23},{8,24},{9,... | collective-permute-start | bytes 983048 | tf_op jit(solution)/shard_map/ppermute | solution.py:1444
  259.9 8.0 %collective-permute-start.43 = (bf16[2,9,16,128]{3,2,1,0:T(8,128)(2,1)S(1)}, bf16[2,9,16,128]{3,2,1,0:T(8,128)(2,1)S(1)}, u32[]{:S(2)}, u32[]{:S(2)}) collective-permute-start(bf16[2,9,16,128]{3,2,1,0:T(8,128)(2,1)S(1)} %pad_maximum_fusion.14), channel_id=1, source_target_pairs={{0,2},{1,3},{2,0},{3,1},{4,6},{5,7},{6,4},{7,5},{8,10},{9,11},{10,... | collective-permute-start | bytes 221192 | tf_op jit(solution)/shard_map/ppermute | solution.py:1444
  259.9 8.0 %collective-permute-start.44 = (bf16[2,9,16,128]{3,2,1,0:T(8,128)(2,1)S(1)}, bf16[2,9,16,128]{3,2,1,0:T(8,128)(2,1)S(1)}, u32[]{:S(2)}, u32[]{:S(2)}) collective-permute-start(bf16[2,9,16,128]{3,2,1,0:T(8,128)(2,1)S(1)} %pad_maximum_fusion.15), channel_id=1, source_target_pairs={{0,4},{1,5},{2,6},{3,7},{4,0},{5,1},{6,2},{7,3},{8,12},{9,13},{10,... | collective-permute-start | bytes 221192 | tf_op jit(solution)/shard_map/ppermute | solution.py:1444
  262.6 6.2 %collective-permute-start.45 = (bf16[2,9,16,128]{3,2,1,0:T(8,128)(2,1)S(1)}, bf16[2,9,16,128]{3,2,1,0:T(8,128)(2,1)S(1)}, u32[]{:S(2)}, u32[]{:S(2)}) collective-permute-start(bf16[2,9,16,128]{3,2,1,0:T(8,128)(2,1)S(1)} %pad_maximum_fusion.16), channel_id=1, source_target_pairs={{0,6},{1,7},{2,4},{3,5},{4,2},{5,3},{6,0},{7,1},{8,14},{9,15},{10,... | collective-permute-start | bytes 221192 | tf_op jit(solution)/shard_map/ppermute | solution.py:1444
  268.7 7.0 %collective-permute-start.46 = (bf16[36,16,128]{2,1,0:T(8,128)(2,1)S(1)}, bf16[36,16,128]{2,1,0:T(8,128)(2,1)S(1)}, u32[]{:S(2)}, u32[]{:S(2)}) collective-permute-start(bf16[36,16,128]{2,1,0:T(8,128)(2,1)S(1)} %slice_bitcast_fusion), channel_id=1, source_target_pairs={{0,6},{1,7},{2,4},{3,5},{4,2},{5,3},{6,0},{7,1},{8,14},{9,15},{10,... | collective-permute-start | bytes 442376 | tf_op jit(solution)/shard_map/ppermute | solution.py:1444
  270.6 6.1 %collective-permute-start.47 = (bf16[4,10,16,128]{3,2,1,0:T(8,128)(2,1)S(1)}, bf16[4,10,16,128]{3,2,1,0:T(8,128)(2,1)S(1)}, u32[]{:S(2)}, u32[]{:S(2)}) collective-permute-start(bf16[4,10,16,128]{3,2,1,0:T(8,128)(2,1)S(1)} %add_convert_fusion.9), channel_id=1, source_target_pairs={{0,16},{1,17},{2,18},{3,19},{4,20},{5,21},{6,22},{7,23},{8,24},{9,... | collective-permute-start | bytes 491528 | tf_op jit(solution)/shard_map/ppermute | solution.py:1444
  271.9 5.3 %collective-permute-start.48 = (bf16[4,10,16,128]{3,2,1,0:T(8,128)(2,1)S(1)}, bf16[4,10,16,128]{3,2,1,0:T(8,128)(2,1)S(1)}, u32[]{:S(2)}, u32[]{:S(2)}) collective-permute-start(bf16[4,10,16,128]{3,2,1,0:T(8,128)(2,1)S(1)} %add_convert_fusion.8), channel_id=1, source_target_pairs={{0,1},{1,0},{2,3},{3,2},{4,5},{5,4},{6,7},{7,6},{8,9},{9,8},{10,11... | collective-permute-start | bytes 491528 | tf_op jit(solution)/shard_map/ppermute | solution.py:1444
  277.3 4.5 %collective-permute-start.49 = (bf16[2,10,16,128]{3,2,1,0:T(8,128)(2,1)S(1)}, bf16[2,10,16,128]{3,2,1,0:T(8,128)(2,1)S(1)}, u32[]{:S(2)}, u32[]{:S(2)}) collective-permute-start(bf16[2,10,16,128]{3,2,1,0:T(8,128)(2,1)S(1)} %pad_maximum_fusion.11), channel_id=1, source_target_pairs={{0,2},{1,3},{2,0},{3,1},{4,6},{5,7},{6,4},{7,5},{8,10},{9,11},{10,... | collective-permute-start | bytes 245768 | tf_op jit(solution)/shard_map/ppermute | solution.py:1444
  278.0 5.4 %collective-permute-start.50 = (bf16[2,10,16,128]{3,2,1,0:T(8,128)(2,1)S(1)}, bf16[2,10,16,128]{3,2,1,0:T(8,128)(2,1)S(1)}, u32[]{:S(2)}, u32[]{:S(2)}) collective-permute-start(bf16[2,10,16,128]{3,2,1,0:T(8,128)(2,1)S(1)} %pad_maximum_fusion.12), channel_id=1, source_target_pairs={{0,4},{1,5},{2,6},{3,7},{4,0},{5,1},{6,2},{7,3},{8,12},{9,13},{10,... | collective-permute-start | bytes 245768 | tf_op jit(solution)/shard_map/ppermute | solution.py:1444
  280.4 6.2 %collective-permute-start.51 = (bf16[2,10,16,128]{3,2,1,0:T(8,128)(2,1)S(1)}, bf16[2,10,16,128]{3,2,1,0:T(8,128)(2,1)S(1)}, u32[]{:S(2)}, u32[]{:S(2)}) collective-permute-start(bf16[2,10,16,128]{3,2,1,0:T(8,128)(2,1)S(1)} %pad_maximum_fusion.13), channel_id=1, source_target_pairs={{0,6},{1,7},{2,4},{3,5},{4,2},{5,3},{6,0},{7,1},{8,14},{9,15},{10,... | collective-permute-start | bytes 245768 | tf_op jit(solution)/shard_map/ppermute | solution.py:1444
  289.8 11.0 %collective-permute-start.53 = (f32[128,128]{1,0:T(8,128)}, f32[128,128]{1,0:T(8,128)S(1)}, u32[]{:S(2)}, u32[]{:S(2)}) collective-permute-start(f32[128,128]{1,0:T(8,128)} %get-tuple-element.284), channel_id=1, source_target_pairs={{7,6},{8,7},{9,8},{10,9},{11,10},{12,11},{13,12},{14,13},{15,14},{... | collective-permute-start | bytes 196616 | tf_op jit(solution)/shard_map/ppermute | solution.py:1759
  291.7 9.1 %collective-permute-start.52 = (f32[72,128]{1,0:T(8,128)}, f32[72,128]{1,0:T(8,128)S(1)}, u32[]{:S(2)}, u32[]{:S(2)}) collective-permute-start(f32[72,128]{1,0:T(8,128)} %get-tuple-element.283), channel_id=1, source_target_pairs={{0,1},{1,2},{2,3},{3,4},{4,5},{15,16},{16,17}} | collective-permute-start | bytes 110600 | tf_op jit(solution)/shard_map/ppermute | solution.py:1758
  (47 other events, 339.2 us)

commit v4 on v3

--- a/solution.py
+++ b/solution.py
@@ -1020,7 +1020,7 @@
             dma(6),
             pltpu.SemaphoreType.DMA((4, rows // TALL)),
         ],
-        compiler_params=pltpu.CompilerParams(vmem_limit_bytes=32 * MEGA),
+        compiler_params=pltpu.CompilerParams(vmem_limit_bytes=46 * MEGA),
         cost_estimate=cost(2 * rows * width * FF, 20 * MEGA),
         name="feed_forward_out",
     )(me, u, x1, cot, small, *mlp)

time: 307 us -> 303 us (0.987)
  local copies, waits for them, and re-layouts: 12.6 us -> 6.87 us
  Pallas kernels: 135 us -> 131 us
  waiting for transfers between devices: 76.5 us -> 80.4 us
  other arithmetic: 15 us -> 18.2 us
    unnamed x114 -> x100, local copies, waits for them, and re-layouts: 11 us -> 5.18 us
    ppermute x50, waiting for transfers between devices: 70.7 us -> 74.6 us  [exchange(): return lax.ppermute(values, AXES, [(d, d ^ bit) for d in range(BLOCKS)])]
    convert_element_type x12, other arithmetic: 4.98 us -> 8.89 us  [sent(): return sum_terms([t[t.shape[0] // 2:] for t in terms]).astype(BF16)]
  transfers between devices with their start and end apart: 54 -> 54, of which waited for: 32 -> 31; matrix products, arithmetic and copies ran while one was open for 2% -> 2% of each run, Pallas kernels for 31% -> 30%
where the time goes in v4:
time: 303 us; the launch traced here: 300 us
  Pallas kernels  131 us (43%)
  waiting for transfers between devices  80.4 us (27%)
  starting transfers between devices  60.4 us (20%)
  other arithmetic  18.2 us (6%)
  local copies, waits for them, and re-layouts  6.87 us (2%)
    ppermute x50, waiting for transfers between devices, exchange(): return lax.ppermute(values, AXES, [(d, d ^ bit) for d in range(BLOCKS)])  74.6 us
    ppermute x50, starting transfers between devices, exchange(): return lax.ppermute(values, AXES, [(d, d ^ bit) for d in range(BLOCKS)])  45.4 us
    pallas_call x1, Pallas kernels, feed_forward(): pl.pallas_call(mlp_kernel, out_shape=(shape((rows, FF), BF16), shape((row...  35.3 us
    pallas_call x2, Pallas kernels, attend_back(): pl.pallas_call(partial(attend_back_kernel, group), out_shape=shape((rows,...  20.4 us
    pallas_call x1, Pallas kernels, attend(): pl.pallas_call(attend_kernel, out_shape=(shape((rows, width), BF16), shap...  16.2 us
    pallas_call x1, Pallas kernels, split(): pl.pallas_call(split_kernel, out_shape=(shape((rows, width), F32), shape(...  16.1 us
    pallas_call x1, Pallas kernels, qkv_back(): pl.pallas_call(qkv_back_kernel, out_shape=(shape((rows, width), F32), hal...  13 us
    pallas_call x1, Pallas kernels, project_qkv(): pl.pallas_call(qkv_kernel, out_shape=(shape((rows, width), BF16), shape((...  10.1 us
  transfers between devices with their start and end apart: 54, of which 31 were waited for; matrix products, arithmetic and copies ran while one was open for 2% of the time, Pallas kernels for 30%

profile of v4, /device:TPU:2, one launch (start us, length us, event | category | flops | bytes accessed | tf_op | source)
XLA Modules:
  0.0 299.5 jit_solution(6562363427446679023)
XLA Ops:
  0.6 1.2 convert.64
  1.9 3.4 %collective-permute-start = (bf16[128,128]{1,0:T(8,128)(2,1)S(1)}, bf16[128,128]{1,0:T(8,128)(2,1)S(1)}, u32[]{:S(2)}, u32[]{:S(2)}) collective-permute-start(bf16[128,128]{1,0:T(8,128)(2,1)S(1)} %pad_maximum_fusion.17), channel_id=1, source_target_pairs={{6,7},{7,8},{8,9},{9,10},{10,11},{11,12},{12,13},{13,14},{14,15},{... | collective-permute-start | bytes 98312 | tf_op jit(solution)/shard_map/ppermute | solution.py:1670
  5.4 5.7 %collective-permute-start.1 = (bf16[72,128]{1,0:T(8,128)(2,1)S(1)}, bf16[72,128]{1,0:T(8,128)(2,1)S(1)}, u32[]{:S(2)}, u32[]{:S(2)}) collective-permute-start(bf16[72,128]{1,0:T(8,128)(2,1)S(1)} %pad_maximum_fusion.19), channel_id=1, source_target_pairs={{1,0},{2,1},{3,2},{4,3},{5,4},{16,15},{17,16}} | collective-permute-start | bytes 55304 | tf_op jit(solution)/shard_map/ppermute | solution.py:1669
  13.2 2.1 pack.1
  15.4 4.3 %collective-permute-start.2 = (bf16[2,19,16,128]{3,2,1,0:T(8,128)(2,1)}, bf16[2,19,16,128]{3,2,1,0:T(8,128)(2,1)S(1)}, u32[]{:S(2)}, u32[]{:S(2)}) collective-permute-start(bf16[2,19,16,128]{3,2,1,0:T(8,128)(2,1)} %get-tuple-element.144), channel_id=1, source_target_pairs={{0,2},{1,3},{2,0},{3,1},{4,6},{5,7},{6,4},{7,5},{8,10},{9,11},{10,... | collective-permute-start | bytes 466952 | tf_op jit(solution)/shard_map/ppermute | solution.py:1444
  20.6 3.5 %collective-permute-done.4 = bf16[2,19,16,128]{3,2,1,0:T(8,128)(2,1)S(1)} collective-permute-done((bf16[2,19,16,128]{3,2,1,0:T(8,128)(2,1)}, bf16[2,19,16,128]{3,2,1,0:T(8,128)(2,1)S(1)}, u32[]{:S(2)}, u32[]{:S(2)}) %collective-permute-start.4) | collective-permute-done | bytes 155680 | tf_op jit(solution)/shard_map/ppermute | solution.py:1444
  24.2 3.6 %collective-permute-done.3 = bf16[2,19,16,128]{3,2,1,0:T(8,128)(2,1)S(1)} collective-permute-done((bf16[2,19,16,128]{3,2,1,0:T(8,128)(2,1)}, bf16[2,19,16,128]{3,2,1,0:T(8,128)(2,1)S(1)}, u32[]{:S(2)}, u32[]{:S(2)}) %collective-permute-start.3) | collective-permute-done | bytes 155680 | tf_op jit(solution)/shard_map/ppermute | solution.py:1444
  28.9 2.2 collective-permute-start.8
  32.7 5.9 %collective-permute-done.5 = bf16[4,19,16,128]{3,2,1,0:T(8,128)(2,1)S(1)} collective-permute-done((bf16[4,19,16,128]{3,2,1,0:T(8,128)(2,1)S(1)}, bf16[4,19,16,128]{3,2,1,0:T(8,128)(2,1)S(1)}, u32[]{:S(2)}, u32[]{:S(2)}) %collective-permute-start.5) | collective-permute-done | bytes 311328 | tf_op jit(solution)/shard_map/ppermute | solution.py:1444
  40.8 3.8 %collective-permute-done.7 = bf16[2,36,16,128]{3,2,1,0:T(8,128)(2,1)S(1)} collective-permute-done((bf16[2,36,16,128]{3,2,1,0:T(8,128)(2,1)S(1)}, bf16[2,36,16,128]{3,2,1,0:T(8,128)(2,1)S(1)}, u32[]{:S(2)}, u32[]{:S(2)}) %collective-permute-start.7) | collective-permute-done | bytes 294944 | tf_op jit(solution)/shard_map/ppermute | solution.py:1444
  44.6 1.5 collective-permute-start.13
  46.6 2.9 collective-permute-start.10
  49.5 10.4 %collective-permute-done.13 = bf16[2,36,16,128]{3,2,1,0:T(8,128)(2,1)S(1)} collective-permute-done((bf16[2,36,16,128]{3,2,1,0:T(8,128)(2,1)S(1)}, bf16[2,36,16,128]{3,2,1,0:T(8,128)(2,1)S(1)}, u32[]{:S(2)}, u32[]{:S(2)}) %collective-permute-start.13) | collective-permute-done | bytes 294944 | tf_op jit(solution)/shard_map/ppermute | solution.py:1444
  60.2 2.4 collective-permute-done.9.refs_1_.refs_9_
  62.5 1.4 collective-permute-done.10.refs_5_.refs_13_
  64.4 1.5 collective-permute-done.14.refs_3_.refs_11_
  66.9 1.7 collective-permute-start.16
  68.7 10.1 %qkv_forward.1 = (bf16[1024,768]{1,0:T(8,128)(2,1)}, bf16[1024,2304]{1,0:T(8,128)(2,1)}, f32[88,128]{1,0:T(8,128)}) custom-call(s32[1]{0:T(128)} %bitcast.me_ref, bf16[1024,768]{1,0:T(8,128)(2,1)} %tokens_in.1, bf16[8,19,16,128]{3,2,1,0:T(8,128)(2,1)} %copy-done.1, bf16[8,19,16,128]{3,2,1,0:T(8,128)(2,1)} %copy-done.14, bf16[8,19,16,128]{3,2,1,0:T(8,128)(2,1)} %copy-done.12, ...), custom_call_target="tpu_custom_call" | custom-call | flops 3623878656 | bytes 9437184 | tf_op jit(solution)/shard_map/qkv_forward/pallas_call | solution.py:430
  78.8 3.4 %collective-permute-done.16 = bf16[4,36,16,128]{3,2,1,0:T(8,128)(2,1)S(1)} collective-permute-done((bf16[4,36,16,128]{3,2,1,0:T(8,128)(2,1)S(1)}, bf16[4,36,16,128]{3,2,1,0:T(8,128)(2,1)S(1)}, u32[]{:S(2)}, u32[]{:S(2)}) %collective-permute-start.16) | collective-permute-done | bytes 589856 | tf_op jit(solution)/shard_map/ppermute | solution.py:1444
  82.4 1.4 collective-permute-done.17
  85.1 16.2 %attend_forward.1 = (bf16[1024,768]{1,0:T(8,128)(2,1)}, f32[1024,768]{1,0:T(8,128)}, bf16[1024,768]{1,0:T(8,128)(2,1)}, bf16[1024,768]{1,0:T(8,128)(2,1)}, bf16[...) custom-call(s32[1]{0:T(128)} %bitcast.me_ref, s32[3,8]{1,0:T(4,128)} %pad_add_fusion.windows, ...), custom_call_target="tpu_custom_call" | custom-call | flops 1610612736 | bytes 15728640 | tf_op jit(solution)/shard_map/attend_forward/pallas_call | solution.py:635
  101.3 11.0 %collective-permute-done.18.refs_1_ = bf16[8,36,16,128]{3,2,1,0:T(8,128)(2,1)S(1)} collective-permute-done((bf16[8,36,16,128]{3,2,1,0:T(8,128)(2,1)S(1)}, bf16[8,36,16,128]{3,2,1,0:T(8,128)(2,1)S(1)}, u32[]{:S(2)}, u32[]{:S(2)}) %collective-permute-start.18) | collective-permute-done | bytes 1179680 | tf_op jit(solution)/shard_map/ppermute | solution.py:1444
  113.3 4.0 %collective-permute-done.22.refs_3_ = bf16[8,36,16,128]{3,2,1,0:T(8,128)(2,1)S(1)} collective-permute-done((bf16[8,36,16,128]{3,2,1,0:T(8,128)(2,1)S(1)}, bf16[8,36,16,128]{3,2,1,0:T(8,128)(2,1)S(1)}, u32[]{:S(2)}, u32[]{:S(2)}) %collective-permute-start.22) | collective-permute-done | bytes 1179680 | tf_op jit(solution)/shard_map/ppermute | solution.py:1444
  117.5 2.0 copy-done.28
  119.5 35.3 %feed_forward.1 = (bf16[1024,3072]{1,0:T(8,128)(2,1)}, bf16[1024,3072]{1,0:T(8,128)(2,1)}, f32[24,128]{1,0:T(8,128)S(1)}, bf16[16,36,16,128]{3,2,1,0:T(8,128)(2,...) custom-call(s32[1]{0:T(128)} %bitcast.me_ref, ...), custom_call_target="tpu_custom_call" | custom-call | flops 19327352832 | bytes 41943040 | tf_op jit(solution)/shard_map/feed_forward/pallas_call | solution.py:883
  155.4 9.8 %feed_forward_out.1 = (bf16[1024,768]{1,0:T(8,128)(2,1)}, f32[6,128]{1,0:T(8,128)S(1)}) custom-call(s32[1]{0:T(128)} %bitcast.me_ref, bf16[1024,3072]{1,0:T(8,128)(2,1)} %get-tuple-element.190.u_in, f32[1024,768]{1,0:T(8,128)} %get-tuple-element.191.x1_in, bf16[1024,768]{1,0:T(8,128)(2,1)} %cot_in.3, f32[88,128]{1,0:T(8,128)S(1)} %copy-done.24, ...), custom_call_target="tpu_custom_call" | custom-call | flops 4831838208 | bytes 20971520 | tf_op jit(solution)/shard_map/feed_forward_out/pallas_call | solution.py:1005
  165.3 1.4 add_convert_fusion.1
  166.7 4.0 %add_convert_fusion = bf16[8,36,16,128]{3,2,1,0:T(8,128)(2,1)} fusion(bf16[16,36,16,128]{3,2,1,0:T(8,128)(2,1)} %collective-permute-done.25, bf16[16,36,16,128]{3,2,1,0:T(8,128)(2,1)} %get-tuple-element.200), kind=kLoop, calls=%fused_computation | loop fusion | flops 2359296 | bytes 3538944 | tf_op jit(solution)/shard_map/convert_element_type | solution.py:1493
  170.7 1.8 collective-permute-start.26
  172.4 1.3 collective-permute-start.27
  173.8 16.1 %feed_forward_in.1 = (f32[1024,768]{1,0:T(8,128)}, bf16[1024,768]{1,0:T(8,128)(2,1)}, bf16[2,8,9,16,128]{4,3,2,1,0:T(8,128)(2,1)S(1)}, bf16[2,8,9,16,128]{4,3,2,1,0:T(8,128)(2,1)S(1)}, f32[24,128]{1,0:T(8,128)S(1)}) custom-call(s32[1]{0:T(128)} %bitcast.me_ref, bf16[1024,3072]{1,0:T(8,128)(2,1)} %get-tuple-element.203.dz_in, ...), custom_call_target="tpu_custom_call" | custom-call | flops 7247757312 | bytes 41943040 | tf_op jit(solution)/shard_map/feed_forward_in/pallas_call | solution.py:1119
  190.1 1.4 copy-done.27
  191.5 10.2 %attend_backward.2.dqkv_in.dqkv0_in = bf16[1024,1152]{1,0:T(8,128)(2,1)S(1)} custom-call(s32[3,8]{1,0:T(4,128)S(1)} %copy-done.26, bf16[1024,2304]{1,0:T(8,128)(2,1)S(1)} %bitcast.17, bf16[1024,768]{1,0:T(8,128)(2,1)S(1)} %copy-done.27, f32[48,2,256]{2,1,0:T(2,128)S(1)} %copy-done.29, f32[8,128]{1,0:T(8,128)S(1)} %copy-done.25), custom_call_target="tpu_custom_call" | custom-call | flops 3221225472 | bytes 14680064 | tf_op jit(solution)/shard_map/attend_backward/pallas_call | solution.py:1234
  201.7 3.2 %qkv_weight_grad.1 = (bf16[16,9,16,128]{3,2,1,0:T(8,128)(2,1)S(1)}, bf16[16,9,16,128]{3,2,1,0:T(8,128)(2,1)S(1)}, bf16[16,9,16,128]{3,2,1,0:T(8,128)(2,1)S(1)}, bf16[16,9,16,128]{3,2,1,0:T(8,128)(2,1)S(1)}) custom-call(s32[1]{0:T(128)} %bitcast.me_ref, bf16[1024,768]{1,0:T(8,128)(2,1)S(1)} %copy-done.31, ...), custom_call_target="tpu_custom_call" | custom-call | flops 1811939328 | bytes 7864320 | tf_op jit(solution)/shard_map/qkv_weight_grad/pallas_call | solution.py:1294
  205.0 1.4 add_convert_fusion.3
  206.8 1.5 add_convert_fusion.2
  208.5 1.2 collective-permute-start.29
  210.2 10.2 %attend_backward.3.dqkv1_in = bf16[1024,1152]{1,0:T(8,128)(2,1)S(1)} custom-call(s32[3,8]{1,0:T(4,128)S(1)} %copy-done.26, bf16[1024,2304]{1,0:T(8,128)(2,1)S(1)} %bitcast.17, bf16[1024,768]{1,0:T(8,128)(2,1)S(1)} %copy-done.27, f32[48,2,256]{2,1,0:T(2,128)S(1)} %copy-done.29, f32[8,128]{1,0:T(8,128)S(1)} %copy-done.25), custom_call_target="tpu_custom_call" | custom-call | flops 3221225472 | bytes 14680064 | tf_op jit(solution)/shard_map/attend_backward/pallas_call | solution.py:1234
  220.5 2.9 collective-permute-done.28
  224.0 1.8 convert_add_fusion
  225.8 1.4 convert_add_fusion.1
  228.0 1.1 collective-permute-start.33
  229.1 1.1 collective-permute-start.34
  231.1 13.0 %qkv_backward.1 = (f32[1024,768]{1,0:T(8,128)}, bf16[16,10,16,128]{3,2,1,0:T(8,128)(2,1)S(1)}, bf16[16,10,16,128]{3,2,1,0:T(8,128)(2,1)S(1)}, bf16[16,10,16,128]...) custom-call(s32[1]{0:T(128)} %bitcast.me_ref, bf16[1024,768]{1,0:T(8,128)(2,1)} %tokens_in.1, ...), custom_call_target="tpu_custom_call" | custom-call | flops 5435817984 | bytes 23592960 | tf_op jit(solution)/shard_map/qkv_backward/pallas_call | solution.py:1410
  245.6 2.1 collective-permute-start.40
  247.8 1.7 collective-permute-start.37
  250.4 2.5 collective-permute-done.37
  253.3 1.8 collective-permute-start.41
  255.0 1.1 collective-permute-start.42
  256.3 1.8 collective-permute-start.44
  258.2 2.3 collective-permute-start.45
  260.5 1.9 collective-permute-done.41
  262.6 1.8 collective-permute-done.45
  264.5 2.4 collective-permute-start.46
  268.8 2.8 collective-permute-done.46
  273.7 2.1 collective-permute-start.50
  275.9 1.8 collective-permute-start.51
  277.8 1.3 collective-permute-done.50
  279.1 3.0 %collective-permute-done.51 = bf16[2,10,16,128]{3,2,1,0:T(8,128)(2,1)S(1)} collective-permute-done((bf16[2,10,16,128]{3,2,1,0:T(8,128)(2,1)S(1)}, bf16[2,10,16,128]{3,2,1,0:T(8,128)(2,1)S(1)}, u32[]{:S(2)}, u32[]{:S(2)}) %collective-permute-start.51) | collective-permute-done | bytes 81952 | tf_op jit(solution)/shard_map/ppermute | solution.py:1444
  282.8 2.4 spread.1
  285.2 1.9 collective-permute-start.53
  287.1 3.9 %collective-permute-start.52 = (f32[72,128]{1,0:T(8,128)}, f32[72,128]{1,0:T(8,128)S(1)}, u32[]{:S(2)}, u32[]{:S(2)}) collective-permute-start(f32[72,128]{1,0:T(8,128)} %get-tuple-element.283), channel_id=1, source_target_pairs={{0,1},{1,2},{2,3},{3,4},{4,5},{15,16},{16,17}} | collective-permute-start | bytes 110600 | tf_op jit(solution)/shard_map/ppermute | solution.py:1758
  291.0 5.2 %collective-permute-done.52.below = f32[72,128]{1,0:T(8,128)S(1)} collective-permute-done((f32[72,128]{1,0:T(8,128)}, f32[72,128]{1,0:T(8,128)S(1)}, u32[]{:S(2)}, u32[]{:S(2)}) %collective-permute-start.52) | collective-permute-done | bytes 36896 | tf_op jit(solution)/shard_map/ppermute | solution.py:1758
  296.8 2.2 close.1
  (225 shorter events, 24.7 us)
Async XLA Ops:
  1.9 10.7 %collective-permute-start = (bf16[128,128]{1,0:T(8,128)(2,1)S(1)}, bf16[128,128]{1,0:T(8,128)(2,1)S(1)}, u32[]{:S(2)}, u32[]{:S(2)}) collective-permute-start(bf16[128,128]{1,0:T(8,128)(2,1)S(1)} %pad_maximum_fusion.17), channel_id=1, source_target_pairs={{6,7},{7,8},{8,9},{9,10},{10,11},{11,12},{12,13},{13,14},{14,15},{... | collective-permute-start | bytes 98312 | tf_op jit(solution)/shard_map/ppermute | solution.py:1670
  5.4 7.2 %collective-permute-start.1 = (bf16[72,128]{1,0:T(8,128)(2,1)S(1)}, bf16[72,128]{1,0:T(8,128)(2,1)S(1)}, u32[]{:S(2)}, u32[]{:S(2)}) collective-permute-start(bf16[72,128]{1,0:T(8,128)(2,1)S(1)} %pad_maximum_fusion.19), channel_id=1, source_target_pairs={{1,0},{2,1},{3,2},{4,3},{5,4},{16,15},{17,16}} | collective-permute-start | bytes 55304 | tf_op jit(solution)/shard_map/ppermute | solution.py:1669
  15.3 8.9 %collective-permute-start.4 = (bf16[2,19,16,128]{3,2,1,0:T(8,128)(2,1)}, bf16[2,19,16,128]{3,2,1,0:T(8,128)(2,1)S(1)}, u32[]{:S(2)}, u32[]{:S(2)}) collective-permute-start(bf16[2,19,16,128]{3,2,1,0:T(8,128)(2,1)} %get-tuple-element.144), channel_id=1, source_target_pairs={{0,6},{1,7},{2,4},{3,5},{4,2},{5,3},{6,0},{7,1},{8,14},{9,15},{10,... | collective-permute-start | bytes 466952 | tf_op jit(solution)/shard_map/ppermute | solution.py:1444
  15.3 12.5 %collective-permute-start.3 = (bf16[2,19,16,128]{3,2,1,0:T(8,128)(2,1)}, bf16[2,19,16,128]{3,2,1,0:T(8,128)(2,1)S(1)}, u32[]{:S(2)}, u32[]{:S(2)}) collective-permute-start(bf16[2,19,16,128]{3,2,1,0:T(8,128)(2,1)} %get-tuple-element.144), channel_id=1, source_target_pairs={{0,4},{1,5},{2,6},{3,7},{4,0},{5,1},{6,2},{7,3},{8,12},{9,13},{10,... | collective-permute-start | bytes 466952 | tf_op jit(solution)/shard_map/ppermute | solution.py:1444
  15.4 12.5 %collective-permute-start.2 = (bf16[2,19,16,128]{3,2,1,0:T(8,128)(2,1)}, bf16[2,19,16,128]{3,2,1,0:T(8,128)(2,1)S(1)}, u32[]{:S(2)}, u32[]{:S(2)}) collective-permute-start(bf16[2,19,16,128]{3,2,1,0:T(8,128)(2,1)} %get-tuple-element.144), channel_id=1, source_target_pairs={{0,2},{1,3},{2,0},{3,1},{4,6},{5,7},{6,4},{7,5},{8,10},{9,11},{10,... | collective-permute-start | bytes 466952 | tf_op jit(solution)/shard_map/ppermute | solution.py:1444
  28.9 11.8 %collective-permute-start.8 = (bf16[2,36,16,128]{3,2,1,0:T(8,128)(2,1)S(1)}, bf16[2,36,16,128]{3,2,1,0:T(8,128)(2,1)S(1)}, u32[]{:S(2)}, u32[]{:S(2)}) collective-permute-start(bf16[2,36,16,128]{3,2,1,0:T(8,128)(2,1)S(1)} %copy-done.40), channel_id=1, source_target_pairs={{0,6},{1,7},{2,4},{3,5},{4,2},{5,3},{6,0},{7,1},{8,14},{9,15},{10,... | collective-permute-start | bytes 884744 | tf_op jit(solution)/shard_map/ppermute | solution.py:1444
  31.1 13.5 %collective-permute-start.7 = (bf16[2,36,16,128]{3,2,1,0:T(8,128)(2,1)S(1)}, bf16[2,36,16,128]{3,2,1,0:T(8,128)(2,1)S(1)}, u32[]{:S(2)}, u32[]{:S(2)}) collective-permute-start(bf16[2,36,16,128]{3,2,1,0:T(8,128)(2,1)S(1)} %copy-done.40), channel_id=1, source_target_pairs={{0,2},{1,3},{2,0},{3,1},{4,6},{5,7},{6,4},{7,5},{8,10},{9,11},{10,... | collective-permute-start | bytes 884744 | tf_op jit(solution)/shard_map/ppermute | solution.py:1444
  31.1 7.5 %collective-permute-start.5 = (bf16[4,19,16,128]{3,2,1,0:T(8,128)(2,1)S(1)}, bf16[4,19,16,128]{3,2,1,0:T(8,128)(2,1)S(1)}, u32[]{:S(2)}, u32[]{:S(2)}) collective-permute-start(bf16[4,19,16,128]{3,2,1,0:T(8,128)(2,1)S(1)} %get-tuple-element.146), channel_id=1, source_target_pairs={{0,16},{1,17},{2,18},{3,19},{4,20},{5,21},{6,22},{7,23},{8,24},{9,... | collective-permute-start | bytes 933896 | tf_op jit(solution)/shard_map/ppermute | solution.py:1444
  31.7 8.0 %collective-permute-start.6 = (bf16[4,19,16,128]{3,2,1,0:T(8,128)(2,1)S(1)}, bf16[4,19,16,128]{3,2,1,0:T(8,128)(2,1)S(1)}, u32[]{:S(2)}, u32[]{:S(2)}) collective-permute-start(bf16[4,19,16,128]{3,2,1,0:T(8,128)(2,1)S(1)} %get-tuple-element.147), channel_id=1, source_target_pairs={{0,1},{1,0},{2,3},{3,2},{4,5},{5,4},{6,7},{7,6},{8,9},{9,8},{10,11... | collective-permute-start | bytes 933896 | tf_op jit(solution)/shard_map/ppermute | solution.py:1444
  38.7 21.3 %copy-start.1 = (bf16[8,19,16,128]{3,2,1,0:T(8,128)(2,1)}, bf16[8,19,16,128]{3,2,1,0:T(8,128)(2,1)S(1)}, u32[]{:S(2)}) copy-start(bf16[8,19,16,128]{3,2,1,0:T(8,128)(2,1)S(1)} %pad_maximum_fusion.2.refs_0_.refs_8_) | copy-start | bytes 1867780
  44.6 15.3 %collective-permute-start.13 = (bf16[2,36,16,128]{3,2,1,0:T(8,128)(2,1)S(1)}, bf16[2,36,16,128]{3,2,1,0:T(8,128)(2,1)S(1)}, u32[]{:S(2)}, u32[]{:S(2)}) collective-permute-start(bf16[2,36,16,128]{3,2,1,0:T(8,128)(2,1)S(1)} %copy-done.40), channel_id=1, source_target_pairs={{0,4},{1,5},{2,6},{3,7},{4,0},{5,1},{6,2},{7,3},{8,12},{9,13},{10,... | collective-permute-start | bytes 884744 | tf_op jit(solution)/shard_map/ppermute | solution.py:1444
  46.1 14.0 %collective-permute-start.11 = (bf16[8,19,16,128]{3,2,1,0:T(8,128)(2,1)S(1)}, bf16[8,19,16,128]{3,2,1,0:T(8,128)(2,1)S(1)}, u32[]{:S(2)}, u32[]{:S(2)}) collective-permute-start(bf16[8,19,16,128]{3,2,1,0:T(8,128)(2,1)S(1)} %pad_maximum_fusion.2.refs_0_.refs_8_), channel_id=1, source_target_pairs={{0,8},{1,9},{2,10},{3,11},{4,12},{5,13},{6,14},{7,15},{8,0},{9,1},... | collective-permute-start | bytes 1867784 | tf_op jit(solution)/shard_map/ppermute | solution.py:1444
  46.1 16.4 %collective-permute-start.9 = (bf16[8,19,16,128]{3,2,1,0:T(8,128)(2,1)S(1)}, bf16[8,19,16,128]{3,2,1,0:T(8,128)(2,1)S(1)}, u32[]{:S(2)}, u32[]{:S(2)}) collective-permute-start(bf16[8,19,16,128]{3,2,1,0:T(8,128)(2,1)S(1)} %pad_maximum_fusion.2.refs_0_.refs_8_), channel_id=1, source_target_pairs={{0,1},{1,0},{2,3},{3,2},{4,5},{5,4},{6,7},{7,6},{8,9},{9,8},{10,11... | collective-permute-start | bytes 1867784 | tf_op jit(solution)/shard_map/ppermute | solution.py:1444
  46.1 16.4 %collective-permute-start.12 = (bf16[8,19,16,128]{3,2,1,0:T(8,128)(2,1)S(1)}, bf16[8,19,16,128]{3,2,1,0:T(8,128)(2,1)S(1)}, u32[]{:S(2)}, u32[]{:S(2)}) collective-permute-start(bf16[8,19,16,128]{3,2,1,0:T(8,128)(2,1)S(1)} %pad_maximum_fusion.3.refs_4_.refs_12_), channel_id=1, source_target_pairs={{0,8},{1,9},{2,10},{3,11},{4,12},{5,13},{6,14},{7,15},{8,0},{9,1},... | collective-permute-start | bytes 1867784 | tf_op jit(solution)/shard_map/ppermute | solution.py:1444
  46.6 17.3 %collective-permute-start.10 = (bf16[8,19,16,128]{3,2,1,0:T(8,128)(2,1)S(1)}, bf16[8,19,16,128]{3,2,1,0:T(8,128)(2,1)S(1)}, u32[]{:S(2)}, u32[]{:S(2)}) collective-permute-start(bf16[8,19,16,128]{3,2,1,0:T(8,128)(2,1)S(1)} %pad_maximum_fusion.3.refs_4_.refs_12_), channel_id=1, source_target_pairs={{0,16},{1,17},{2,18},{3,19},{4,20},{5,21},{6,22},{7,23},{8,24},{9,... | collective-permute-start | bytes 1867784 | tf_op jit(solution)/shard_map/ppermute | solution.py:1444
  63.9 2.1 collective-permute-start.14
  63.9 2.9 collective-permute-start.15
  66.9 15.4 %collective-permute-start.16 = (bf16[4,36,16,128]{3,2,1,0:T(8,128)(2,1)S(1)}, bf16[4,36,16,128]{3,2,1,0:T(8,128)(2,1)S(1)}, u32[]{:S(2)}, u32[]{:S(2)}) collective-permute-start(bf16[4,36,16,128]{3,2,1,0:T(8,128)(2,1)S(1)} %pad_maximum_fusion.4), channel_id=1, source_target_pairs={{0,16},{1,17},{2,18},{3,19},{4,20},{5,21},{6,22},{7,23},{8,24},{9,... | collective-permute-start | bytes 1769480 | tf_op jit(solution)/shard_map/ppermute | solution.py:1444
  68.6 15.1 %collective-permute-start.17 = (bf16[4,36,16,128]{3,2,1,0:T(8,128)(2,1)S(1)}, bf16[4,36,16,128]{3,2,1,0:T(8,128)(2,1)S(1)}, u32[]{:S(2)}, u32[]{:S(2)}) collective-permute-start(bf16[4,36,16,128]{3,2,1,0:T(8,128)(2,1)S(1)} %pad_maximum_fusion.5), channel_id=1, source_target_pairs={{0,1},{1,0},{2,3},{3,2},{4,5},{5,4},{6,7},{7,6},{8,9},{9,8},{10,11... | collective-permute-start | bytes 1769480 | tf_op jit(solution)/shard_map/ppermute | solution.py:1444
  83.8 71.5 %copy-start = (bf16[8,36,16,128]{3,2,1,0:T(8,128)(2,1)}, bf16[8,36,16,128]{3,2,1,0:T(8,128)(2,1)S(1)}, u32[]{:S(2)}) copy-start(bf16[8,36,16,128]{3,2,1,0:T(8,128)(2,1)S(1)} %pad_maximum_fusion.1.refs_4_) | copy-start | bytes 3538948
  83.8 17.4 %collective-permute-start.20 = (bf16[8,36,16,128]{3,2,1,0:T(8,128)(2,1)S(1)}, bf16[8,36,16,128]{3,2,1,0:T(8,128)(2,1)S(1)}, u32[]{:S(2)}, u32[]{:S(2)}) collective-permute-start(bf16[8,36,16,128]{3,2,1,0:T(8,128)(2,1)S(1)} %pad_maximum_fusion.refs_0_), channel_id=1, source_target_pairs={{0,8},{1,9},{2,10},{3,11},{4,12},{5,13},{6,14},{7,15},{8,0},{9,1},... | collective-permute-start | bytes 3538952 | tf_op jit(solution)/shard_map/ppermute | solution.py:1444
  83.9 28.4 %collective-permute-start.18 = (bf16[8,36,16,128]{3,2,1,0:T(8,128)(2,1)S(1)}, bf16[8,36,16,128]{3,2,1,0:T(8,128)(2,1)S(1)}, u32[]{:S(2)}, u32[]{:S(2)}) collective-permute-start(bf16[8,36,16,128]{3,2,1,0:T(8,128)(2,1)S(1)} %pad_maximum_fusion.refs_0_), channel_id=1, source_target_pairs={{0,1},{1,0},{2,3},{3,2},{4,5},{5,4},{6,7},{7,6},{8,9},{9,8},{10,11... | collective-permute-start | bytes 3538952 | tf_op jit(solution)/shard_map/ppermute | solution.py:1444
  84.3 28.0 %collective-permute-start.21 = (bf16[8,36,16,128]{3,2,1,0:T(8,128)(2,1)S(1)}, bf16[8,36,16,128]{3,2,1,0:T(8,128)(2,1)S(1)}, u32[]{:S(2)}, u32[]{:S(2)}) collective-permute-start(bf16[8,36,16,128]{3,2,1,0:T(8,128)(2,1)S(1)} %pad_maximum_fusion.1.refs_4_), channel_id=1, source_target_pairs={{0,8},{1,9},{2,10},{3,11},{4,12},{5,13},{6,14},{7,15},{8,0},{9,1},... | collective-permute-start | bytes 3538952 | tf_op jit(solution)/shard_map/ppermute | solution.py:1444
  84.4 28.3 %collective-permute-start.19 = (bf16[8,36,16,128]{3,2,1,0:T(8,128)(2,1)S(1)}, bf16[8,36,16,128]{3,2,1,0:T(8,128)(2,1)}, u32[]{:S(2)}, u32[]{:S(2)}) collective-permute-start(bf16[8,36,16,128]{3,2,1,0:T(8,128)(2,1)S(1)} %pad_maximum_fusion.1.refs_4_), channel_id=1, source_target_pairs={{0,16},{1,17},{2,18},{3,19},{4,20},{5,21},{6,22},{7,23},{8,24},{9,... | collective-permute-start | bytes 3538952 | tf_op jit(solution)/shard_map/ppermute | solution.py:1444
  85.1 32.4 %copy-start.24 = (f32[88,128]{1,0:T(8,128)S(1)}, f32[88,128]{1,0:T(8,128)}, u32[]{:S(2)}) copy-start(f32[88,128]{1,0:T(8,128)} %get-tuple-element.180.small) | copy-start | bytes 135172
  101.2 54.1 %copy-start.5 = (bf16[8,36,16,128]{3,2,1,0:T(8,128)(2,1)}, bf16[8,36,16,128]{3,2,1,0:T(8,128)(2,1)S(1)}, u32[]{:S(2)}) copy-start(bf16[8,36,16,128]{3,2,1,0:T(8,128)(2,1)S(1)} %collective-permute-done.20.refs_2_) | copy-start | bytes 3538948
  112.3 43.1 %copy-start.7 = (bf16[8,36,16,128]{3,2,1,0:T(8,128)(2,1)}, bf16[8,36,16,128]{3,2,1,0:T(8,128)(2,1)S(1)}, u32[]{:S(2)}) copy-start(bf16[8,36,16,128]{3,2,1,0:T(8,128)(2,1)S(1)} %collective-permute-done.18.refs_1_) | copy-start | bytes 3538948
  112.3 43.1 %copy-start.9 = (bf16[8,36,16,128]{3,2,1,0:T(8,128)(2,1)}, bf16[8,36,16,128]{3,2,1,0:T(8,128)(2,1)S(1)}, u32[]{:S(2)}) copy-start(bf16[8,36,16,128]{3,2,1,0:T(8,128)(2,1)S(1)} %collective-permute-done.21.refs_6_) | copy-start | bytes 3538948
  112.7 4.5 %collective-permute-start.22 = (bf16[8,36,16,128]{3,2,1,0:T(8,128)(2,1)S(1)}, bf16[8,36,16,128]{3,2,1,0:T(8,128)(2,1)S(1)}, u32[]{:S(2)}, u32[]{:S(2)}) collective-permute-start(bf16[8,36,16,128]{3,2,1,0:T(8,128)(2,1)S(1)} %collective-permute-done.18.refs_1_), channel_id=1, source_target_pairs={{0,8},{1,9},{2,10},{3,11},{4,12},{5,13},{6,14},{7,15},{8,0},{9,1},... | collective-permute-start | bytes 3538952 | tf_op jit(solution)/shard_map/ppermute | solution.py:1444
  112.8 4.7 %collective-permute-start.23 = (bf16[8,36,16,128]{3,2,1,0:T(8,128)(2,1)}, bf16[8,36,16,128]{3,2,1,0:T(8,128)(2,1)S(1)}, u32[]{:S(2)}, u32[]{:S(2)}) collective-permute-start(bf16[8,36,16,128]{3,2,1,0:T(8,128)(2,1)} %collective-permute-done.19.refs_5_), channel_id=1, source_target_pairs={{0,8},{1,9},{2,10},{3,11},{4,12},{5,13},{6,14},{7,15},{8,0},{9,1},... | collective-permute-start | bytes 3538952 | tf_op jit(solution)/shard_map/ppermute | solution.py:1444
  117.2 38.1 %copy-start.10 = (bf16[8,36,16,128]{3,2,1,0:T(8,128)(2,1)}, bf16[8,36,16,128]{3,2,1,0:T(8,128)(2,1)S(1)}, u32[]{:S(2)}) copy-start(bf16[8,36,16,128]{3,2,1,0:T(8,128)(2,1)S(1)} %collective-permute-done.22.refs_3_) | copy-start | bytes 3538948
  117.5 37.3 %copy-start.11 = (bf16[8,36,16,128]{3,2,1,0:T(8,128)(2,1)}, bf16[8,36,16,128]{3,2,1,0:T(8,128)(2,1)S(1)}, u32[]{:S(2)}) copy-start(bf16[8,36,16,128]{3,2,1,0:T(8,128)(2,1)S(1)} %collective-permute-done.23.refs_7_) | copy-start | bytes 3538948
  154.8 10.4 %collective-permute-start.24 = (bf16[16,36,16,128]{3,2,1,0:T(8,128)(2,1)}, bf16[16,36,16,128]{3,2,1,0:T(8,128)(2,1)S(1)}, u32[]{:S(2)}, u32[]{:S(2)}) collective-permute-start(bf16[16,36,16,128]{3,2,1,0:T(8,128)(2,1)} %get-tuple-element.195), channel_id=1, source_target_pairs={{0,8},{1,9},{2,10},{3,11},{4,12},{5,13},{6,14},{7,15},{8,0},{9,1},... | collective-permute-start | bytes 7077896 | tf_op jit(solution)/shard_map/ppermute | solution.py:1444
  154.9 10.3 %collective-permute-start.25 = (bf16[16,36,16,128]{3,2,1,0:T(8,128)(2,1)}, bf16[16,36,16,128]{3,2,1,0:T(8,128)(2,1)}, u32[]{:S(2)}, u32[]{:S(2)}) collective-permute-start(bf16[16,36,16,128]{3,2,1,0:T(8,128)(2,1)} %get-tuple-element.196), channel_id=1, source_target_pairs={{0,8},{1,9},{2,10},{3,11},{4,12},{5,13},{6,14},{7,15},{8,0},{9,1},... | collective-permute-start | bytes 7077896 | tf_op jit(solution)/shard_map/ppermute | solution.py:1444
  165.2 24.8 %copy-start.35 = (bf16[16,36,16,128]{3,2,1,0:T(8,128)(2,1)}, bf16[16,36,16,128]{3,2,1,0:T(8,128)(2,1)S(1)}, u32[]{:S(2)}) copy-start(bf16[16,36,16,128]{3,2,1,0:T(8,128)(2,1)S(1)} %collective-permute-done.24) | copy-start | bytes 7077892
  166.7 23.3 %slice-start = ((s8[4718592]{0:T(1024)(128)(4,1)}), s8[4194304]{0:T(1024)(128)(4,1)S(1)}, s32[]{:S(2)}) async-start(s8[4718592]{0:T(1024)(128)(4,1)} %bitcast.16), calls=%async_computation | async-start | bytes 8388608
  170.7 34.3 %collective-permute-start.26 = (bf16[8,36,16,128]{3,2,1,0:T(8,128)(2,1)}, bf16[8,36,16,128]{3,2,1,0:T(8,128)(2,1)}, u32[]{:S(2)}, u32[]{:S(2)}) collective-permute-start(bf16[8,36,16,128]{3,2,1,0:T(8,128)(2,1)} %add_convert_fusion.1), channel_id=1, source_target_pairs={{0,1},{1,0},{2,3},{3,2},{4,5},{5,4},{6,7},{7,6},{8,9},{9,8},{10,11... | collective-permute-start | bytes 3538952 | tf_op jit(solution)/shard_map/ppermute | solution.py:1444
  172.4 32.6 %collective-permute-start.27 = (bf16[8,36,16,128]{3,2,1,0:T(8,128)(2,1)}, bf16[8,36,16,128]{3,2,1,0:T(8,128)(2,1)}, u32[]{:S(2)}, u32[]{:S(2)}) collective-permute-start(bf16[8,36,16,128]{3,2,1,0:T(8,128)(2,1)} %add_convert_fusion), channel_id=1, source_target_pairs={{0,16},{1,17},{2,18},{3,19},{4,20},{5,21},{6,22},{7,23},{8,24},{9,... | collective-permute-start | bytes 3538952 | tf_op jit(solution)/shard_map/ppermute | solution.py:1444
  208.3 15.1 %collective-permute-start.28 = (bf16[4,36,16,128]{3,2,1,0:T(8,128)(2,1)S(1)}, bf16[4,36,16,128]{3,2,1,0:T(8,128)(2,1)S(1)}, u32[]{:S(2)}, u32[]{:S(2)}) collective-permute-start(bf16[4,36,16,128]{3,2,1,0:T(8,128)(2,1)S(1)} %add_convert_fusion.3), channel_id=1, source_target_pairs={{0,16},{1,17},{2,18},{3,19},{4,20},{5,21},{6,22},{7,23},{8,24},{9,... | collective-permute-start | bytes 1769480 | tf_op jit(solution)/shard_map/ppermute | solution.py:1444
  208.5 15.5 %collective-permute-start.29 = (bf16[4,36,16,128]{3,2,1,0:T(8,128)(2,1)S(1)}, bf16[4,36,16,128]{3,2,1,0:T(8,128)(2,1)S(1)}, u32[]{:S(2)}, u32[]{:S(2)}) collective-permute-start(bf16[4,36,16,128]{3,2,1,0:T(8,128)(2,1)S(1)} %add_convert_fusion.2), channel_id=1, source_target_pairs={{0,1},{1,0},{2,3},{3,2},{4,5},{5,4},{6,7},{7,6},{8,9},{9,8},{10,11... | collective-permute-start | bytes 1769480 | tf_op jit(solution)/shard_map/ppermute | solution.py:1444
  209.7 14.3 %collective-permute-start.30 = (bf16[16,9,16,128]{3,2,1,0:T(8,128)(2,1)S(1)}, bf16[16,9,16,128]{3,2,1,0:T(8,128)(2,1)S(1)}, u32[]{:S(2)}, u32[]{:S(2)}) collective-permute-start(bf16[16,9,16,128]{3,2,1,0:T(8,128)(2,1)S(1)} %get-tuple-element.226), channel_id=1, source_target_pairs={{0,8},{1,9},{2,10},{3,11},{4,12},{5,13},{6,14},{7,15},{8,0},{9,1},... | collective-permute-start | bytes 1769480 | tf_op jit(solution)/shard_map/ppermute | solution.py:1444
  209.7 14.3 %collective-permute-start.31 = (bf16[16,9,16,128]{3,2,1,0:T(8,128)(2,1)S(1)}, bf16[16,9,16,128]{3,2,1,0:T(8,128)(2,1)S(1)}, u32[]{:S(2)}, u32[]{:S(2)}) collective-permute-start(bf16[16,9,16,128]{3,2,1,0:T(8,128)(2,1)S(1)} %get-tuple-element.227), channel_id=1, source_target_pairs={{0,8},{1,9},{2,10},{3,11},{4,12},{5,13},{6,14},{7,15},{8,0},{9,1},... | collective-permute-start | bytes 1769480 | tf_op jit(solution)/shard_map/ppermute | solution.py:1444
  227.6 16.5 %collective-permute-start.32 = (bf16[8,9,16,128]{3,2,1,0:T(8,128)(2,1)S(1)}, bf16[8,9,16,128]{3,2,1,0:T(8,128)(2,1)S(1)}, u32[]{:S(2)}, u32[]{:S(2)}) collective-permute-start(bf16[8,9,16,128]{3,2,1,0:T(8,128)(2,1)S(1)} %add_convert_fusion.7), channel_id=1, source_target_pairs={{0,1},{1,0},{2,3},{3,2},{4,5},{5,4},{6,7},{7,6},{8,9},{9,8},{10,11... | collective-permute-start | bytes 884744 | tf_op jit(solution)/shard_map/ppermute | solution.py:1444
  228.0 16.2 %collective-permute-start.33 = (bf16[8,9,16,128]{3,2,1,0:T(8,128)(2,1)S(1)}, bf16[8,9,16,128]{3,2,1,0:T(8,128)(2,1)S(1)}, u32[]{:S(2)}, u32[]{:S(2)}) collective-permute-start(bf16[8,9,16,128]{3,2,1,0:T(8,128)(2,1)S(1)} %add_convert_fusion.6), channel_id=1, source_target_pairs={{0,16},{1,17},{2,18},{3,19},{4,20},{5,21},{6,22},{7,23},{8,24},{9,... | collective-permute-start | bytes 884744 | tf_op jit(solution)/shard_map/ppermute | solution.py:1444
  229.1 15.1 %collective-permute-start.34 = (bf16[2,36,16,128]{3,2,1,0:T(8,128)(2,1)S(1)}, bf16[2,36,16,128]{3,2,1,0:T(8,128)(2,1)S(1)}, u32[]{:S(2)}, u32[]{:S(2)}) collective-permute-start(bf16[2,36,16,128]{3,2,1,0:T(8,128)(2,1)S(1)} %pad_maximum_fusion.8), channel_id=1, source_target_pairs={{0,2},{1,3},{2,0},{3,1},{4,6},{5,7},{6,4},{7,5},{8,10},{9,11},{10,... | collective-permute-start | bytes 884744 | tf_op jit(solution)/shard_map/ppermute | solution.py:1444
  230.1 14.8 %collective-permute-start.35 = (bf16[2,36,16,128]{3,2,1,0:T(8,128)(2,1)S(1)}, bf16[2,36,16,128]{3,2,1,0:T(8,128)(2,1)S(1)}, u32[]{:S(2)}, u32[]{:S(2)}) collective-permute-start(bf16[2,36,16,128]{3,2,1,0:T(8,128)(2,1)S(1)} %pad_maximum_fusion.9), channel_id=1, source_target_pairs={{0,4},{1,5},{2,6},{3,7},{4,0},{5,1},{6,2},{7,3},{8,12},{9,13},{10,... | collective-permute-start | bytes 884744 | tf_op jit(solution)/shard_map/ppermute | solution.py:1444
  245.1 5.2 %collective-permute-start.36 = (bf16[4,9,16,128]{3,2,1,0:T(8,128)(2,1)S(1)}, bf16[4,9,16,128]{3,2,1,0:T(8,128)(2,1)S(1)}, u32[]{:S(2)}, u32[]{:S(2)}) collective-permute-start(bf16[4,9,16,128]{3,2,1,0:T(8,128)(2,1)S(1)} %add_convert_fusion.11), channel_id=1, source_target_pairs={{0,16},{1,17},{2,18},{3,19},{4,20},{5,21},{6,22},{7,23},{8,24},{9,... | collective-permute-start | bytes 442376 | tf_op jit(solution)/shard_map/ppermute | solution.py:1444
  245.6 7.6 %collective-permute-start.40 = (bf16[36,16,128]{2,1,0:T(8,128)(2,1)S(1)}, bf16[36,16,128]{2,1,0:T(8,128)(2,1)S(1)}, u32[]{:S(2)}, u32[]{:S(2)}) collective-permute-start(bf16[36,16,128]{2,1,0:T(8,128)(2,1)S(1)} %slice_bitcast_fusion.1), channel_id=1, source_target_pairs={{0,6},{1,7},{2,4},{3,5},{4,2},{5,3},{6,0},{7,1},{8,14},{9,15},{10,... | collective-permute-start | bytes 442376 | tf_op jit(solution)/shard_map/ppermute | solution.py:1444
  247.8 5.1 %collective-permute-start.37 = (bf16[4,9,16,128]{3,2,1,0:T(8,128)(2,1)S(1)}, bf16[4,9,16,128]{3,2,1,0:T(8,128)(2,1)S(1)}, u32[]{:S(2)}, u32[]{:S(2)}) collective-permute-start(bf16[4,9,16,128]{3,2,1,0:T(8,128)(2,1)S(1)} %add_convert_fusion.10), channel_id=1, source_target_pairs={{0,1},{1,0},{2,3},{3,2},{4,5},{5,4},{6,7},{7,6},{8,9},{9,8},{10,11... | collective-permute-start | bytes 442376 | tf_op jit(solution)/shard_map/ppermute | solution.py:1444
  249.5 3.6 %collective-permute-start.38 = (bf16[16,10,16,128]{3,2,1,0:T(8,128)(2,1)S(1)}, bf16[16,10,16,128]{3,2,1,0:T(8,128)(2,1)S(1)}, u32[]{:S(2)}, u32[]{:S(2)}) collective-permute-start(bf16[16,10,16,128]{3,2,1,0:T(8,128)(2,1)S(1)} %get-tuple-element.258), channel_id=1, source_target_pairs={{0,8},{1,9},{2,10},{3,11},{4,12},{5,13},{6,14},{7,15},{8,0},{9,1},... | collective-permute-start | bytes 1966088 | tf_op jit(solution)/shard_map/ppermute | solution.py:1444
  249.5 3.7 %collective-permute-start.39 = (bf16[16,10,16,128]{3,2,1,0:T(8,128)(2,1)S(1)}, bf16[16,10,16,128]{3,2,1,0:T(8,128)(2,1)S(1)}, u32[]{:S(2)}, u32[]{:S(2)}) collective-permute-start(bf16[16,10,16,128]{3,2,1,0:T(8,128)(2,1)S(1)} %get-tuple-element.260), channel_id=1, source_target_pairs={{0,8},{1,9},{2,10},{3,11},{4,12},{5,13},{6,14},{7,15},{8,0},{9,1},... | collective-permute-start | bytes 1966088 | tf_op jit(solution)/shard_map/ppermute | solution.py:1444
  253.3 9.1 %collective-permute-start.41 = (bf16[8,10,16,128]{3,2,1,0:T(8,128)(2,1)S(1)}, bf16[8,10,16,128]{3,2,1,0:T(8,128)(2,1)S(1)}, u32[]{:S(2)}, u32[]{:S(2)}) collective-permute-start(bf16[8,10,16,128]{3,2,1,0:T(8,128)(2,1)S(1)} %add_convert_fusion.5), channel_id=1, source_target_pairs={{0,1},{1,0},{2,3},{3,2},{4,5},{5,4},{6,7},{7,6},{8,9},{9,8},{10,11... | collective-permute-start | bytes 983048 | tf_op jit(solution)/shard_map/ppermute | solution.py:1444
  255.0 7.5 %collective-permute-start.42 = (bf16[8,10,16,128]{3,2,1,0:T(8,128)(2,1)S(1)}, bf16[8,10,16,128]{3,2,1,0:T(8,128)(2,1)S(1)}, u32[]{:S(2)}, u32[]{:S(2)}) collective-permute-start(bf16[8,10,16,128]{3,2,1,0:T(8,128)(2,1)S(1)} %add_convert_fusion.4), channel_id=1, source_target_pairs={{0,16},{1,17},{2,18},{3,19},{4,20},{5,21},{6,22},{7,23},{8,24},{9,... | collective-permute-start | bytes 983048 | tf_op jit(solution)/shard_map/ppermute | solution.py:1444
  256.1 6.4 %collective-permute-start.43 = (bf16[2,9,16,128]{3,2,1,0:T(8,128)(2,1)S(1)}, bf16[2,9,16,128]{3,2,1,0:T(8,128)(2,1)S(1)}, u32[]{:S(2)}, u32[]{:S(2)}) collective-permute-start(bf16[2,9,16,128]{3,2,1,0:T(8,128)(2,1)S(1)} %pad_maximum_fusion.14), channel_id=1, source_target_pairs={{0,2},{1,3},{2,0},{3,1},{4,6},{5,7},{6,4},{7,5},{8,10},{9,11},{10,... | collective-permute-start | bytes 221192 | tf_op jit(solution)/shard_map/ppermute | solution.py:1444
  256.3 6.2 %collective-permute-start.44 = (bf16[2,9,16,128]{3,2,1,0:T(8,128)(2,1)S(1)}, bf16[2,9,16,128]{3,2,1,0:T(8,128)(2,1)S(1)}, u32[]{:S(2)}, u32[]{:S(2)}) collective-permute-start(bf16[2,9,16,128]{3,2,1,0:T(8,128)(2,1)S(1)} %pad_maximum_fusion.15), channel_id=1, source_target_pairs={{0,4},{1,5},{2,6},{3,7},{4,0},{5,1},{6,2},{7,3},{8,12},{9,13},{10,... | collective-permute-start | bytes 221192 | tf_op jit(solution)/shard_map/ppermute | solution.py:1444
  258.2 6.3 %collective-permute-start.45 = (bf16[2,9,16,128]{3,2,1,0:T(8,128)(2,1)S(1)}, bf16[2,9,16,128]{3,2,1,0:T(8,128)(2,1)S(1)}, u32[]{:S(2)}, u32[]{:S(2)}) collective-permute-start(bf16[2,9,16,128]{3,2,1,0:T(8,128)(2,1)S(1)} %pad_maximum_fusion.16), channel_id=1, source_target_pairs={{0,6},{1,7},{2,4},{3,5},{4,2},{5,3},{6,0},{7,1},{8,14},{9,15},{10,... | collective-permute-start | bytes 221192 | tf_op jit(solution)/shard_map/ppermute | solution.py:1444
  264.5 7.1 %collective-permute-start.46 = (bf16[36,16,128]{2,1,0:T(8,128)(2,1)S(1)}, bf16[36,16,128]{2,1,0:T(8,128)(2,1)S(1)}, u32[]{:S(2)}, u32[]{:S(2)}) collective-permute-start(bf16[36,16,128]{2,1,0:T(8,128)(2,1)S(1)} %slice_bitcast_fusion), channel_id=1, source_target_pairs={{0,6},{1,7},{2,4},{3,5},{4,2},{5,3},{6,0},{7,1},{8,14},{9,15},{10,... | collective-permute-start | bytes 442376 | tf_op jit(solution)/shard_map/ppermute | solution.py:1444
  266.9 5.7 %collective-permute-start.47 = (bf16[4,10,16,128]{3,2,1,0:T(8,128)(2,1)S(1)}, bf16[4,10,16,128]{3,2,1,0:T(8,128)(2,1)S(1)}, u32[]{:S(2)}, u32[]{:S(2)}) collective-permute-start(bf16[4,10,16,128]{3,2,1,0:T(8,128)(2,1)S(1)} %add_convert_fusion.9), channel_id=1, source_target_pairs={{0,16},{1,17},{2,18},{3,19},{4,20},{5,21},{6,22},{7,23},{8,24},{9,... | collective-permute-start | bytes 491528 | tf_op jit(solution)/shard_map/ppermute | solution.py:1444
  267.8 5.3 %collective-permute-start.48 = (bf16[4,10,16,128]{3,2,1,0:T(8,128)(2,1)S(1)}, bf16[4,10,16,128]{3,2,1,0:T(8,128)(2,1)S(1)}, u32[]{:S(2)}, u32[]{:S(2)}) collective-permute-start(bf16[4,10,16,128]{3,2,1,0:T(8,128)(2,1)S(1)} %add_convert_fusion.8), channel_id=1, source_target_pairs={{0,1},{1,0},{2,3},{3,2},{4,5},{5,4},{6,7},{7,6},{8,9},{9,8},{10,11... | collective-permute-start | bytes 491528 | tf_op jit(solution)/shard_map/ppermute | solution.py:1444
  273.3 4.5 %collective-permute-start.49 = (bf16[2,10,16,128]{3,2,1,0:T(8,128)(2,1)S(1)}, bf16[2,10,16,128]{3,2,1,0:T(8,128)(2,1)S(1)}, u32[]{:S(2)}, u32[]{:S(2)}) collective-permute-start(bf16[2,10,16,128]{3,2,1,0:T(8,128)(2,1)S(1)} %pad_maximum_fusion.11), channel_id=1, source_target_pairs={{0,2},{1,3},{2,0},{3,1},{4,6},{5,7},{6,4},{7,5},{8,10},{9,11},{10,... | collective-permute-start | bytes 245768 | tf_op jit(solution)/shard_map/ppermute | solution.py:1444
  273.7 5.3 %collective-permute-start.50 = (bf16[2,10,16,128]{3,2,1,0:T(8,128)(2,1)S(1)}, bf16[2,10,16,128]{3,2,1,0:T(8,128)(2,1)S(1)}, u32[]{:S(2)}, u32[]{:S(2)}) collective-permute-start(bf16[2,10,16,128]{3,2,1,0:T(8,128)(2,1)S(1)} %pad_maximum_fusion.12), channel_id=1, source_target_pairs={{0,4},{1,5},{2,6},{3,7},{4,0},{5,1},{6,2},{7,3},{8,12},{9,13},{10,... | collective-permute-start | bytes 245768 | tf_op jit(solution)/shard_map/ppermute | solution.py:1444
  275.9 6.2 %collective-permute-start.51 = (bf16[2,10,16,128]{3,2,1,0:T(8,128)(2,1)S(1)}, bf16[2,10,16,128]{3,2,1,0:T(8,128)(2,1)S(1)}, u32[]{:S(2)}, u32[]{:S(2)}) collective-permute-start(bf16[2,10,16,128]{3,2,1,0:T(8,128)(2,1)S(1)} %pad_maximum_fusion.13), channel_id=1, source_target_pairs={{0,6},{1,7},{2,4},{3,5},{4,2},{5,3},{6,0},{7,1},{8,14},{9,15},{10,... | collective-permute-start | bytes 245768 | tf_op jit(solution)/shard_map/ppermute | solution.py:1444
  285.2 11.0 %collective-permute-start.53 = (f32[128,128]{1,0:T(8,128)}, f32[128,128]{1,0:T(8,128)S(1)}, u32[]{:S(2)}, u32[]{:S(2)}) collective-permute-start(f32[128,128]{1,0:T(8,128)} %get-tuple-element.284), channel_id=1, source_target_pairs={{7,6},{8,7},{9,8},{10,9},{11,10},{12,11},{13,12},{14,13},{15,14},{... | collective-permute-start | bytes 196616 | tf_op jit(solution)/shard_map/ppermute | solution.py:1759
  287.1 9.1 %collective-permute-start.52 = (f32[72,128]{1,0:T(8,128)}, f32[72,128]{1,0:T(8,128)S(1)}, u32[]{:S(2)}, u32[]{:S(2)}) collective-permute-start(f32[72,128]{1,0:T(8,128)} %get-tuple-element.283), channel_id=1, source_target_pairs={{0,1},{1,2},{2,3},{3,4},{4,5},{15,16},{16,17}} | collective-permute-start | bytes 110600 | tf_op jit(solution)/shard_map/ppermute | solution.py:1758
  (40 other events, 315.9 us)
